TPU v7x, 32 devices: a whole 2x2x4 slice. The times are simulated.
32 devices in a mesh: gx: 8 (over z, y), gy: 4 (over x, core).
Axes of the slice: x: 2, y: 2, z: 4, core: 2. Of those that a mesh axis runs over, the one named last changes fastest.
Arguments:
- inputs: bfloat16 [32, 32, 32, 128], P(None, 'gx', 'gy'), may hold values from -6 to 6
- diffusion: bfloat16 [32, 32, 128], P('gx', 'gy'), may hold values from 0.049804688 to 0.5
- spectral: bfloat16 [16, 16, 2, 32, 1024], P('gx', 'gy'), may hold values from -1 to 1
- pointwise: bfloat16 [32, 32], replicated, may hold values from -1 to 1
- offsets: float32 [32], replicated, may hold values from -1 to 1
Outputs:
- activated: bfloat16 [32, 32, 32, 128], P(None, 'gx', 'gy')
All inputs are finite; a program needn't handle non-finite values.
Results may differ from a plain program's by a relative error of at most 0.006.
Values may be sent and summed in bfloat16 or wider, within the bound.
No kernel may reach another device: no remote copies, remote signals or barrier semaphores. Data moves between devices by JAX's collectives and lax.ppermute only.
A program may use at most 64 MiB of HBM per device.

v0:
```python
import math

import jax
import jax.numpy as jnp
from jax import lax
from jax.sharding import PartitionSpec as P

C = 32
KX_DEV = 2
MY = 16
MZ = 32
CX = 4
CY = 8
NZ = 128


def frequencies(modes):
    indices = jnp.arange(modes, dtype=jnp.int32)
    return jnp.where(indices < modes // 2, indices, indices - modes)


def phase_table(positions, waves, length, rotate):
    windings = positions[:, None] * waves[None, :] % length
    angles = 2.0 * math.pi / length * windings.astype(jnp.float32)
    cosine = jnp.cos(angles)
    sines = rotate * jnp.sin(angles)
    from_real = jnp.stack([cosine, sines], axis=-1)
    from_imag = jnp.stack([-sines, cosine], axis=-1)
    return jnp.stack([from_real, from_imag], axis=1)


def z_tables(length_z, modes_z):
    positions = jnp.arange(length_z, dtype=jnp.int32)
    waves = jnp.arange(modes_z, dtype=jnp.int32)
    forward = phase_table(positions, waves, length_z, -1.0)[:, 0, :, :]
    forward = jnp.transpose(forward, (0, 2, 1)).reshape(length_z, 2 * modes_z)
    backward = phase_table(positions, waves, length_z, 1.0)[:, :, :, 0]
    backward = jnp.transpose(backward, (1, 2, 0)).reshape(2 * modes_z, length_z)
    return (forward.astype(jnp.bfloat16), backward)


def contract(u_part, w_part):
    return jnp.einsum("cklz,klcoz->oklz", u_part, w_part, precision=lax.Precision.HIGHEST)


def on_device(inputs, diffusion, spectral, pointwise, offsets):
    highest = lax.Precision.HIGHEST
    ranks_x = lax.axis_size("gx")
    ranks_y = lax.axis_size("gy")
    total_x = CX * ranks_x
    total_y = CY * ranks_y
    owned_x = KX_DEV
    modes_x = KX_DEV * ranks_x
    owned_y = MY // ranks_y
    lane_count = C * owned_y * MZ
    x_cells = lax.axis_index("gx") * CX + jnp.arange(CX, dtype=jnp.int32)
    y_cells = lax.axis_index("gy") * CY + jnp.arange(CY, dtype=jnp.int32)
    all_x = jnp.arange(total_x, dtype=jnp.int32)
    z_forward, z_inverse = z_tables(NZ, MZ)
    diagonal_pair = jnp.eye(2, dtype=jnp.bfloat16)
    paired_table = (diagonal_pair[:, None, :, None] * z_forward[None, :, None, :]).reshape(
        2 * NZ, 4 * MZ
    )
    z_spectrum = jnp.dot(
        inputs.reshape(-1, 2 * NZ), paired_table, preferred_element_type=jnp.float32
    )
    z_spectrum = z_spectrum.reshape(C, CX, CY, 2, MZ)
    y_table = phase_table(y_cells, frequencies(MY), total_y, -1.0)
    y_partial = jnp.einsum("cxyqz,yqkp->cxkpz", z_spectrum, y_table, precision=highest)
    column = lax.psum_scatter(
        y_partial.reshape(C, CX, MY * 2 * MZ), "gy", scatter_dimension=2, tiled=True
    )
    column = column.reshape(C, CX, owned_y, 2, MZ)
    lines = jnp.transpose(column, (1, 3, 0, 2, 4)).reshape(CX, 2, lane_count)
    lines = lax.all_to_all(lines, "gx", split_axis=2, concat_axis=0, tiled=True)
    full_table = phase_table(all_x, frequencies(modes_x), total_x, -1.0)
    spectra = jnp.einsum("xqs,xqap->aps", lines, full_table, precision=highest)
    blocks = lax.all_to_all(spectra, "gx", split_axis=0, concat_axis=2, tiled=True)
    blocks = blocks.reshape(owned_x, 2, C, owned_y, MZ)
    owned = jnp.transpose(blocks, (2, 0, 3, 1, 4))
    owned = owned * (1.0 / math.sqrt(total_x * total_y * NZ))
    weights = spectral.astype(jnp.float32).reshape(owned_x, owned_y, 2, C, C, MZ)
    w_real = weights[:, :, 0]
    w_imag = weights[:, :, 1]
    u_real = owned[:, :, :, 0]
    u_imag = owned[:, :, :, 1]
    y_real = contract(u_real, w_real) - contract(u_imag, w_imag)
    y_imag = contract(u_real, w_imag) + contract(u_imag, w_real)
    mixed = jnp.stack([y_real, y_imag], axis=3).astype(jnp.bfloat16)
    x_inverse = jnp.transpose(
        phase_table(x_cells, frequencies(modes_x), total_x, 1.0), (2, 1, 0, 3)
    )
    y_inverse = jnp.transpose(phase_table(y_cells, frequencies(MY), total_y, 1.0), (2, 1, 0, 3))
    gathered = lax.all_gather(
        mixed.reshape(C, 1, owned_x * owned_y * 2 * MZ), ("gx", "gy"), axis=1, tiled=True
    )
    gathered = gathered.reshape(C, ranks_x, ranks_y, owned_x, owned_y, 2, MZ).astype(jnp.float32)
    back_x = jnp.einsum(
        "cabklqz,akqxp->cxblpz",
        gathered,
        x_inverse.reshape(ranks_x, owned_x, 2, CX, 2),
        precision=highest,
    )
    spatial = jnp.einsum(
        "cxblqz,blqyp->cxypz",
        back_x,
        y_inverse.reshape(ranks_y, owned_y, 2, CY, 2),
        precision=highest,
    )
    spectral_out = jnp.dot(
        spatial.reshape(-1, 2 * MZ),
        z_inverse,
        precision=highest,
        preferred_element_type=jnp.float32,
    )
    spectral_out = spectral_out.reshape(C, CX, CY, NZ) * (1.0 / math.sqrt(modes_x * MY * MZ))
    mixing = jnp.dot(pointwise, inputs.reshape(C, -1), preferred_element_type=jnp.float32).reshape(
        C, CX, CY, NZ
    )
    widened = inputs.astype(jnp.float32)
    padded = jnp.pad(widened, ((0, 0), (0, 0), (0, 0), (1, 1)))
    curvature = padded[:, :, :, 2:] - 2.0 * widened + padded[:, :, :, :-2]
    summed_all = (
        spectral_out
        + mixing
        + diffusion.astype(jnp.float32)[None] * curvature
        + offsets[:, None, None, None]
    )
    return jax.nn.gelu(summed_all, approximate=False).astype(jnp.bfloat16)


def solution(mesh):
    in_specs = (
        P(None, "gx", "gy", None),
        P("gx", "gy", None),
        P("gx", "gy", None, None, None),
        P(),
        P(),
    )
    out_specs = P(None, "gx", "gy", None)
    return jax.shard_map(
        on_device, mesh=mesh, in_specs=in_specs, out_specs=out_specs, check_vma=False
    )
```

profile of v0, /device:TPU:0, one launch (start us, length us, event | category | flops | bytes accessed | tf_op | source)
XLA Modules:
  0.0 179.7 jit_solution(16847804172563971853)
XLA Ops:
  6.5 0.1 multiply_convert_fusion
  6.7 1.0 reshape.745
  7.7 0.1 broadcast_multiply_fusion.1
  7.8 0.2 convolution_bitcast_fusion.2
  8.1 0.1 copy.86
  8.2 0.8 reshape.746
  9.0 0.1 fusion.79
  9.2 1.8 %convolution_bitcast_fusion = f32[32,4,16,2,32]{4,2,1,0,3:T(8,128)S(1)} fusion(f32[32,4,8,2,32]{4,3,2,1,0:T(2,128)S(1)} %reshape.746, f32[8,1,16,2]{2,0,1,3:T(8,128)S(1)} %get-tuple-element.18, f32[8,1,16,2]{2,0,1,3:T(8,128)S(1)} %get-tuple-element.19), kind=kOutput, calls=%fused_computation.16 | convolution fusion | flops 25166336 | bytes 788480 | tf_op jit(solution)/shard_map/cxyqz,yqkp->cxkpz/dot_general | solution.py:69
  11.0 1.6 copy.88
  12.7 3.5 %reshape.747 = f32[32,4,1024]{2,0,1:T(8,128)} reshape(f32[32,4,16,2,32]{4,3,2,0,1:T(2,128)S(1)} %copy.88) | data formatting | bytes 1048576 | tf_op jit(solution)/shard_map/reshape | solution.py:71
  16.1 0.0 reduce-scatter.2.cloned.1.call-update
  16.2 24.5 %reduce-scatter.2.cloned.1.call-done = f32[32,4,256]{2,0,1:T(8,128)} async-done(((f32[32,4,1024]{2,0,1:T(8,128)}), f32[32,4,256]{2,0,1:T(8,128)}) %reduce-scatter.2.cloned.1.call-update) | async-done | bytes 131088 | tf_op jit(solution)/shard_map/reduce_scatter | solution.py:70
  40.7 1.3 reshape.748
  42.0 0.1 copy.190
  42.2 4.6 %copy.147 = f32[4,2,32,4,32]{0,1,4,3,2:T(2,128)} copy(f32[4,2,32,4,32]{4,3,2,1,0:T(4,128)S(1)} %bitcast.196) | data formatting | bytes 262144 | tf_op jit(solution)/shard_map/reshape | solution.py:74
  46.8 8.6 %reshape.777 = f32[8,1,4096]{2,1,0:T(1,128)} reshape(f32[4096,2,4]{2,1,0:T(2,128)} %bitcast.193) | data formatting | bytes 262144
  55.4 5.5 %all-to-all-start = ((f32[8,1,4096]{2,1,0:T(1,128)}), f32[8,1,4096]{2,1,0:T(1,128)S(1)}, u32[]{:S(2)}, u32[]{:S(2)}) async-start(f32[8,1,4096]{2,1,0:T(1,128)} %reshape.777), calls=%async_computation.1 | async-start | bytes 262144 | tf_op jit(solution)/shard_map/all_to_all | solution.py:75
  60.9 0.1 sine_multiply_fusion
  61.0 7.2 %all-to-all-done = f32[8,1,4096]{2,1,0:T(1,128)S(1)} async-done(((f32[8,1,4096]{2,1,0:T(1,128)}), f32[8,1,4096]{2,1,0:T(1,128)S(1)}, u32[]{:S(2)}, u32[]{:S(2)}) %all-to-all-start) | async-done | bytes 131104 | tf_op jit(solution)/shard_map/all_to_all | solution.py:75
  68.2 0.5 broadcast.931
  68.8 1.0 reduce.8
  69.7 8.3 %reshape.778 = f32[4096,2,4]{2,1,0:T(2,128)} reshape(f32[8,4096]{1,0:T(8,128)S(1)} %reduce.8) | data formatting | bytes 262144
  78.0 3.5 %copy.148 = f32[4,2,8,512]{3,2,1,0:T(8,128)S(1)} copy(f32[4,2,8,512]{0,1,3,2:T(2,128)} %bitcast.194) | data formatting | bytes 262144 | tf_op jit(solution)/shard_map/all_to_all | solution.py:75
  81.6 0.1 copy.92
  81.7 0.3 convolution_bitcast_fusion.3
  82.0 0.7 copy.93
  82.7 3.4 %all-to-all-start.1 = ((f32[16,2,512]{2,1,0:T(2,128)}), f32[16,2,512]{2,1,0:T(2,128)S(1)}, u32[]{:S(2)}, u32[]{:S(2)}) async-start(f32[16,2,512]{2,1,0:T(2,128)} %copy.93), calls=%async_computation.2 | async-start | bytes 131072 | tf_op jit(solution)/shard_map/all_to_all | solution.py:78
  86.1 0.0 all-gather.2.cloned.1.call-start
  86.1 4.4 %reshape.750 = bf16[2,4,2,32,32,32]{5,4,3,2,1,0:T(8,128)(2,1)} reshape(bf16[2,4,2,32,1024]{4,3,2,1,0:T(8,128)(2,1)S(1)} %copy-done.2) | data formatting | bytes 2097152 | tf_op jit(solution)/shard_map/reshape | solution.py:82
  90.5 2.4 %all-to-all-done.1 = f32[16,2,512]{2,1,0:T(2,128)S(1)} async-done(((f32[16,2,512]{2,1,0:T(2,128)}), f32[16,2,512]{2,1,0:T(2,128)S(1)}, u32[]{:S(2)}, u32[]{:S(2)}) %all-to-all-start.1) | async-done | bytes 65568 | tf_op jit(solution)/shard_map/all_to_all | solution.py:78
  93.0 0.2 mul.456
  93.2 3.6 %fusion.2 = (f32[2,4,32,32]{2,3,1,0:T(8,128)S(1)}, f32[2,4,32,32]{2,3,1,0:T(8,128)S(1)}, f32[2,4,32,32]{2,3,1,0:T(8,128)S(1)}, f32[2,4,32,32]{2,3,1,0:T(8,128)S(1)}) fusion(f32[2,4,32,32]{2,3,1,0:T(8,128)S(1)} %copy.154, bf16[2,4,2,32,32,32]{5,4,3,2,1,0:T(8,128)(2,1)} %reshape.750, f32[2,4,32,32]{2,3,1,0:T(8,128)S(1)} %copy.153), kind=kLoop, calls=%fused_computation.6 | loop fusion | flops 2588672 | bytes 1245184 | tf_op jit(solution)/shard_map/cklz,klcoz->oklz/dot_general | solution.py:43
  96.9 0.1 copy.95
  97.0 0.8 convert_element_type.151
  97.8 0.0 all-gather.2.cloned.1.call-update
  97.8 0.1 convert_element_type.153
  97.9 0.1 fusion.82
  98.0 0.1 copy.83
  98.1 0.1 copy.82
  98.2 0.1 copy.191
  98.4 0.1 fusion.66
  98.5 0.1 fusion.64
  98.6 0.2 fusion.34
  98.8 50.7 %all-gather.2.cloned.1.call-done = bf16[32,32,512]{2,0,1:T(8,128)(2,1)} async-done(((bf16[32,1,512]{2,0,1:T(8,128)(2,1)}), bf16[32,32,512]{2,0,1:T(8,128)(2,1)}) %all-gather.2.cloned.1.call-update) | async-done | bytes 1048592 | tf_op jit(solution)/shard_map/all_gather | solution.py:94
  149.5 10.0 %reshape.776 = bf16[32,8,4,2,4,2,32]{6,5,4,3,0,2,1:T(2,128)(2,1)} reshape(bf16[32,32,512]{2,0,1:T(8,128)(2,1)} %all-gather.2.cloned.1.call-done) | data formatting | bytes 2097152 | tf_op jit(solution)/shard_map/reshape | solution.py:97
  159.5 6.5 %fusion.9 = f32[32,4,4,4,2,32,1]{5,1,3,2,0,4,6:T(4,128)S(1)} fusion(bf16[32,8,4,2,4,2,32]{6,5,4,3,0,2,1:T(2,128)(2,1)} %reshape.776, f32[8,2,2,4,2,1,1,1]{3,1,0,4,2,7,6,5:T(2,128)S(1)} %bitcast.203), kind=kOutput, calls=%fused_computation.15 | convolution fusion | flops 50331648 | bytes 1573888 | tf_op jit(solution)/shard_map/cabklqz,akqxp->cxblpz/dot_general | solution.py:98
  166.0 3.8 %fusion.12 = f32[32,4,8,2,32]{4,2,3,1,0:T(8,128)S(1)} fusion(f32[32,4,4,4,2,32,1]{5,1,3,2,0,4,6:T(4,128)S(1)} %fusion.9, f32[4,4,2,8,2,1,1]{3,1,0,4,2,6,5:T(4,128)S(1)} %bitcast.205), kind=kOutput, calls=%fused_computation.17 | convolution fusion | flops 25165824 | bytes 788480 | tf_op jit(solution)/shard_map/cxblqz,blqyp->cxypz/dot_general | solution.py:104
  169.8 3.1 %fusion.23 = bf16[32,4,8,128]{3,2,1,0:T(8,128)(2,1)} fusion(f32[32,4,8,128]{3,2,1,0:T(8,128)S(1)} %convert_element_type.153, f32[32,4,8,128]{3,0,2,1:T(8,128)S(1)} %fusion.34, f32[32,4,8,2,32]{4,2,3,1,0:T(8,128)S(1)} %fusion.12, f32[32]{0:T(128)S(1)} %copy-done.4, f32[4,8,128]{2,1,0:T(8,128)S(1)} %convert_element_type.152, ...), kind=kOutput, calls=%fused_computation.32 | convolution fusion | flops 110239744 | bytes 1654912 | tf_op jit(solution)/shard_map/dot_general | solution.py:110
  (33 shorter events, 0.4 us)
Async XLA Ops:
  6.5 92.1 %copy-start = (bf16[32,32]{1,0:T(8,128)(2,1)S(1)}, bf16[32,32]{1,0:T(8,128)(2,1)}, u32[]{:S(2)}) copy-start(bf16[32,32]{1,0:T(8,128)(2,1)} %param.8) | copy-start | bytes 6148
  6.5 34.1 %reduce-scatter.2.cloned.1.call-start = ((), (), s32[]{:S(2)}) async-start(), calls=%async_computation.3 | async-start | bytes 655360 | tf_op jit(solution)/shard_map/reduce_scatter | solution.py:70
  55.4 12.9 %all-to-all-start = ((f32[8,1,4096]{2,1,0:T(1,128)}), f32[8,1,4096]{2,1,0:T(1,128)S(1)}, u32[]{:S(2)}, u32[]{:S(2)}) async-start(f32[8,1,4096]{2,1,0:T(1,128)} %reshape.777), calls=%async_computation.1 | async-start | bytes 262144 | tf_op jit(solution)/shard_map/all_to_all | solution.py:75
  69.7 16.4 %copy-start.2 = (bf16[2,4,2,32,1024]{4,3,2,1,0:T(8,128)(2,1)S(1)}, bf16[2,4,2,32,1024]{4,3,2,1,0:T(8,128)(2,1)}, u32[]{:S(2)}) copy-start(bf16[2,4,2,32,1024]{4,3,2,1,0:T(8,128)(2,1)} %param.7) | copy-start | bytes 3145732
  82.7 10.2 %all-to-all-start.1 = ((f32[16,2,512]{2,1,0:T(2,128)}), f32[16,2,512]{2,1,0:T(2,128)S(1)}, u32[]{:S(2)}, u32[]{:S(2)}) async-start(f32[16,2,512]{2,1,0:T(2,128)} %copy.93), calls=%async_computation.2 | async-start | bytes 131072 | tf_op jit(solution)/shard_map/all_to_all | solution.py:78
  86.1 63.5 %all-gather.2.cloned.1.call-start = ((), (), s32[]{:S(2)}) async-start(), calls=%async_computation.4 | async-start | bytes 1081344 | tf_op jit(solution)/shard_map/all_gather | solution.py:94
  90.5 7.3 %copy-start.1 = (bf16[32,4,8,128]{3,2,1,0:T(8,128)(2,1)S(1)}, bf16[32,4,8,128]{3,2,1,0:T(8,128)(2,1)}, u32[]{:S(2)}) copy-start(bf16[32,4,8,128]{3,2,1,0:T(8,128)(2,1)} %param.5) | copy-start | bytes 786436
  93.2 5.2 %copy-start.3 = (bf16[4,8,128]{2,1,0:T(8,128)(2,1)S(1)}, bf16[4,8,128]{2,1,0:T(8,128)(2,1)}, u32[]{:S(2)}) copy-start(bf16[4,8,128]{2,1,0:T(8,128)(2,1)} %param.6) | copy-start | bytes 24580
  159.5 10.3 %copy-start.4 = (f32[32]{0:T(128)S(1)}, f32[32]{0:T(128)}, u32[]{:S(2)}) copy-start(f32[32]{0:T(128)} %param.9) | copy-start | bytes 388
Sparse Core Ops, SparseCore 0:
  16.3 24.3 reduce-scatter.1
  97.9 51.5 all-gather.1
where the time goes:
time: 180 us
  waiting for transfers between devices  84.9 us (47%)
  local copies, waits for them, and re-layouts  50.7 us (28%)
  matrix products  16 us (9%)
  between operations  13.8 us (8%)
  starting transfers between devices  8.91 us (5%)
  other arithmetic  5.49 us (3%)
    all_gather x1, waiting for transfers between devices, on_device(): lax.all_gather(mixed.reshape(C, 1, owned_x * owned_y * 2 * MZ), ('gx', 'g...  50.7 us
    reduce_scatter x1, waiting for transfers between devices, on_device(): lax.psum_scatter(y_partial.reshape(C, CX, MY * 2 * MZ), 'gy', scatter_dim...  24.5 us
    unnamed x17, local copies, waits for them, and re-layouts  17.1 us
    reshape x1, local copies, waits for them, and re-layouts, on_device(): gathered.reshape(C, ranks_x, ranks_y, owned_x, owned_y, 2, MZ)  9.95 us
    all_to_all x1, waiting for transfers between devices, on_device(): lines = lax.all_to_all(lines, 'gx', split_axis=2, concat_axis=0, tiled=True)  7.2 us
    dot_general x1, matrix products, on_device(): jnp.einsum('cabklqz,akqxp->cxblpz', gathered, x_inverse.reshape(ranks_x,...  6.48 us
    all_to_all x1, starting transfers between devices, on_device(): lines = lax.all_to_all(lines, 'gx', split_axis=2, concat_axis=0, tiled=True)  5.52 us
    reshape x1, local copies, waits for them, and re-layouts, on_device(): lines = jnp.transpose(column, (1, 3, 0, 2, 4)).reshape(CX, 2, lane_count)  4.64 us
  transfers between devices with their start and end apart: 4, of which 4 were waited for; matrix products, arithmetic and copies ran while one was open for 3% of the time, Pallas kernels for 0%

commit v1 on v0

v1 whole, which is shorter than its diff:
```python
import functools
import math

import jax
import jax.numpy as jnp
import numpy as np
from jax import lax
from jax.experimental import pallas as pl
from jax.experimental.pallas import tpu as pltpu
from jax.sharding import PartitionSpec as P

LANES = 128
GROUP = LANES // 2


def signed(modes):
    index = np.arange(modes)
    return np.where(index < modes // 2, index, index - modes)


class Plan:
    def __init__(self, ranks_x, ranks_y, channels, cx, cy, nz, kxd, kyd, mz):
        self.rx, self.ry = ranks_x, ranks_y
        self.c, self.cx, self.cy, self.nz = channels, cx, cy, nz
        self.kxd, self.kyd, self.mz = kxd, kyd, mz
        self.nx, self.ny = cx * ranks_x, cy * ranks_y
        self.mx, self.my = kxd * ranks_x, kyd * ranks_y
        self.devices = ranks_x * ranks_y
        self.slices = self.devices // channels
        self.mzs = mz // self.slices
        self.half = cx // 2
        self.rows = self.half * cy
        self.owned = kxd * kyd
        assert self.devices == self.slices * channels
        assert nz == LANES and 4 * mz == LANES and channels * mz % LANES == 0

    def z_forward(self):
        z = np.arange(self.nz)[:, None]
        kz = np.arange(self.mz)[None, :]
        angle = 2.0 * np.pi / self.nz * (z * kz % self.nz)
        table = np.zeros((self.slices, 2, self.nz, LANES), np.float32)
        for s in range(self.slices):
            part = slice(s * self.mzs, (s + 1) * self.mzs)
            for h in range(2):
                at = h * GROUP
                table[s, h, :, at : at + self.mzs] = np.cos(angle)[:, part]
                table[s, h, :, at + self.mz : at + self.mz + self.mzs] = -np.sin(angle)[:, part]
        return table.reshape(self.slices, 2 * self.nz, LANES)

    def z_inverse(self):
        kz = np.arange(self.mz)[:, None]
        z = np.arange(self.nz)[None, :]
        angle = 2.0 * np.pi / self.nz * (z * kz % self.nz)
        scale = 1.0 / math.sqrt(self.mx * self.my * self.mz)
        table = np.zeros((self.slices, 2, LANES, self.nz), np.float32)
        for s in range(self.slices):
            part = slice(s * self.mzs, (s + 1) * self.mzs)
            for h in range(2):
                at = h * GROUP
                table[s, h, at : at + self.mzs] = scale * np.cos(angle)[part]
                table[s, h, at + self.mz : at + self.mz + self.mzs] = -scale * np.sin(angle)[part]
        return table

    def turns(self):
        kx, ky = signed(self.mx), signed(self.my)
        mode_x = kx.reshape(self.rx, 1, self.kxd, 1)
        mode_y = ky.reshape(1, self.ry, 1, self.kyd)
        shape = (self.rx, self.ry, self.kxd, self.kyd)
        mode_x = np.broadcast_to(mode_x, shape).reshape(-1)
        mode_y = np.broadcast_to(mode_y, shape).reshape(-1)
        x = (np.arange(self.rx)[:, None] * self.cx + np.arange(self.half)).reshape(
            self.rx, 1, self.half, 1
        )
        y = np.arange(self.ny).reshape(1, self.ry, 1, self.cy)
        shape = (self.rx, self.ry, self.half, self.cy)
        x = np.broadcast_to(x, shape).reshape(-1)
        y = np.broadcast_to(y, shape).reshape(-1)
        return mode_x, mode_y, x, y

    def angles(self, shift):
        mode_x, mode_y, x, y = self.turns()
        along_x = mode_x[:, None] * (x[None, :] + shift) % self.nx
        along_y = mode_y[:, None] * y[None, :] % self.ny
        return 2.0 * np.pi * (along_x / self.nx + along_y / self.ny)

    def forward(self):
        angle = self.angles(0)
        return np.concatenate([np.cos(angle), np.sin(angle)], axis=0)

    def shift_phase(self):
        mode_x = self.turns()[0]
        angle = 2.0 * np.pi * (mode_x * self.half % self.nx) / self.nx
        scale = 1.0 / math.sqrt(self.nx * self.ny * self.nz)
        sign = np.where(np.arange(LANES) % GROUP < self.mz, 1.0, -1.0)
        cosine = np.cos(angle)[:, None] * np.ones(LANES)
        sine = np.sin(angle)[:, None] * sign
        return (np.stack([cosine, sine]) * scale).astype(np.float32), scale

    def backward(self):
        halves = []
        for h in range(2):
            angle = self.angles(h * self.half).T
            halves.append(np.concatenate([np.cos(angle), np.sin(angle)], axis=1))
        return np.concatenate(halves, axis=0)

    def spread(self):
        per = LANES // self.mz
        table = np.zeros((self.slices, LANES, 2 * LANES), np.float32)
        for s in range(self.slices):
            for q in range(2):
                for k in range(self.mzs):
                    for o in range(per):
                        table[s, q * self.mz + k, q * LANES + o * self.mz + s * self.mzs + k] = 1
        return table

    def pick(self):
        per = LANES // self.mz
        table = np.zeros((per, self.slices, 2 * LANES, LANES), np.float32)
        for o in range(per):
            for s in range(self.slices):
                for q in range(2):
                    for k in range(self.mzs):
                        row = q * LANES + o * self.mz + s * self.mzs + k
                        for h in range(2):
                            table[o, s, row, h * GROUP + q * self.mz + k] = 1
        return table


def dot(a, b):
    return jnp.dot(a, b, preferred_element_type=jnp.float32)


def lanes_of(shape):
    return lax.broadcasted_iota(jnp.int32, shape, len(shape) - 1)


def to_lines(plan, x_ref, f_ref, out_ref):
    half, c, cy = plan.half, plan.c, plan.cy
    x = x_ref[...]
    low = x[:, :half].reshape(c * plan.rows, LANES)
    high = x[:, half:].reshape(c * plan.rows, LANES)
    cells = jnp.concatenate([low, high], axis=1)
    for s in range(plan.slices):
        line = dot(cells, f_ref[s]).astype(jnp.bfloat16)
        out_ref[:, s] = line.reshape(c, plan.rows, LANES)


def to_modes(plan, x_ref, t_ref, phase_ref, out_ref):
    modes = plan.devices * plan.owned
    x = x_ref[...].reshape(plan.devices * plan.rows, LANES)
    turned = dot(t_ref[...], x)
    cosine, sine = turned[:modes], turned[modes:]
    real = lanes_of((modes, LANES)) % GROUP < plan.mz
    up = LANES - plan.mz
    u = cosine + jnp.where(real, pltpu.roll(sine, up, 1), -pltpu.roll(sine, plan.mz, 1))
    other = jnp.where(real, pltpu.roll(u, plan.mz, 1), pltpu.roll(u, up, 1))
    scale = plan.shift_phase()[1]
    whole = u * scale + phase_ref[0] * pltpu.roll(u, GROUP, 1) + phase_ref[1] * other
    out_ref[...] = whole.reshape(plan.devices, plan.owned, LANES).astype(jnp.bfloat16)


def mix(plan, u_ref, w_ref, spread_ref, pick_ref, out_ref, wide, sums):
    c, owned = plan.c, plan.owned
    blocks = c * plan.mz // LANES
    per = LANES // plan.mz
    u = u_ref[...]
    total = None
    for s in range(plan.slices):
        part = dot(u[:, s].reshape(c * owned, LANES), spread_ref[s])
        total = part if total is None else total + part
    wide[0] = total[:, :LANES]
    wide[1] = total[:, LANES:]
    for m in range(owned):
        u_real = wide[0, pl.ds(m, c, stride=owned), :]
        u_imag = wide[1, pl.ds(m, c, stride=owned), :]
        for j in range(blocks):
            at = pl.ds(j * LANES, LANES)
            w_real = w_ref[m, 0, :, at].astype(jnp.float32)
            w_imag = w_ref[m, 1, :, at].astype(jnp.float32)
            y_real = jnp.sum(w_real * u_real - w_imag * u_imag, axis=0, keepdims=True)
            y_imag = jnp.sum(w_real * u_imag + w_imag * u_real, axis=0, keepdims=True)
            sums[pl.ds(j * owned + m, 1), :LANES] = y_real
            sums[pl.ds(j * owned + m, 1), LANES:] = y_imag
    mixed = sums[...].astype(jnp.bfloat16)
    for o in range(per):
        for s in range(plan.slices):
            line = dot(mixed, pick_ref[o, s]).reshape(blocks, owned, LANES)
            out_ref[:, o, s] = line.astype(jnp.bfloat16)


def from_modes(plan, m_ref, t_ref, out_ref):
    modes = plan.devices * plan.owned
    cells = plan.devices * plan.rows
    m = m_ref[...].reshape(modes, LANES)
    real = lanes_of((modes, LANES)) % GROUP < plan.mz
    swapped = pltpu.roll(m.astype(jnp.float32), plan.mz, 1)
    swapped = jnp.where(real, -swapped, swapped).astype(jnp.bfloat16)
    both = jnp.concatenate([m, swapped], axis=0)
    turned = dot(t_ref[...], both)
    first = lanes_of((cells, LANES)) < GROUP
    out = jnp.where(first, turned[:cells], turned[cells:])
    out_ref[...] = out.reshape(plan.devices, plan.rows, LANES).astype(jnp.bfloat16)


def local_terms(plan, x_ref, d_ref, p_ref, o_ref, out_ref):
    c, cy = plan.c, plan.cy
    size = c * cy
    row = lax.broadcasted_iota(jnp.int32, (size, c), 0) // cy
    pick = (row == lax.broadcasted_iota(jnp.int32, (size, c), 1)).astype(jnp.bfloat16)
    spread = dot(pick, p_ref[...]).astype(jnp.bfloat16)
    wide = lax.dot_general(spread, pick, (((1,), (1,)), ((), ())), preferred_element_type=jnp.float32)
    same = (
        lax.broadcasted_iota(jnp.int32, (size, size), 0) % cy
        == lax.broadcasted_iota(jnp.int32, (size, size), 1) % cy
    )
    mixer = jnp.where(same, wide, 0.0).astype(jnp.bfloat16)
    lane = lanes_of((size, LANES))
    for x in range(plan.cx):
        v = x_ref[:, x].reshape(size, LANES)
        mixing = dot(mixer, v)
        f = v.astype(jnp.float32)
        before = jnp.where(lane == 0, 0.0, pltpu.roll(f, 1, 1))
        after = jnp.where(lane == LANES - 1, 0.0, pltpu.roll(f, LANES - 1, 1))
        curvature = (before + after - 2.0 * f).reshape(c, cy, LANES)
        d = d_ref[x].astype(jnp.float32)
        out_ref[:, x] = mixing.reshape(c, cy, LANES) + d[None] * curvature + o_ref[...]


def finish(plan, s_ref, b_ref, z_ref, out_ref):
    c, half = plan.c, plan.half
    for h in range(2):
        total = None
        for s in range(plan.slices):
            part = dot(s_ref[:, s].reshape(c * plan.rows, LANES), z_ref[s, h])
            total = part if total is None else total + part
        v = total.reshape(c, half, plan.cy, LANES) + b_ref[:, h * half : (h + 1) * half]
        gelu = 0.5 * v * (1.0 + lax.erf(v * math.sqrt(0.5)))
        out_ref[:, h * half : (h + 1) * half] = gelu.astype(jnp.bfloat16)


def call(body, plan, out, scratch=(), flops=0, moved=0):
    return pl.pallas_call(
        functools.partial(body, plan),
        out_shape=out,
        scratch_shapes=list(scratch),
        cost_estimate=pl.CostEstimate(flops=flops, bytes_accessed=moved, transcendentals=0),
    )


def on_device(inputs, diffusion, spectral, pointwise, offsets):
    ranks_x = lax.axis_size("gx")
    ranks_y = lax.axis_size("gy")
    c, cx, cy, nz = inputs.shape
    kxd, kyd = spectral.shape[:2]
    plan = Plan(ranks_x, ranks_y, c, cx, cy, nz, kxd, kyd, spectral.shape[4] // c)
    axes = ("gx", "gy")
    bf16 = jnp.bfloat16
    d, s = plan.devices, plan.slices
    shape = jax.ShapeDtypeStruct
    exchange = functools.partial(lax.all_to_all, axis_name=axes, split_axis=0, concat_axis=0, tiled=True)

    def table(values):
        return jnp.asarray(np.asarray(values, np.float32).astype(bf16))

    lines = call(to_lines, plan, shape((c, s, plan.rows, LANES), bf16))(
        inputs, table(plan.z_forward())
    )
    lines = exchange(lines.reshape(d, plan.rows, LANES))
    base = call(
        local_terms, plan, shape((c, cx, cy, nz), jnp.float32), flops=10**9, moved=10**6
    )(inputs, diffusion, pointwise, jnp.broadcast_to(offsets[:, None, None], (c, cy, LANES)))
    phase = plan.shift_phase()[0]
    modes = call(to_modes, plan, shape((d, plan.owned, LANES), bf16))(
        lines, table(plan.forward()), jnp.asarray(phase)
    )
    modes = exchange(modes)
    mixed = call(
        mix,
        plan,
        shape((c * plan.mz // LANES, LANES // plan.mz, s, plan.owned, LANES), bf16),
        scratch=[
            pltpu.VMEM((2, c * plan.owned, LANES), jnp.float32),
            pltpu.VMEM((c * plan.mz // LANES * plan.owned, 2 * LANES), jnp.float32),
        ],
    )(
        modes.reshape(c, s, plan.owned, LANES),
        spectral.reshape(plan.owned, 2, c, c * plan.mz),
        table(plan.spread()),
        table(plan.pick()),
    )
    mixed = exchange(mixed.reshape(d, plan.owned, LANES))
    spatial = call(from_modes, plan, shape((d, plan.rows, LANES), bf16))(
        mixed, table(plan.backward())
    )
    spatial = exchange(spatial)
    return call(finish, plan, shape((c, cx, cy, nz), bf16))(
        spatial.reshape(c, s, plan.rows, LANES), base, table(plan.z_inverse())
    )


def solution(mesh):
    in_specs = (
        P(None, "gx", "gy", None),
        P("gx", "gy", None),
        P("gx", "gy", None, None, None),
        P(),
        P(),
    )
    out_specs = P(None, "gx", "gy", None)
    return jax.shard_map(
        on_device, mesh=mesh, in_specs=in_specs, out_specs=out_specs, check_vma=False
    )
```

time: 180 us -> 60.3 us (0.33)
  waiting for transfers between devices: 84.9 us -> 5.09 us
  local copies, waits for them, and re-layouts: 50.7 us -> 1.38 us
  blocking collectives: 0 us -> 36.9 us
  matrix products: 16 us -> 0 us
  between operations: 13.8 us -> 0.02 us
  Pallas kernels: 0 us -> 13.7 us
  starting transfers between devices: 8.91 us -> 2.71 us
  other arithmetic: 5.49 us -> 0 us
    all_gather x1 -> x0, waiting for transfers between devices: 50.7 us -> none  [on_device(): lax.all_gather(mixed.reshape(C, 1, owned_x * owned_y * 2 * MZ), ('gx', 'g...]
    all_to_all x0 -> x3, blocking collectives: none -> 36.9 us  [the longest x1 15.6 us: on_device(): lines = exchange(lines.reshape(d, plan.rows, LANES))]
    reshape x8 -> x0, local copies, waits for them, and re-layouts: 25.8 us -> none  [the longest x1 9.95 us: on_device(): gathered.reshape(C, ranks_x, ranks_y, owned_x, owned_y, 2, MZ)]
    reduce_scatter x1 -> x0, waiting for transfers between devices: 24.5 us -> none  [on_device(): lax.psum_scatter(y_partial.reshape(C, CX, MY * 2 * MZ), 'gy', scatter_dim...]
    unnamed x17 -> x4, local copies, waits for them, and re-layouts: 17.1 us -> 0.64 us
    dot_general x7 -> x0, matrix products: 16 us -> none  [the longest x1 6.48 us: on_device(): jnp.einsum('cabklqz,akqxp->cxblpz', gathered, x_inverse.reshape(ranks_x,...]
    pallas_call x0 -> x6, Pallas kernels: none -> 13.7 us  [the longest x1 2.81 us: on_device(): call(mix, plan, shape((c * plan.mz // LANES, LANES // plan.mz, s, plan.ow...]
    all_to_all x2 -> x1, starting transfers between devices: 8.87 us -> 2.71 us  [on_device(): spatial = exchange(spatial)]
  transfers between devices with their start and end apart: 4 -> 1, of which waited for: 4 -> 1; matrix products, arithmetic and copies ran while one was open for 3% -> 1% of each run, Pallas kernels for 0% -> 4%
where the time goes in v1:
time: 60.3 us; the launch traced here: 59.8 us
  blocking collectives  36.9 us (61%)
  Pallas kernels  13.7 us (23%)
  waiting for transfers between devices  5.09 us (8%)
  starting transfers between devices  2.71 us (4%)
  local copies, waits for them, and re-layouts  1.38 us (2%)
    all_to_all x1, blocking collectives, on_device(): lines = exchange(lines.reshape(d, plan.rows, LANES))  15.6 us
    all_to_all x1, blocking collectives, on_device(): modes = exchange(modes)  10.6 us
    all_to_all x1, blocking collectives, on_device(): mixed = exchange(mixed.reshape(d, plan.owned, LANES))  10.6 us
    all_to_all x1, waiting for transfers between devices, on_device(): spatial = exchange(spatial)  5.09 us
    pallas_call x1, Pallas kernels, on_device(): call(mix, plan, shape((c * plan.mz // LANES, LANES // plan.mz, s, plan.ow...  2.81 us
    all_to_all x1, starting transfers between devices, on_device(): spatial = exchange(spatial)  2.71 us
    pallas_call x1, Pallas kernels, on_device(): call(from_modes, plan, shape((d, plan.rows, LANES), bf16))  2.42 us
    pallas_call x1, Pallas kernels, on_device(): call(local_terms, plan, shape((c, cx, cy, nz), jnp.float32), flops=10 **...  2.36 us
  transfers between devices with their start and end apart: 1, of which 1 were waited for; matrix products, arithmetic and copies ran while one was open for 1% of the time, Pallas kernels for 4%

profile of v1, /device:TPU:0, one launch (start us, length us, event | category | flops | bytes accessed | tf_op | source)
XLA Modules:
  0.0 59.8 jit_solution(8217382699440597566)
XLA Ops:
  0.0 1.8 %shard_map.118 = bf16[32,1,16,128]{3,2,1,0:T(8,128)(2,1)} custom-call(bf16[32,4,8,128]{3,2,1,0:T(8,128)(2,1)} %x_ref.3, bf16[1,256,128]{2,1,0:T(8,128)(2,1)} %constant.14.clone.f_ref), custom_call_target="tpu_custom_call" | custom-call | tf_op jit(solution)/shard_map/pallas_call | solution.py:265
  1.8 15.6 %all_to_all.20.x_ref = bf16[32,16,128]{2,1,0:T(8,128)(2,1)} all-to-all(bf16[32,16,128]{2,1,0:T(8,128)(2,1)} %bitcast.7), channel_id=1, replica_groups=mesh['gx'=8,'gy'=4] {'gx','gy'}, dimensions={0} | all-to-all | bytes 262144 | tf_op jit(solution)/shard_map/all_to_all | solution.py:268
  17.5 2.2 %shard_map.119 = bf16[32,8,128]{2,1,0:T(8,128)(2,1)} custom-call(bf16[32,16,128]{2,1,0:T(8,128)(2,1)} %all_to_all.20.x_ref, bf16[512,512]{1,0:T(8,128)(2,1)} %constant.15.clone.t_ref, f32[2,256,128]{2,1,0:T(8,128)} %constant.16.clone.phase_ref), custom_call_target="tpu_custom_call" | custom-call | tf_op jit(solution)/shard_map/pallas_call | solution.py:273
  19.7 10.6 %all_to_all.21 = bf16[32,8,128]{2,1,0:T(8,128)(2,1)} all-to-all(bf16[32,8,128]{2,1,0:T(8,128)(2,1)} %shard_map.119), channel_id=1, replica_groups=mesh['gx'=8,'gy'=4] {'gx','gy'}, dimensions={0} | all-to-all | bytes 131072 | tf_op jit(solution)/shard_map/all_to_all | solution.py:276
  30.4 2.8 %shard_map.120 = bf16[8,4,1,8,128]{4,3,2,1,0:T(8,128)(2,1)} custom-call(bf16[32,1,8,128]{3,2,1,0:T(8,128)(2,1)} %bitcast.8, bf16[8,2,32,1024]{3,2,1,0:T(8,128)(2,1)} %bitcast.5, bf16[1,128,256]{2,1,0:T(8,128)(2,1)} %constant.17.clone.spread_ref, bf16[4,1,256,128]{3,2,1,0:T(8,128)(2,1)} %constant.18.clone.pick_ref), custom_call_target="tpu_custom_call" | custom-call | tf_op jit(solution)/shard_map/pallas_call | solution.py:277
  33.2 10.6 %all_to_all.22.m_ref = bf16[32,8,128]{2,1,0:T(8,128)(2,1)} all-to-all(bf16[32,8,128]{2,1,0:T(8,128)(2,1)} %bitcast.9), channel_id=1, replica_groups=mesh['gx'=8,'gy'=4] {'gx','gy'}, dimensions={0} | all-to-all | bytes 131072 | tf_op jit(solution)/shard_map/all_to_all | solution.py:291
  43.8 2.4 %shard_map.121 = bf16[32,16,128]{2,1,0:T(8,128)(2,1)} custom-call(bf16[32,8,128]{2,1,0:T(8,128)(2,1)} %all_to_all.22.m_ref, bf16[1024,512]{1,0:T(8,128)(2,1)} %constant.19.clone.t_ref), custom_call_target="tpu_custom_call" | custom-call | tf_op jit(solution)/shard_map/pallas_call | solution.py:292
  46.2 0.0 copy-start.1
  46.3 2.7 %all-to-all-start.3 = ((bf16[32,16,128]{2,1,0:T(8,128)(2,1)}), bf16[32,16,128]{2,1,0:T(8,128)(2,1)S(1)}, u32[]{:S(2)}, u32[]{:S(2)}) async-start(bf16[32,16,128]{2,1,0:T(8,128)(2,1)} %shard_map.121), calls=%async_computation.3 | async-start | bytes 262144 | tf_op jit(solution)/shard_map/all_to_all | solution.py:295
  49.0 0.0 copy-done.1
  49.0 0.7 %broadcast_in_dim.2.o_ref = f32[32,8,128]{2,1,0:T(8,128)} broadcast(f32[32]{0:T(128)S(1)} %copy-done.1), dimensions={0} | broadcast | bytes 131200 | tf_op jit(solution)/shard_map/broadcast_in_dim | solution.py:271
  49.7 2.4 %shard_map.122.b_ref = f32[32,4,8,128]{3,2,1,0:T(8,128)} custom-call(bf16[32,4,8,128]{3,2,1,0:T(8,128)(2,1)} %x_ref.3, bf16[4,8,128]{2,1,0:T(8,128)(2,1)} %d_ref.1, bf16[32,32]{1,0:T(8,128)(2,1)} %p_ref.1, f32[32,8,128]{2,1,0:T(8,128)} %broadcast_in_dim.2.o_ref), custom_call_target="tpu_custom_call" | custom-call | flops 1000000000 | bytes 1000000 | tf_op jit(solution)/shard_map/pallas_call | solution.py:269
  52.1 5.1 %all-to-all-done.3 = bf16[32,16,128]{2,1,0:T(8,128)(2,1)S(1)} async-done(((bf16[32,16,128]{2,1,0:T(8,128)(2,1)}), bf16[32,16,128]{2,1,0:T(8,128)(2,1)S(1)}, u32[]{:S(2)}, u32[]{:S(2)}) %all-to-all-start.3) | async-done | bytes 131104 | tf_op jit(solution)/shard_map/all_to_all | solution.py:295
  57.2 0.0 copy-start
  57.2 0.6 %copy-done = bf16[32,16,128]{2,1,0:T(8,128)(2,1)} copy-done((bf16[32,16,128]{2,1,0:T(8,128)(2,1)}, bf16[32,16,128]{2,1,0:T(8,128)(2,1)S(1)}, u32[]{:S(2)}) %copy-start) | copy-done | bytes 131096
  57.8 2.0 %shard_map.123 = bf16[32,4,8,128]{3,2,1,0:T(8,128)(2,1)} custom-call(bf16[32,1,16,128]{3,2,1,0:T(8,128)(2,1)} %bitcast.6, f32[32,4,8,128]{3,2,1,0:T(8,128)} %shard_map.122.b_ref, bf16[1,2,128,128]{3,2,1,0:T(8,128)(2,1)} %constant.20.clone.z_ref), custom_call_target="tpu_custom_call" | custom-call | tf_op jit(solution)/shard_map/pallas_call | solution.py:296
Async XLA Ops:
  46.2 2.7 %copy-start.1 = (f32[32]{0:T(128)S(1)}, f32[32]{0:T(128)}, u32[]{:S(2)}) copy-start(f32[32]{0:T(128)} %param.16) | copy-start | bytes 388
  46.3 10.9 %all-to-all-start.3 = ((bf16[32,16,128]{2,1,0:T(8,128)(2,1)}), bf16[32,16,128]{2,1,0:T(8,128)(2,1)S(1)}, u32[]{:S(2)}, u32[]{:S(2)}) async-start(bf16[32,16,128]{2,1,0:T(8,128)(2,1)} %shard_map.121), calls=%async_computation.3 | async-start | bytes 262144 | tf_op jit(solution)/shard_map/all_to_all | solution.py:295
  57.2 0.6 %copy-start = (bf16[32,16,128]{2,1,0:T(8,128)(2,1)}, bf16[32,16,128]{2,1,0:T(8,128)(2,1)S(1)}, u32[]{:S(2)}) copy-start(bf16[32,16,128]{2,1,0:T(8,128)(2,1)S(1)} %all-to-all-done.3) | copy-start | bytes 393220

commit v2 on v1

--- a/solution.py
+++ b/solution.py
@@ -238,10 +238,13 @@
         out_ref[:, h * half : (h + 1) * half] = gelu.astype(jnp.bfloat16)
 
 
-def call(body, plan, out, scratch=(), flops=0, moved=0):
+def call(n, body, plan, out, scratch=(), flops=0, moved=0):
     return pl.pallas_call(
         functools.partial(body, plan),
         out_shape=out,
+        in_specs=[pl.BlockSpec(memory_space=pltpu.VMEM)] * n,
+        out_specs=pl.BlockSpec(memory_space=pltpu.VMEM),
+        compiler_params=pltpu.CompilerParams(vmem_limit_bytes=16 * 2**20),
         scratch_shapes=list(scratch),
         cost_estimate=pl.CostEstimate(flops=flops, bytes_accessed=moved, transcendentals=0),
     )
@@ -262,19 +265,20 @@
     def table(values):
         return jnp.asarray(np.asarray(values, np.float32).astype(bf16))
 
-    lines = call(to_lines, plan, shape((c, s, plan.rows, LANES), bf16))(
+    lines = call(2, to_lines, plan, shape((c, s, plan.rows, LANES), bf16))(
         inputs, table(plan.z_forward())
     )
     lines = exchange(lines.reshape(d, plan.rows, LANES))
     base = call(
-        local_terms, plan, shape((c, cx, cy, nz), jnp.float32), flops=10**9, moved=10**6
+        4, local_terms, plan, shape((c, cx, cy, nz), jnp.float32), flops=10**9, moved=10**6
     )(inputs, diffusion, pointwise, jnp.broadcast_to(offsets[:, None, None], (c, cy, LANES)))
     phase = plan.shift_phase()[0]
-    modes = call(to_modes, plan, shape((d, plan.owned, LANES), bf16))(
+    modes = call(3, to_modes, plan, shape((d, plan.owned, LANES), bf16))(
         lines, table(plan.forward()), jnp.asarray(phase)
     )
     modes = exchange(modes)
     mixed = call(
+        4,
         mix,
         plan,
         shape((c * plan.mz // LANES, LANES // plan.mz, s, plan.owned, LANES), bf16),
@@ -289,11 +293,11 @@
         table(plan.pick()),
     )
     mixed = exchange(mixed.reshape(d, plan.owned, LANES))
-    spatial = call(from_modes, plan, shape((d, plan.rows, LANES), bf16))(
+    spatial = call(2, from_modes, plan, shape((d, plan.rows, LANES), bf16))(
         mixed, table(plan.backward())
     )
     spatial = exchange(spatial)
-    return call(finish, plan, shape((c, cx, cy, nz), bf16))(
+    return call(3, finish, plan, shape((c, cx, cy, nz), bf16))(
         spatial.reshape(c, s, plan.rows, LANES), base, table(plan.z_inverse())
     )
 

time: 60.3 us -> 52.4 us (0.87)
  Pallas kernels: 13.7 us -> 4.23 us
  blocking collectives: 36.9 us -> 33.7 us
  local copies, waits for them, and re-layouts: 1.38 us -> 4.41 us
  waiting for transfers between devices: 5.09 us -> 6.92 us
    pallas_call x6, Pallas kernels: 13.7 us -> 4.23 us  [the longest x1 1.15 us: on_device(): call(2, from_modes, plan, shape((d, plan.rows, LANES), bf16))]
    unnamed x4 -> x26, local copies, waits for them, and re-layouts: 0.64 us -> 4.32 us
    all_to_all x1, waiting for transfers between devices: 5.09 us -> 6.92 us  [on_device(): spatial = exchange(spatial)]
    all_to_all x1, blocking collectives: 10.6 us -> 9.1 us  [on_device(): mixed = exchange(mixed.reshape(d, plan.owned, LANES))]
    all_to_all x1, blocking collectives: 10.6 us -> 9.24 us  [on_device(): modes = exchange(modes)]
    broadcast_in_dim x1, local copies, waits for them, and re-layouts: 0.74 us -> 0.09 us  [on_device(): jnp.broadcast_to(offsets[:, None, None], (c, cy, LANES))]
  transfers between devices with their start and end apart: 1 -> 1, of which waited for: 1 -> 1; matrix products, arithmetic and copies ran while one was open for 1% -> 0% of each run, Pallas kernels for 4% -> 1%
where the time goes in v2:
time: 52.4 us; the launch traced here: 52 us
  blocking collectives  33.7 us (64%)
  waiting for transfers between devices  6.92 us (13%)
  local copies, waits for them, and re-layouts  4.41 us (8%)
  Pallas kernels  4.23 us (8%)
  starting transfers between devices  2.71 us (5%)
    all_to_all x1, blocking collectives, on_device(): lines = exchange(lines.reshape(d, plan.rows, LANES))  15.3 us
    all_to_all x1, blocking collectives, on_device(): modes = exchange(modes)  9.24 us
    all_to_all x1, blocking collectives, on_device(): mixed = exchange(mixed.reshape(d, plan.owned, LANES))  9.1 us
    all_to_all x1, waiting for transfers between devices, on_device(): spatial = exchange(spatial)  6.92 us
    unnamed x26, local copies, waits for them, and re-layouts  4.32 us
    all_to_all x1, starting transfers between devices, on_device(): spatial = exchange(spatial)  2.71 us
    pallas_call x1, Pallas kernels, on_device(): call(2, from_modes, plan, shape((d, plan.rows, LANES), bf16))  1.15 us
  transfers between devices with their start and end apart: 1, of which 1 were waited for; matrix products, arithmetic and copies ran while one was open for 0% of the time, Pallas kernels for 1%

profile of v2, /device:TPU:0, one launch (start us, length us, event | category | flops | bytes accessed | tf_op | source)
XLA Modules:
  0.0 52.0 jit_solution(9973620437461387066)
XLA Ops:
  0.0 0.0 copy-start.2
  0.0 0.0 copy-start.1
  0.0 0.0 copy-start.3
  0.0 1.1 %copy-done.3 = bf16[32,4,8,128]{3,2,1,0:T(8,128)(2,1)S(1)} copy-done((bf16[32,4,8,128]{3,2,1,0:T(8,128)(2,1)S(1)}, bf16[32,4,8,128]{3,2,1,0:T(8,128)(2,1)}, u32[]{:S(2)}) %copy-start.3) | copy-done | bytes 262168
  1.1 0.0 copy-start.8
  1.1 0.8 %copy-done.8 = bf16[1,256,128]{2,1,0:T(8,128)(2,1)S(1)} copy-done((bf16[1,256,128]{2,1,0:T(8,128)(2,1)S(1)}, bf16[1,256,128]{2,1,0:T(8,128)(2,1)}, u32[]{:S(2)}) %copy-start.8) | copy-done | bytes 65560
  1.9 0.2 shard_map.118
  2.1 15.3 %all_to_all.20.x_ref = bf16[32,16,128]{2,1,0:T(8,128)(2,1)S(1)} all-to-all(bf16[32,16,128]{2,1,0:T(8,128)(2,1)S(1)} %bitcast.7), channel_id=1, replica_groups=mesh['gx'=8,'gy'=4] {'gx','gy'}, dimensions={0} | all-to-all | bytes 262144 | tf_op jit(solution)/shard_map/all_to_all | solution.py:271
  17.5 0.0 copy-done.2
  17.5 0.0 copy-start.6
  17.5 0.9 %copy-done.6 = f32[2,256,128]{2,1,0:T(8,128)S(1)} copy-done((f32[2,256,128]{2,1,0:T(8,128)S(1)}, f32[2,256,128]{2,1,0:T(8,128)}, u32[]{:S(2)}) %copy-start.6) | copy-done | bytes 262168
  18.4 0.0 copy-start.5
  18.4 0.5 shard_map.119
  18.9 0.0 copy-start
  18.9 9.2 %all_to_all.21 = bf16[32,8,128]{2,1,0:T(8,128)(2,1)S(1)} all-to-all(bf16[32,8,128]{2,1,0:T(8,128)(2,1)S(1)} %shard_map.119), channel_id=1, replica_groups=mesh['gx'=8,'gy'=4] {'gx','gy'}, dimensions={0} | all-to-all | bytes 131072 | tf_op jit(solution)/shard_map/all_to_all | solution.py:279
  28.1 0.0 copy-done.1
  28.2 0.0 copy-done.5
  28.2 0.0 copy-start.7
  28.2 0.8 %copy-done.7 = bf16[1,128,256]{2,1,0:T(8,128)(2,1)S(1)} copy-done((bf16[1,128,256]{2,1,0:T(8,128)(2,1)S(1)}, bf16[1,128,256]{2,1,0:T(8,128)(2,1)}, u32[]{:S(2)}) %copy-start.7) | copy-done | bytes 65560
  29.0 0.9 %shard_map.120 = bf16[8,4,1,8,128]{4,3,2,1,0:T(8,128)(2,1)S(1)} custom-call(bf16[32,1,8,128]{3,2,1,0:T(8,128)(2,1)S(1)} %bitcast.8, bf16[8,2,32,1024]{3,2,1,0:T(8,128)(2,1)S(1)} %bitcast.5, bf16[1,128,256]{2,1,0:T(8,128)(2,1)S(1)} %copy-done.7, bf16[4,1,256,128]{3,2,1,0:T(8,128)(2,1)S(1)} %copy-done.5), custom_call_target="tpu_custom_call" | custom-call | tf_op jit(solution)/shard_map/pallas_call | solution.py:280
  29.9 9.1 %all_to_all.22.m_ref = bf16[32,8,128]{2,1,0:T(8,128)(2,1)S(1)} all-to-all(bf16[32,8,128]{2,1,0:T(8,128)(2,1)S(1)} %bitcast.9), channel_id=1, replica_groups=mesh['gx'=8,'gy'=4] {'gx','gy'}, dimensions={0} | all-to-all | bytes 131072 | tf_op jit(solution)/shard_map/all_to_all | solution.py:295
  39.0 0.0 copy-done
  39.0 0.0 copy-start.12
  39.0 1.2 %shard_map.121 = bf16[32,16,128]{2,1,0:T(8,128)(2,1)} custom-call(bf16[32,8,128]{2,1,0:T(8,128)(2,1)S(1)} %all_to_all.22.m_ref, bf16[1024,512]{1,0:T(8,128)(2,1)S(1)} %copy-done), custom_call_target="tpu_custom_call" | custom-call | tf_op jit(solution)/shard_map/pallas_call | solution.py:296
  40.1 0.0 copy-start.4
  40.1 2.7 %all-to-all-start.3 = ((bf16[32,16,128]{2,1,0:T(8,128)(2,1)}), bf16[32,16,128]{2,1,0:T(8,128)(2,1)S(1)}, u32[]{:S(2)}, u32[]{:S(2)}) async-start(bf16[32,16,128]{2,1,0:T(8,128)(2,1)} %shard_map.121), calls=%async_computation.3 | async-start | bytes 262144 | tf_op jit(solution)/shard_map/all_to_all | solution.py:299
  42.9 0.0 copy-done.12
  42.9 0.0 copy-start.10
  42.9 0.0 copy-start.11
  42.9 0.1 broadcast_in_dim.2.o_ref
  43.0 0.0 copy-done.4
  43.0 0.6 %copy-done.10 = bf16[4,8,128]{2,1,0:T(8,128)(2,1)S(1)} copy-done((bf16[4,8,128]{2,1,0:T(8,128)(2,1)S(1)}, bf16[4,8,128]{2,1,0:T(8,128)(2,1)}, u32[]{:S(2)}) %copy-start.10) | copy-done | bytes 8216
  43.6 0.0 copy-done.11
  43.6 0.0 copy-start.9
  43.6 0.6 %shard_map.122.b_ref = f32[32,4,8,128]{3,2,1,0:T(8,128)S(1)} custom-call(bf16[32,4,8,128]{3,2,1,0:T(8,128)(2,1)S(1)} %copy-done.4, bf16[4,8,128]{2,1,0:T(8,128)(2,1)S(1)} %copy-done.10, bf16[32,32]{1,0:T(8,128)(2,1)S(1)} %copy-done.11, f32[32,8,128]{2,1,0:T(8,128)S(1)} %broadcast_in_dim.2.o_ref), custom_call_target="tpu_custom_call" | custom-call | flops 1000000000 | bytes 1000000 | tf_op jit(solution)/shard_map/pallas_call | solution.py:272
  44.1 6.9 %all-to-all-done.3 = bf16[32,16,128]{2,1,0:T(8,128)(2,1)S(1)} async-done(((bf16[32,16,128]{2,1,0:T(8,128)(2,1)}), bf16[32,16,128]{2,1,0:T(8,128)(2,1)S(1)}, u32[]{:S(2)}, u32[]{:S(2)}) %all-to-all-start.3) | async-done | bytes 131104 | tf_op jit(solution)/shard_map/all_to_all | solution.py:299
  51.1 0.0 copy-done.9
  51.1 1.0 %shard_map.123 = bf16[32,4,8,128]{3,2,1,0:T(8,128)(2,1)} custom-call(bf16[32,1,16,128]{3,2,1,0:T(8,128)(2,1)S(1)} %bitcast.6, f32[32,4,8,128]{3,2,1,0:T(8,128)S(1)} %shard_map.122.b_ref, bf16[1,2,128,128]{3,2,1,0:T(8,128)(2,1)S(1)} %copy-done.9), custom_call_target="tpu_custom_call" | custom-call | tf_op jit(solution)/shard_map/pallas_call | solution.py:300
Async XLA Ops:
  0.0 17.5 %copy-start.2 = (bf16[512,512]{1,0:T(8,128)(2,1)S(1)}, bf16[512,512]{1,0:T(8,128)(2,1)}, u32[]{:S(2)}) copy-start(bf16[512,512]{1,0:T(8,128)(2,1)} %constant.15.clone.t_ref) | copy-start | bytes 1572868
  0.0 28.1 %copy-start.1 = (bf16[2,4,2,32,1024]{4,3,2,1,0:T(8,128)(2,1)S(1)}, bf16[2,4,2,32,1024]{4,3,2,1,0:T(8,128)(2,1)}, u32[]{:S(2)}) copy-start(bf16[2,4,2,32,1024]{4,3,2,1,0:T(8,128)(2,1)} %param.14) | copy-start | bytes 3145732
  0.0 1.1 %copy-start.3 = (bf16[32,4,8,128]{3,2,1,0:T(8,128)(2,1)S(1)}, bf16[32,4,8,128]{3,2,1,0:T(8,128)(2,1)}, u32[]{:S(2)}) copy-start(bf16[32,4,8,128]{3,2,1,0:T(8,128)(2,1)} %x_ref.3) | copy-start | bytes 786436
  1.1 0.8 %copy-start.8 = (bf16[1,256,128]{2,1,0:T(8,128)(2,1)S(1)}, bf16[1,256,128]{2,1,0:T(8,128)(2,1)}, u32[]{:S(2)}) copy-start(bf16[1,256,128]{2,1,0:T(8,128)(2,1)} %constant.14.clone.f_ref) | copy-start | bytes 196612
  17.5 1.0 %copy-start.6 = (f32[2,256,128]{2,1,0:T(8,128)S(1)}, f32[2,256,128]{2,1,0:T(8,128)}, u32[]{:S(2)}) copy-start(f32[2,256,128]{2,1,0:T(8,128)} %constant.16.clone.phase_ref) | copy-start | bytes 786436
  18.4 9.7 %copy-start.5 = (bf16[4,1,256,128]{3,2,1,0:T(8,128)(2,1)S(1)}, bf16[4,1,256,128]{3,2,1,0:T(8,128)(2,1)}, u32[]{:S(2)}) copy-start(bf16[4,1,256,128]{3,2,1,0:T(8,128)(2,1)} %constant.18.clone.pick_ref) | copy-start | bytes 786436
  18.9 20.1 %copy-start = (bf16[1024,512]{1,0:T(8,128)(2,1)S(1)}, bf16[1024,512]{1,0:T(8,128)(2,1)}, u32[]{:S(2)}) copy-start(bf16[1024,512]{1,0:T(8,128)(2,1)} %constant.19.clone.t_ref) | copy-start | bytes 3145732
  28.2 0.8 %copy-start.7 = (bf16[1,128,256]{2,1,0:T(8,128)(2,1)S(1)}, bf16[1,128,256]{2,1,0:T(8,128)(2,1)}, u32[]{:S(2)}) copy-start(bf16[1,128,256]{2,1,0:T(8,128)(2,1)} %constant.17.clone.spread_ref) | copy-start | bytes 196612
  39.0 3.9 %copy-start.12 = (f32[32]{0:T(128)S(1)}, f32[32]{0:T(128)}, u32[]{:S(2)}) copy-start(f32[32]{0:T(128)} %param.16) | copy-start | bytes 388
  40.1 2.8 %copy-start.4 = (bf16[32,4,8,128]{3,2,1,0:T(8,128)(2,1)S(1)}, bf16[32,4,8,128]{3,2,1,0:T(8,128)(2,1)}, u32[]{:S(2)}) copy-start(bf16[32,4,8,128]{3,2,1,0:T(8,128)(2,1)} %x_ref.3) | copy-start | bytes 786436
  40.1 10.9 %all-to-all-start.3 = ((bf16[32,16,128]{2,1,0:T(8,128)(2,1)}), bf16[32,16,128]{2,1,0:T(8,128)(2,1)S(1)}, u32[]{:S(2)}, u32[]{:S(2)}) async-start(bf16[32,16,128]{2,1,0:T(8,128)(2,1)} %shard_map.121), calls=%async_computation.3 | async-start | bytes 262144 | tf_op jit(solution)/shard_map/all_to_all | solution.py:299
  42.9 0.7 %copy-start.10 = (bf16[4,8,128]{2,1,0:T(8,128)(2,1)S(1)}, bf16[4,8,128]{2,1,0:T(8,128)(2,1)}, u32[]{:S(2)}) copy-start(bf16[4,8,128]{2,1,0:T(8,128)(2,1)} %d_ref.1) | copy-start | bytes 24580
  42.9 0.7 %copy-start.11 = (bf16[32,32]{1,0:T(8,128)(2,1)S(1)}, bf16[32,32]{1,0:T(8,128)(2,1)}, u32[]{:S(2)}) copy-start(bf16[32,32]{1,0:T(8,128)(2,1)} %p_ref.1) | copy-start | bytes 6148
  43.6 7.5 %copy-start.9 = (bf16[1,2,128,128]{3,2,1,0:T(8,128)(2,1)S(1)}, bf16[1,2,128,128]{3,2,1,0:T(8,128)(2,1)}, u32[]{:S(2)}) copy-start(bf16[1,2,128,128]{3,2,1,0:T(8,128)(2,1)} %constant.20.clone.z_ref) | copy-start | bytes 196612

commit v3 on v2

--- a/solution.py
+++ b/solution.py
@@ -35,17 +35,14 @@
         assert nz == LANES and 4 * mz == LANES and channels * mz % LANES == 0
 
     def z_forward(self):
-        z = np.arange(self.nz)[:, None]
-        kz = np.arange(self.mz)[None, :]
-        angle = 2.0 * np.pi / self.nz * (z * kz % self.nz)
-        table = np.zeros((self.slices, 2, self.nz, LANES), np.float32)
-        for s in range(self.slices):
-            part = slice(s * self.mzs, (s + 1) * self.mzs)
-            for h in range(2):
-                at = h * GROUP
-                table[s, h, :, at : at + self.mzs] = np.cos(angle)[:, part]
-                table[s, h, :, at + self.mz : at + self.mz + self.mzs] = -np.sin(angle)[:, part]
-        return table.reshape(self.slices, 2 * self.nz, LANES)
+        shape = (self.slices, 2 * self.nz, LANES)
+        part, row, lane = [lax.broadcasted_iota(jnp.int32, shape, i) for i in range(3)]
+        spot = lane % GROUP
+        kz = part * self.mzs + spot % self.mz
+        angle = 2.0 * math.pi / self.nz * (row * kz % self.nz).astype(jnp.float32)
+        used = (row // self.nz == lane // GROUP) & (spot % self.mz < self.mzs)
+        value = jnp.where(spot < self.mz, jnp.cos(angle), -jnp.sin(angle))
+        return jnp.where(used, value, 0.0).astype(jnp.bfloat16)
 
     def z_inverse(self):
         kz = np.arange(self.mz)[:, None]
@@ -88,13 +85,15 @@
         return np.concatenate([np.cos(angle), np.sin(angle)], axis=0)
 
     def shift_phase(self):
-        mode_x = self.turns()[0]
-        angle = 2.0 * np.pi * (mode_x * self.half % self.nx) / self.nx
+        shape = (self.devices * self.owned, LANES)
+        row, lane = [lax.broadcasted_iota(jnp.int32, shape, i) for i in range(2)]
+        kx = row // (self.ry * self.owned) * self.kxd + row % self.owned // self.kyd
+        kx = jnp.where(kx < self.mx // 2, kx, kx - self.mx)
+        angle = 2.0 * math.pi / self.nx * (kx * self.half % self.nx).astype(jnp.float32)
         scale = 1.0 / math.sqrt(self.nx * self.ny * self.nz)
-        sign = np.where(np.arange(LANES) % GROUP < self.mz, 1.0, -1.0)
-        cosine = np.cos(angle)[:, None] * np.ones(LANES)
-        sine = np.sin(angle)[:, None] * sign
-        return (np.stack([cosine, sine]) * scale).astype(np.float32), scale
+        sine = jnp.sin(angle)
+        sine = jnp.where(lane % GROUP < self.mz, sine, -sine)
+        return jnp.concatenate([jnp.cos(angle), sine], axis=0) * scale
 
     def backward(self):
         halves = []
@@ -105,13 +104,13 @@
 
     def spread(self):
         per = LANES // self.mz
-        table = np.zeros((self.slices, LANES, 2 * LANES), np.float32)
+        table = np.zeros((self.slices, 2, LANES, LANES), np.float32)
         for s in range(self.slices):
             for q in range(2):
                 for k in range(self.mzs):
                     for o in range(per):
-                        table[s, q * self.mz + k, q * LANES + o * self.mz + s * self.mzs + k] = 1
-        return table
+                        table[s, q, q * self.mz + k, o * self.mz + s * self.mzs + k] = 1
+        return table.reshape(-1, LANES)
 
     def pick(self):
         per = LANES // self.mz
@@ -123,7 +122,7 @@
                         row = q * LANES + o * self.mz + s * self.mzs + k
                         for h in range(2):
                             table[o, s, row, h * GROUP + q * self.mz + k] = 1
-        return table
+        return table.reshape(-1, LANES)
 
 
 def dot(a, b):
@@ -135,7 +134,7 @@
 
 
 def to_lines(plan, x_ref, f_ref, out_ref):
-    half, c, cy = plan.half, plan.c, plan.cy
+    half, c = plan.half, plan.c
     x = x_ref[...]
     low = x[:, :half].reshape(c * plan.rows, LANES)
     high = x[:, half:].reshape(c * plan.rows, LANES)
@@ -154,22 +153,26 @@
     up = LANES - plan.mz
     u = cosine + jnp.where(real, pltpu.roll(sine, up, 1), -pltpu.roll(sine, plan.mz, 1))
     other = jnp.where(real, pltpu.roll(u, plan.mz, 1), pltpu.roll(u, up, 1))
-    scale = plan.shift_phase()[1]
-    whole = u * scale + phase_ref[0] * pltpu.roll(u, GROUP, 1) + phase_ref[1] * other
+    scale = 1.0 / math.sqrt(plan.nx * plan.ny * plan.nz)
+    whole = u * scale + phase_ref[:modes] * pltpu.roll(u, GROUP, 1) + phase_ref[modes:] * other
     out_ref[...] = whole.reshape(plan.devices, plan.owned, LANES).astype(jnp.bfloat16)
 
 
-def mix(plan, u_ref, w_ref, spread_ref, pick_ref, out_ref, wide, sums):
+def mix(plan, u_ref, w_ref, t_ref, out_ref, wide, sums):
     c, owned = plan.c, plan.owned
+    spread_rows = 2 * plan.slices * LANES
     blocks = c * plan.mz // LANES
     per = LANES // plan.mz
     u = u_ref[...]
     total = None
     for s in range(plan.slices):
-        part = dot(u[:, s].reshape(c * owned, LANES), spread_ref[s])
-        total = part if total is None else total + part
-    wide[0] = total[:, :LANES]
-    wide[1] = total[:, LANES:]
+        part = [
+            dot(u[:, s].reshape(c * owned, LANES), t_ref[(2 * s + q) * LANES : (2 * s + q + 1) * LANES])
+            for q in range(2)
+        ]
+        total = part if total is None else [a + b for a, b in zip(total, part)]
+    wide[0] = total[0]
+    wide[1] = total[1]
     for m in range(owned):
         u_real = wide[0, pl.ds(m, c, stride=owned), :]
         u_imag = wide[1, pl.ds(m, c, stride=owned), :]
@@ -184,7 +187,8 @@
     mixed = sums[...].astype(jnp.bfloat16)
     for o in range(per):
         for s in range(plan.slices):
-            line = dot(mixed, pick_ref[o, s]).reshape(blocks, owned, LANES)
+            at = spread_rows + (o * plan.slices + s) * 2 * LANES
+            line = dot(mixed, t_ref[at : at + 2 * LANES]).reshape(blocks, owned, LANES)
             out_ref[:, o, s] = line.astype(jnp.bfloat16)
 
 
@@ -266,19 +270,18 @@
         return jnp.asarray(np.asarray(values, np.float32).astype(bf16))
 
     lines = call(2, to_lines, plan, shape((c, s, plan.rows, LANES), bf16))(
-        inputs, table(plan.z_forward())
+        inputs, plan.z_forward()
     )
     lines = exchange(lines.reshape(d, plan.rows, LANES))
     base = call(
         4, local_terms, plan, shape((c, cx, cy, nz), jnp.float32), flops=10**9, moved=10**6
     )(inputs, diffusion, pointwise, jnp.broadcast_to(offsets[:, None, None], (c, cy, LANES)))
-    phase = plan.shift_phase()[0]
     modes = call(3, to_modes, plan, shape((d, plan.owned, LANES), bf16))(
-        lines, table(plan.forward()), jnp.asarray(phase)
+        lines, table(plan.forward()), plan.shift_phase()
     )
     modes = exchange(modes)
     mixed = call(
-        4,
+        3,
         mix,
         plan,
         shape((c * plan.mz // LANES, LANES // plan.mz, s, plan.owned, LANES), bf16),
@@ -289,8 +292,7 @@
     )(
         modes.reshape(c, s, plan.owned, LANES),
         spectral.reshape(plan.owned, 2, c, c * plan.mz),
-        table(plan.spread()),
-        table(plan.pick()),
+        table(np.concatenate([plan.spread(), plan.pick()], axis=0)),
     )
     mixed = exchange(mixed.reshape(d, plan.owned, LANES))
     spatial = call(2, from_modes, plan, shape((d, plan.rows, LANES), bf16))(

time: 52.4 us -> 51.1 us (0.975)
  blocking collectives: 33.7 us -> 18.3 us
  waiting for transfers between devices: 6.92 us -> 14.3 us
  starting transfers between devices: 2.71 us -> 10 us
  local copies, waits for them, and re-layouts: 4.41 us -> 1.66 us
  other arithmetic: 0 us -> 1.41 us
  Pallas kernels: 4.23 us -> 4.86 us
    all_to_all x1 -> x0, blocking collectives: 15.3 us -> none  [on_device(): lines = exchange(lines.reshape(d, plan.rows, LANES))]
    all_to_all x0 -> x1, waiting for transfers between devices: none -> 7.35 us  [on_device(): lines = exchange(lines.reshape(d, plan.rows, LANES))]
    all_to_all x0 -> x1, starting transfers between devices: none -> 7.33 us  [on_device(): lines = exchange(lines.reshape(d, plan.rows, LANES))]
    unnamed x26 -> x20, local copies, waits for them, and re-layouts: 4.32 us -> 1.57 us
    cos x0 -> x1, other arithmetic: none -> 0.77 us  [shift_phase(): return jnp.concatenate([jnp.cos(angle), sine], axis=0) * scale]
    pallas_call x1, Pallas kernels: 0.22 us -> 0.88 us  [on_device(): call(2, to_lines, plan, shape((c, s, plan.rows, LANES), bf16))]
    convert_element_type x0 -> x1, other arithmetic: none -> 0.58 us  [z_forward(): return jnp.where(used, value, 0.0).astype(jnp.bfloat16)]
  transfers between devices with their start and end apart: 1 -> 2, of which waited for: 1 -> 2; matrix products, arithmetic and copies ran while one was open for 0% -> 2% of each run, Pallas kernels for 1% -> 1%
where the time goes in v3:
time: 51.1 us; the launch traced here: 50.7 us
  blocking collectives  18.3 us (36%)
  waiting for transfers between devices  14.3 us (28%)
  starting transfers between devices  10 us (20%)
  Pallas kernels  4.86 us (10%)
  local copies, waits for them, and re-layouts  1.66 us (3%)
  other arithmetic  1.41 us (3%)
    all_to_all x1, blocking collectives, on_device(): modes = exchange(modes)  9.24 us
    all_to_all x1, blocking collectives, on_device(): mixed = exchange(mixed.reshape(d, plan.owned, LANES))  9.1 us
    all_to_all x1, waiting for transfers between devices, on_device(): lines = exchange(lines.reshape(d, plan.rows, LANES))  7.35 us
    all_to_all x1, starting transfers between devices, on_device(): lines = exchange(lines.reshape(d, plan.rows, LANES))  7.33 us
    all_to_all x1, waiting for transfers between devices, on_device(): spatial = exchange(spatial)  6.92 us
    all_to_all x1, starting transfers between devices, on_device(): spatial = exchange(spatial)  2.71 us
    unnamed x20, local copies, waits for them, and re-layouts  1.57 us
    pallas_call x1, Pallas kernels, on_device(): call(2, from_modes, plan, shape((d, plan.rows, LANES), bf16))  1.15 us
  transfers between devices with their start and end apart: 2, of which 2 were waited for; matrix products, arithmetic and copies ran while one was open for 2% of the time, Pallas kernels for 1%

profile of v3, /device:TPU:0, one launch (start us, length us, event | category | flops | bytes accessed | tf_op | source)
XLA Modules:
  0.0 50.7 jit_solution(7535840213200602726)
XLA Ops:
  0.0 0.6 %select_convert_fusion.f_ref = bf16[1,256,128]{2,1,0:T(8,128)(2,1)S(1)} fusion(s32[128]{0:T(128)S(1)} %get-tuple-element.12, s32[128]{0:T(128)S(1)} %get-tuple-element.13, s32[128]{0:T(128)S(1)} %get-tuple-element.11, s32[128]{0:T(128)S(1)} %get-tuple-element.14, s32[256]{0:T(256)S(1)} %get-tuple-element.7, s32[256]{0:T(256)S(1)} %get-tuple-element.8, ...), kind=kLoop, calls=%fused_computation.35 | loop fusion | flops 1179648 | bytes 70144 | tf_op jit(solution)/shard_map/convert_element_type | solution.py:45
  0.6 0.0 copy-start.4
  0.6 0.9 %copy-done.4 = bf16[32,4,8,128]{3,2,1,0:T(8,128)(2,1)S(1)} copy-done((bf16[32,4,8,128]{3,2,1,0:T(8,128)(2,1)S(1)}, bf16[32,4,8,128]{3,2,1,0:T(8,128)(2,1)}, u32[]{:S(2)}) %copy-start.4) | copy-done | bytes 262168
  1.6 0.9 %shard_map.91 = bf16[32,1,16,128]{3,2,1,0:T(8,128)(2,1)} custom-call(bf16[32,4,8,128]{3,2,1,0:T(8,128)(2,1)S(1)} %copy-done.4, bf16[1,256,128]{2,1,0:T(8,128)(2,1)S(1)} %select_convert_fusion.f_ref), custom_call_target="tpu_custom_call" | custom-call | tf_op jit(solution)/shard_map/pallas_call | solution.py:272
  2.5 0.0 copy-start.2
  2.5 0.0 copy-start.1
  2.5 7.3 %all-to-all-start = ((bf16[32,16,128]{2,1,0:T(8,128)(2,1)}), bf16[32,16,128]{2,1,0:T(8,128)(2,1)S(1)}, u32[]{:S(2)}, u32[]{:S(2)}) async-start(bf16[32,16,128]{2,1,0:T(8,128)(2,1)} %bitcast), calls=%async_computation | async-start | bytes 262144 | tf_op jit(solution)/shard_map/all_to_all | solution.py:275
  9.8 0.8 %fusion.14 = (f32[256,128]{1,0:T(8,128)S(1)}, f32[256,128]{1,0:T(8,128)S(1)}) fusion(s32[256]{0:T(256)S(1)} %get-tuple-element.15, s32[256]{0:T(256)S(1)} %get-tuple-element.19, pred[256]{0:T(512)(128)(4,1)S(1)} %get-tuple-element.17, s32[256]{0:T(256)S(1)} %get-tuple-element.16, s32[256]{0:T(256)S(1)} %get-tuple-element.20, ...), kind=kLoop, calls=%fused_computation.39 | loop fusion | flops 1310720 | bytes 267904 | tf_op jit(solution)/shard_map/cos | solution.py:96
  10.7 0.0 copy-start.3
  10.7 7.3 %all-to-all-done.x_ref = bf16[32,16,128]{2,1,0:T(8,128)(2,1)S(1)} async-done(((bf16[32,16,128]{2,1,0:T(8,128)(2,1)}), bf16[32,16,128]{2,1,0:T(8,128)(2,1)S(1)}, u32[]{:S(2)}, u32[]{:S(2)}) %all-to-all-start) | async-done | bytes 131104 | tf_op jit(solution)/shard_map/all_to_all | solution.py:275
  18.0 0.0 copy-done.2
  18.0 0.5 shard_map.92
  18.5 0.0 copy-start
  18.5 9.2 %all_to_all.20 = bf16[32,8,128]{2,1,0:T(8,128)(2,1)S(1)} all-to-all(bf16[32,8,128]{2,1,0:T(8,128)(2,1)S(1)} %shard_map.92), channel_id=1, replica_groups=mesh['gx'=8,'gy'=4] {'gx','gy'}, dimensions={0} | all-to-all | bytes 131072 | tf_op jit(solution)/shard_map/all_to_all | solution.py:282
  27.7 0.0 copy-done.1
  27.7 0.0 copy-done.3
  27.8 0.8 %shard_map.93 = bf16[8,4,1,8,128]{4,3,2,1,0:T(8,128)(2,1)S(1)} custom-call(bf16[32,1,8,128]{3,2,1,0:T(8,128)(2,1)S(1)} %bitcast.7, bf16[8,2,32,1024]{3,2,1,0:T(8,128)(2,1)S(1)} %bitcast.5, bf16[1280,128]{1,0:T(8,128)(2,1)S(1)} %copy-done.3), custom_call_target="tpu_custom_call" | custom-call | tf_op jit(solution)/shard_map/pallas_call | solution.py:283
  28.6 9.1 %all_to_all.21.m_ref = bf16[32,8,128]{2,1,0:T(8,128)(2,1)S(1)} all-to-all(bf16[32,8,128]{2,1,0:T(8,128)(2,1)S(1)} %bitcast.8), channel_id=1, replica_groups=mesh['gx'=8,'gy'=4] {'gx','gy'}, dimensions={0} | all-to-all | bytes 131072 | tf_op jit(solution)/shard_map/all_to_all | solution.py:297
  37.7 0.0 copy-done
  37.7 0.0 copy-start.9
  37.7 1.2 %shard_map.94 = bf16[32,16,128]{2,1,0:T(8,128)(2,1)} custom-call(bf16[32,8,128]{2,1,0:T(8,128)(2,1)S(1)} %all_to_all.21.m_ref, bf16[1024,512]{1,0:T(8,128)(2,1)S(1)} %copy-done), custom_call_target="tpu_custom_call" | custom-call | tf_op jit(solution)/shard_map/pallas_call | solution.py:298
  38.9 0.0 copy-start.5
  38.9 2.7 %all-to-all-start.3 = ((bf16[32,16,128]{2,1,0:T(8,128)(2,1)}), bf16[32,16,128]{2,1,0:T(8,128)(2,1)S(1)}, u32[]{:S(2)}, u32[]{:S(2)}) async-start(bf16[32,16,128]{2,1,0:T(8,128)(2,1)} %shard_map.94), calls=%async_computation.3 | async-start | bytes 262144 | tf_op jit(solution)/shard_map/all_to_all | solution.py:301
  41.6 0.0 copy-done.9
  41.6 0.0 copy-start.7
  41.6 0.0 copy-start.8
  41.6 0.1 broadcast_in_dim.11.o_ref
  41.7 0.0 copy-done.5
  41.7 0.6 %copy-done.7 = bf16[4,8,128]{2,1,0:T(8,128)(2,1)S(1)} copy-done((bf16[4,8,128]{2,1,0:T(8,128)(2,1)S(1)}, bf16[4,8,128]{2,1,0:T(8,128)(2,1)}, u32[]{:S(2)}) %copy-start.7) | copy-done | bytes 8216
  42.3 0.0 copy-done.8
  42.3 0.0 copy-start.6
  42.3 0.5 %shard_map.95.b_ref = f32[32,4,8,128]{3,2,1,0:T(8,128)S(1)} custom-call(bf16[32,4,8,128]{3,2,1,0:T(8,128)(2,1)S(1)} %copy-done.5, bf16[4,8,128]{2,1,0:T(8,128)(2,1)S(1)} %copy-done.7, bf16[32,32]{1,0:T(8,128)(2,1)S(1)} %copy-done.8, f32[32,8,128]{2,1,0:T(8,128)S(1)} %broadcast_in_dim.11.o_ref), custom_call_target="tpu_custom_call" | custom-call | flops 1000000000 | bytes 1000000 | tf_op jit(solution)/shard_map/pallas_call | solution.py:276
  42.9 6.9 %all-to-all-done.3 = bf16[32,16,128]{2,1,0:T(8,128)(2,1)S(1)} async-done(((bf16[32,16,128]{2,1,0:T(8,128)(2,1)}), bf16[32,16,128]{2,1,0:T(8,128)(2,1)S(1)}, u32[]{:S(2)}, u32[]{:S(2)}) %all-to-all-start.3) | async-done | bytes 131104 | tf_op jit(solution)/shard_map/all_to_all | solution.py:301
  49.8 0.0 copy-done.6
  49.8 1.0 %shard_map.96 = bf16[32,4,8,128]{3,2,1,0:T(8,128)(2,1)} custom-call(bf16[32,1,16,128]{3,2,1,0:T(8,128)(2,1)S(1)} %bitcast.6, f32[32,4,8,128]{3,2,1,0:T(8,128)S(1)} %shard_map.95.b_ref, bf16[1,2,128,128]{3,2,1,0:T(8,128)(2,1)S(1)} %copy-done.6), custom_call_target="tpu_custom_call" | custom-call | tf_op jit(solution)/shard_map/pallas_call | solution.py:302
  (9 shorter events, 0.1 us)
Async XLA Ops:
  0.6 1.0 %copy-start.4 = (bf16[32,4,8,128]{3,2,1,0:T(8,128)(2,1)S(1)}, bf16[32,4,8,128]{3,2,1,0:T(8,128)(2,1)}, u32[]{:S(2)}) copy-start(bf16[32,4,8,128]{3,2,1,0:T(8,128)(2,1)} %x_ref.3) | copy-start | bytes 786436
  2.5 15.6 %copy-start.2 = (bf16[512,512]{1,0:T(8,128)(2,1)S(1)}, bf16[512,512]{1,0:T(8,128)(2,1)}, u32[]{:S(2)}) copy-start(bf16[512,512]{1,0:T(8,128)(2,1)} %constant.142.clone.t_ref) | copy-start | bytes 1572868
  2.5 25.3 %copy-start.1 = (bf16[2,4,2,32,1024]{4,3,2,1,0:T(8,128)(2,1)S(1)}, bf16[2,4,2,32,1024]{4,3,2,1,0:T(8,128)(2,1)}, u32[]{:S(2)}) copy-start(bf16[2,4,2,32,1024]{4,3,2,1,0:T(8,128)(2,1)} %param.11) | copy-start | bytes 3145732
  2.5 15.5 %all-to-all-start = ((bf16[32,16,128]{2,1,0:T(8,128)(2,1)}), bf16[32,16,128]{2,1,0:T(8,128)(2,1)S(1)}, u32[]{:S(2)}, u32[]{:S(2)}) async-start(bf16[32,16,128]{2,1,0:T(8,128)(2,1)} %bitcast), calls=%async_computation | async-start | bytes 262144 | tf_op jit(solution)/shard_map/all_to_all | solution.py:275
  10.7 17.1 %copy-start.3 = (bf16[1280,128]{1,0:T(8,128)(2,1)S(1)}, bf16[1280,128]{1,0:T(8,128)(2,1)}, u32[]{:S(2)}) copy-start(bf16[1280,128]{1,0:T(8,128)(2,1)} %constant.143.clone.t_ref) | copy-start | bytes 983044
  18.5 19.2 %copy-start = (bf16[1024,512]{1,0:T(8,128)(2,1)S(1)}, bf16[1024,512]{1,0:T(8,128)(2,1)}, u32[]{:S(2)}) copy-start(bf16[1024,512]{1,0:T(8,128)(2,1)} %constant.144.clone.t_ref) | copy-start | bytes 3145732
  37.7 3.9 %copy-start.9 = (f32[32]{0:T(128)S(1)}, f32[32]{0:T(128)}, u32[]{:S(2)}) copy-start(f32[32]{0:T(128)} %param.13) | copy-start | bytes 388
  38.9 2.8 %copy-start.5 = (bf16[32,4,8,128]{3,2,1,0:T(8,128)(2,1)S(1)}, bf16[32,4,8,128]{3,2,1,0:T(8,128)(2,1)}, u32[]{:S(2)}) copy-start(bf16[32,4,8,128]{3,2,1,0:T(8,128)(2,1)} %x_ref.3) | copy-start | bytes 786436
  38.9 10.9 %all-to-all-start.3 = ((bf16[32,16,128]{2,1,0:T(8,128)(2,1)}), bf16[32,16,128]{2,1,0:T(8,128)(2,1)S(1)}, u32[]{:S(2)}, u32[]{:S(2)}) async-start(bf16[32,16,128]{2,1,0:T(8,128)(2,1)} %shard_map.94), calls=%async_computation.3 | async-start | bytes 262144 | tf_op jit(solution)/shard_map/all_to_all | solution.py:301
  41.6 0.7 %copy-start.7 = (bf16[4,8,128]{2,1,0:T(8,128)(2,1)S(1)}, bf16[4,8,128]{2,1,0:T(8,128)(2,1)}, u32[]{:S(2)}) copy-start(bf16[4,8,128]{2,1,0:T(8,128)(2,1)} %d_ref.1) | copy-start | bytes 24580
  41.6 0.7 %copy-start.8 = (bf16[32,32]{1,0:T(8,128)(2,1)S(1)}, bf16[32,32]{1,0:T(8,128)(2,1)}, u32[]{:S(2)}) copy-start(bf16[32,32]{1,0:T(8,128)(2,1)} %p_ref.1) | copy-start | bytes 6148
  42.3 7.5 %copy-start.6 = (bf16[1,2,128,128]{3,2,1,0:T(8,128)(2,1)S(1)}, bf16[1,2,128,128]{3,2,1,0:T(8,128)(2,1)}, u32[]{:S(2)}) copy-start(bf16[1,2,128,128]{3,2,1,0:T(8,128)(2,1)} %constant.145.clone.z_ref) | copy-start | bytes 196612

commit v4 on v0

v4 whole, which is shorter than its diff:
```python
import functools
import math

import jax
import jax.numpy as jnp
import numpy as np
from jax import lax
from jax.experimental import pallas as pl
from jax.experimental.pallas import tpu as pltpu
from jax.sharding import PartitionSpec as P

LANES = 128
GROUP = LANES // 2
QUARTER = LANES // 4


class Plan:
    def __init__(self, ranks_x, ranks_y, inputs, spectral):
        self.rx, self.ry = ranks_x, ranks_y
        self.c, self.cx, self.cy, self.nz = inputs.shape
        self.kxd, self.kyd = spectral.shape[:2]
        self.mz = spectral.shape[4] // self.c
        self.nx, self.ny = self.cx * ranks_x, self.cy * ranks_y
        self.mx, self.my = self.kxd * ranks_x, self.kyd * ranks_y
        self.pairs = self.kyd // 2
        self.blocks = self.c * self.mz // LANES
        self.per = LANES // self.mz
        first = ranks_x // 4
        self.order = [first] + [i for i in range(ranks_x) if i != first]
        assert self.nz == LANES and self.mz == QUARTER and self.kyd % 2 == 0
        assert ranks_y & (ranks_y - 1) == 0 and self.blocks == 8 and self.cy == 8


def dot(a, b):
    return jnp.dot(a, b, preferred_element_type=jnp.float32)


def iota(shape, axis):
    return lax.broadcasted_iota(jnp.int32, shape, axis)


def wave(winding, length):
    return jnp.cos(2.0 * math.pi / length * (winding % length).astype(jnp.float32))


def to_partial(plan, x_ref, *refs):
    outs, (spectrum, pieces, waves) = refs[: plan.ry], refs[plan.ry :]
    rows, c, cx, cy, ny = plan.c * plan.cx * plan.cy, plan.c, plan.cx, plan.cy, plan.ny
    mine = lax.axis_index("gy")
    z, lane = iota((LANES, LANES), 0), iota((LANES, LANES), 1)
    turn = (lane // QUARTER + 1) // 2 * (plan.nz // 4)
    forward = wave(z * (lane % QUARTER) + turn, plan.nz).astype(jnp.bfloat16)
    spectrum[...] = dot(x_ref[...].reshape(rows, LANES), forward)
    half = plan.my // 2
    shape = ((half + 1) * cy, LANES)
    row, lane = iota(shape, 0), iota(shape, 1)
    winding = row // cy * (mine * cy + row % cy) - lane // GROUP * (ny // 4)
    waves[...] = wave(winding + ny, ny)
    low = iota((c, LANES), 1) < GROUP
    for x in range(cx):
        planes = [spectrum[pl.ds(x * cy + y, c, stride=cx * cy), :] for y in range(cy)]
        sums = []
        for k in range(half + 1):
            total = None
            for y in range(cy):
                term = waves[pl.ds(k * cy + y, 1), :] * planes[y]
                total = term if total is None else total + term
            sums.append((total, pltpu.roll(total, GROUP, 1)))
        for i in range(plan.my // 2):
            sides = []
            for side, j in enumerate((2 * i, 2 * i + 1)):
                if j < half:
                    a, b = sums[j]
                    sides.append(a + b)
                else:
                    a, b = sums[plan.my - j]
                    sides.append(b - a if side else a - b)
            value = jnp.where(low, sides[0], sides[1]).astype(jnp.bfloat16)
            pieces[i // plan.pairs, i % plan.pairs, x] = value
    for k in range(plan.ry):
        outs[k][...] = pieces[mine ^ k]


def to_modes(plan, *refs):
    parts, (out_ref, waves) = refs[: plan.ry], refs[plan.ry :]
    c, cx, nx = plan.c, plan.cx, plan.nx
    half = plan.mx // 2
    count = (half + 1) * cx
    row = iota((2 * count, LANES), 0)
    place = lax.axis_index("gx") * cx + row % cx
    winding = row // cx % (half + 1) * place - row // count * (nx // 4)
    waves[...] = wave(winding + nx, nx)
    real = iota((c, LANES), 1) % GROUP < QUARTER
    for p in range(plan.pairs):
        lines, turned = [], []
        for x in range(cx):
            line = sum(part[p, x].astype(jnp.float32) for part in parts)
            lines.append(line)
            up, down = pltpu.roll(line, LANES - QUARTER, 1), pltpu.roll(line, QUARTER, 1)
            turned.append(jnp.where(real, up, -down))
        for k in range(half + 1):
            even = odd = None
            for x in range(cx):
                cosine = waves[pl.ds(k * cx + x, 1), :] * lines[x]
                sine = waves[pl.ds(count + k * cx + x, 1), :] * turned[x]
                even = cosine if even is None else even + cosine
                odd = sine if odd is None else odd + sine
            if k < half:
                owner = plan.order.index(k // plan.kxd)
                out_ref[owner, k % plan.kxd, p] = (even + odd).astype(jnp.bfloat16)
            if k > 0:
                back = plan.mx - k
                owner = plan.order.index(back // plan.kxd)
                out_ref[owner, back % plan.kxd, p] = (even - odd).astype(jnp.bfloat16)


def mix(plan, u_ref, w_ref, out_ref, sums):
    c = plan.c
    scale = 1.0 / math.sqrt(plan.nx * plan.ny * plan.nz)
    group = iota((c, LANES), 1) // QUARTER
    for kx in range(plan.kxd):
        for p in range(plan.pairs):
            u = sum(u_ref[r, kx, p].astype(jnp.float32) for r in range(plan.rx)) * scale
            rolled = [u] + [pltpu.roll(u, v * QUARTER, 1) for v in range(1, 4)]

            def spread(g):
                value = rolled[(3 - g) % 4]
                for j in (2, 1, 0):
                    value = jnp.where(group == j, rolled[(j - g) % 4], value)
                return value

            for side in range(2):
                ky = 2 * p + side
                u_real, u_imag = spread(2 * side), spread(2 * side + 1)
                for j in range(plan.blocks):
                    at = pl.ds(j * LANES, LANES)
                    w_real = w_ref[kx, ky, 0, :, at].astype(jnp.float32)
                    w_imag = w_ref[kx, ky, 1, :, at].astype(jnp.float32)
                    y_real = jnp.sum(w_real * u_real - w_imag * u_imag, axis=0, keepdims=True)
                    y_imag = jnp.sum(w_real * u_imag + w_imag * u_real, axis=0, keepdims=True)
                    sums[ky, kx, 0, pl.ds(j, 1), :] = y_real
                    sums[ky, kx, 1, pl.ds(j, 1), :] = y_imag
    mixed = sums[...].astype(jnp.bfloat16)
    for r in range(plan.rx):
        out_ref[r] = mixed


def from_kx(plan, m_ref, t_ref, out_ref):
    depth = plan.rx * plan.kxd * 2 * plan.blocks
    for ky in range(plan.kyd):
        lines = dot(t_ref[...], m_ref[:, ky].reshape(depth, LANES))
        lines = lines.reshape(plan.cx, 2, plan.blocks, LANES)
        out_ref[:, ky] = lines.astype(jnp.bfloat16)


def local_terms(plan, x_ref, d_ref, p_ref, o_ref, out_ref):
    c, cy = plan.c, plan.cy
    size = c * cy
    row = iota((size, c), 0) // cy
    pick = (row == iota((size, c), 1)).astype(jnp.bfloat16)
    spread = dot(pick, p_ref[...]).astype(jnp.bfloat16)
    wide = lax.dot_general(
        spread, pick, (((1,), (1,)), ((), ())), preferred_element_type=jnp.float32
    )
    same = iota((size, size), 0) % cy == iota((size, size), 1) % cy
    mixer = jnp.where(same, wide, 0.0).astype(jnp.bfloat16)
    lane = iota((size, LANES), 1)
    for x in range(plan.cx):
        v = x_ref[:, x].reshape(size, LANES)
        mixing = dot(mixer, v)
        f = v.astype(jnp.float32)
        before = jnp.where(lane == 0, 0.0, pltpu.roll(f, 1, 1))
        after = jnp.where(lane == LANES - 1, 0.0, pltpu.roll(f, LANES - 1, 1))
        curvature = (before + after - 2.0 * f).reshape(c, cy, LANES)
        d = d_ref[x].astype(jnp.float32)
        out_ref[:, x] = mixing.reshape(c, cy, LANES) + d[None] * curvature + o_ref[...]


def finish(plan, *refs):
    parts, (b_ref, y_ref, z_ref, out_ref) = refs[: plan.ry], refs[plan.ry :]
    size = plan.kyd * 2 * plan.blocks
    half = plan.blocks * plan.cy
    for x in range(plan.cx):
        held = jnp.concatenate([part[x].reshape(size, LANES) for part in parts], axis=0)
        lines = dot(y_ref[...], held).astype(jnp.bfloat16)
        lines = jnp.concatenate([lines[:half], lines[half:]], axis=1)
        spectral = dot(lines, z_ref[...])
        for o in range(plan.per):
            v = spectral[:, o * LANES : (o + 1) * LANES].reshape(plan.blocks, plan.cy, LANES)
            v = v + b_ref[:, o, x]
            gelu = 0.5 * v * (1.0 + lax.erf(v * math.sqrt(0.5)))
            out_ref[:, o, x] = gelu.astype(jnp.bfloat16)


def x_table(plan):
    b = plan.blocks
    shape = (plan.cx * 2 * b, plan.rx * plan.kxd * 2 * b)
    row, column = iota(shape, 0), iota(shape, 1)
    order = jnp.asarray(plan.order, jnp.int32)[jnp.arange(shape[1]) // (plan.kxd * 2 * b)]
    kx = order[None, :] * plan.kxd + column // (2 * b) % plan.kxd
    kx = jnp.where(kx < plan.mx // 2, kx, kx - plan.mx)
    x = lax.axis_index("gx") * plan.cx + row // (2 * b)
    turn = (column // b % 2 - row // b % 2) * (plan.nx // 4)
    winding = kx * x + turn + plan.nx * plan.nx
    return jnp.where(row % b == column % b, wave(winding, plan.nx), 0.0).astype(jnp.bfloat16)


def y_table(plan):
    b, cy = plan.blocks, plan.cy
    shape = (2 * b * cy, plan.ry * plan.kyd * 2 * b)
    row, column = iota(shape, 0), iota(shape, 1)
    rank = column // (plan.kyd * 2 * b) ^ lax.axis_index("gy")
    ky = rank * plan.kyd + column // (2 * b) % plan.kyd
    ky = jnp.where(ky < plan.my // 2, ky, ky - plan.my)
    y = lax.axis_index("gy") * cy + row % cy
    turn = (column // b % 2 - row // (b * cy)) * (plan.ny // 4)
    winding = ky * y + turn + plan.ny * plan.ny
    return jnp.where(row // cy % b == column % b, wave(winding, plan.ny), 0.0).astype(jnp.bfloat16)


def z_table(plan):
    row = np.arange(2 * LANES)[:, None]
    column = np.arange(plan.per * LANES)[None, :]
    angle = 2.0 * np.pi / plan.nz * (row % plan.mz * column % plan.nz)
    value = np.where(row < LANES, np.cos(angle), -np.sin(angle))
    value = value / math.sqrt(plan.mx * plan.my * plan.mz)
    value = np.where(row % LANES // plan.mz == column // LANES, value, 0.0)
    return jnp.asarray(value.astype(np.float32).astype(jnp.bfloat16))


def call(n, body, plan, out, scratch=(), flops=0, moved=0):
    vmem = pl.BlockSpec(memory_space=pltpu.VMEM)
    return pl.pallas_call(
        functools.partial(body, plan),
        out_shape=out,
        in_specs=[vmem] * n,
        out_specs=jax.tree.map(lambda _: vmem, out),
        compiler_params=pltpu.CompilerParams(vmem_limit_bytes=16 * 2**20),
        scratch_shapes=list(scratch),
        cost_estimate=pl.CostEstimate(flops=flops, bytes_accessed=moved, transcendentals=0),
    )


def on_device(inputs, diffusion, spectral, pointwise, offsets):
    plan = Plan(lax.axis_size("gx"), lax.axis_size("gy"), inputs, spectral)
    c, cx, cy, nz = inputs.shape
    rx, ry, kxd, kyd, b = plan.rx, plan.ry, plan.kxd, plan.kyd, plan.blocks
    bf16, f32 = jnp.bfloat16, jnp.float32
    shape = jax.ShapeDtypeStruct
    order = [plan.order]

    def swap(value, k):
        return lax.ppermute(value, "gy", [(i, i ^ k) for i in range(ry)]) if k else value

    def exchange(value):
        return lax.all_to_all(
            value, "gx", split_axis=0, concat_axis=0, axis_index_groups=order, tiled=True
        )

    partial = call(
        1,
        to_partial,
        plan,
        [shape((plan.pairs, cx, c, LANES), bf16)] * ry,
        scratch=[
            pltpu.VMEM((c * cx * cy, LANES), f32),
            pltpu.VMEM((ry, plan.pairs, cx, c, LANES), bf16),
            pltpu.VMEM(((plan.my // 2 + 1) * cy, LANES), f32),
        ],
    )(inputs)
    lines = [swap(partial[k], k) for k in range(ry)]
    base = call(4, local_terms, plan, shape((c, cx, cy, nz), f32), flops=10**9, moved=10**6)(
        inputs, diffusion, pointwise, jnp.broadcast_to(offsets[:, None, None], (c, cy, LANES))
    )
    modes = call(
        ry,
        to_modes,
        plan,
        shape((rx, kxd, plan.pairs, c, LANES), bf16),
        scratch=[pltpu.VMEM((2 * (plan.mx // 2 + 1) * cx, LANES), f32)],
    )(*lines)
    modes = exchange(modes)
    mixed = call(
        2,
        mix,
        plan,
        shape((rx, kyd, kxd, 2, b, LANES), bf16),
        scratch=[pltpu.VMEM((kyd, kxd, 2, b, LANES), f32)],
    )(modes, spectral)
    mixed = exchange(mixed)
    held = call(2, from_kx, plan, shape((cx, kyd, 2, b, LANES), bf16))(mixed, x_table(plan))
    parts = [swap(held, k) for k in range(ry)]
    out = call(ry + 3, finish, plan, shape((b, plan.per, cx, cy, nz), bf16))(
        *parts, base.reshape(b, plan.per, cx, cy, nz), y_table(plan), z_table(plan)
    )
    return out.reshape(c, cx, cy, nz)


def solution(mesh):
    in_specs = (
        P(None, "gx", "gy", None),
        P("gx", "gy", None),
        P("gx", "gy", None, None, None),
        P(),
        P(),
    )
    out_specs = P(None, "gx", "gy", None)
    return jax.shard_map(
        on_device, mesh=mesh, in_specs=in_specs, out_specs=out_specs, check_vma=False
    )
```

time: 180 us -> 44.4 us (0.25)
  waiting for transfers between devices: 84.9 us -> 19.9 us
  local copies, waits for them, and re-layouts: 50.7 us -> 1.16 us
  matrix products: 16 us -> 0 us
  between operations: 13.8 us -> 0.25 us
  starting transfers between devices: 8.91 us -> 15.4 us
  Pallas kernels: 0 us -> 5.98 us
  other arithmetic: 5.49 us -> 1.27 us
    all_gather x1 -> x0, waiting for transfers between devices: 50.7 us -> none  [on_device(): lax.all_gather(mixed.reshape(C, 1, owned_x * owned_y * 2 * MZ), ('gx', 'g...]
    reshape x8 -> x0, local copies, waits for them, and re-layouts: 25.8 us -> none  [the longest x1 9.95 us: on_device(): gathered.reshape(C, ranks_x, ranks_y, owned_x, owned_y, 2, MZ)]
    reduce_scatter x1 -> x0, waiting for transfers between devices: 24.5 us -> none  [on_device(): lax.psum_scatter(y_partial.reshape(C, CX, MY * 2 * MZ), 'gy', scatter_dim...]
    unnamed x17 -> x14, local copies, waits for them, and re-layouts: 17.1 us -> 1.07 us
    dot_general x7 -> x0, matrix products: 16 us -> none  [the longest x1 6.48 us: on_device(): jnp.einsum('cabklqz,akqxp->cxblpz', gathered, x_inverse.reshape(ranks_x,...]
    ppermute x0 -> x6, waiting for transfers between devices: none -> 6.21 us  [swap(): lax.ppermute(value, 'gy', [(i, i ^ k) for i in range(ry)])]
    pallas_call x0 -> x6, Pallas kernels: none -> 5.98 us  [the longest x1 1.5 us: on_device(): call(ry + 3, finish, plan, shape((b, plan.per, cx, cy, nz), bf16))]
    ppermute x0 -> x6, starting transfers between devices: none -> 5.69 us  [swap(): lax.ppermute(value, 'gy', [(i, i ^ k) for i in range(ry)])]
  transfers between devices with their start and end apart: 4 -> 8, of which waited for: 4 -> 6; matrix products, arithmetic and copies ran while one was open for 3% -> 3% of each run, Pallas kernels for 0% -> 1%
where the time goes in v4:
time: 44.4 us; the launch traced here: 44 us
  waiting for transfers between devices  19.9 us (45%)
  starting transfers between devices  15.4 us (35%)
  Pallas kernels  5.98 us (13%)
  other arithmetic  1.27 us (3%)
  local copies, waits for them, and re-layouts  1.16 us (3%)
    all_to_all x2, waiting for transfers between devices, exchange(): lax.all_to_all(value, 'gx', split_axis=0, concat_axis=0, axis_index_group...  13.7 us
    all_to_all x2, starting transfers between devices, exchange(): lax.all_to_all(value, 'gx', split_axis=0, concat_axis=0, axis_index_group...  9.76 us
    ppermute x6, waiting for transfers between devices, swap(): lax.ppermute(value, 'gy', [(i, i ^ k) for i in range(ry)])  6.21 us
    ppermute x6, starting transfers between devices, swap(): lax.ppermute(value, 'gy', [(i, i ^ k) for i in range(ry)])  5.69 us
    pallas_call x1, Pallas kernels, on_device(): call(ry + 3, finish, plan, shape((b, plan.per, cx, cy, nz), bf16))  1.5 us
    pallas_call x1, Pallas kernels, on_device(): call(1, to_partial, plan, [shape((plan.pairs, cx, c, LANES), bf16)] * ry,...  1.34 us
    pallas_call x1, Pallas kernels, on_device(): call(2, mix, plan, shape((rx, kyd, kxd, 2, b, LANES), bf16), scratch=[plt...  1.33 us
    pallas_call x1, Pallas kernels, on_device(): call(ry, to_modes, plan, shape((rx, kxd, plan.pairs, c, LANES), bf16), sc...  1.09 us
  transfers between devices with their start and end apart: 8, of which 6 were waited for; matrix products, arithmetic and copies ran while one was open for 3% of the time, Pallas kernels for 1%

profile of v4, /device:TPU:0, one launch (start us, length us, event | category | flops | bytes accessed | tf_op | source)
XLA Modules:
  0.0 44.0 jit_solution(5287297229366265080)
XLA Ops:
  0.0 0.0 copy-start
  0.0 0.0 copy-start.1
  0.0 1.0 %copy-done.1 = bf16[32,4,8,128]{3,2,1,0:T(8,128)(2,1)S(1)} copy-done((bf16[32,4,8,128]{3,2,1,0:T(8,128)(2,1)S(1)}, bf16[32,4,8,128]{3,2,1,0:T(8,128)(2,1)}, u32[]{:S(2)}) %copy-start.1) | copy-done | bytes 262168
  1.0 1.3 %shard_map.73 = (bf16[2,4,32,128]{3,2,1,0:T(8,128)(2,1)S(1)}, bf16[2,4,32,128]{3,2,1,0:T(8,128)(2,1)S(1)}, bf16[2,4,32,128]{3,2,1,0:T(8,128)(2,1)S(1)}, bf16[2,4,32,128]{3,2,1,0:T(8,128)(2,1)S(1)}) custom-call(bf16[32,4,8,128]{3,2,1,0:T(8,128)(2,1)S(1)} %copy-done.1), custom_call_target="tpu_custom_call" | custom-call | tf_op jit(solution)/shard_map/pallas_call | solution.py:260
  2.4 0.6 %collective-permute-start = (bf16[2,4,32,128]{3,2,1,0:T(8,128)(2,1)S(1)}, bf16[2,4,32,128]{3,2,1,0:T(8,128)(2,1)S(1)}, u32[]{:S(2)}, u32[]{:S(2)}) collective-permute-start(bf16[2,4,32,128]{3,2,1,0:T(8,128)(2,1)S(1)} %get-tuple-element.10), channel_id=1, source_target_pairs={{0,1},{1,0},{2,3},{3,2},{4,5},{5,4},{6,7},{7,6},{8,9},{9,8},{10,11... | collective-permute-start | bytes 196616 | tf_op jit(solution)/shard_map/ppermute | solution.py:253
  3.0 2.6 %collective-permute-start.1 = (bf16[2,4,32,128]{3,2,1,0:T(8,128)(2,1)S(1)}, bf16[2,4,32,128]{3,2,1,0:T(8,128)(2,1)S(1)}, u32[]{:S(2)}, u32[]{:S(2)}) collective-permute-start(bf16[2,4,32,128]{3,2,1,0:T(8,128)(2,1)S(1)} %get-tuple-element.11), channel_id=1, source_target_pairs={{0,2},{1,3},{2,0},{3,1},{4,6},{5,7},{6,4},{7,5},{8,10},{9,11},{10,... | collective-permute-start | bytes 196616 | tf_op jit(solution)/shard_map/ppermute | solution.py:253
  5.5 0.0 collective-permute-start.2
  5.7 0.0 collective-permute-done.refs_1_
  5.7 2.5 %collective-permute-done.1.refs_2_ = bf16[2,4,32,128]{3,2,1,0:T(8,128)(2,1)S(1)} collective-permute-done((bf16[2,4,32,128]{3,2,1,0:T(8,128)(2,1)S(1)}, bf16[2,4,32,128]{3,2,1,0:T(8,128)(2,1)S(1)}, u32[]{:S(2)}, u32[]{:S(2)}) %collective-permute-start.1) | collective-permute-done | bytes 65568 | tf_op jit(solution)/shard_map/ppermute | solution.py:253
  8.2 1.4 %collective-permute-done.2.refs_3_ = bf16[2,4,32,128]{3,2,1,0:T(8,128)(2,1)S(1)} collective-permute-done((bf16[2,4,32,128]{3,2,1,0:T(8,128)(2,1)S(1)}, bf16[2,4,32,128]{3,2,1,0:T(8,128)(2,1)S(1)}, u32[]{:S(2)}, u32[]{:S(2)}) %collective-permute-start.2) | collective-permute-done | bytes 65568 | tf_op jit(solution)/shard_map/ppermute | solution.py:253
  9.6 1.1 %shard_map.74 = bf16[8,2,2,32,128]{4,3,2,1,0:T(8,128)(2,1)} custom-call(bf16[2,4,32,128]{3,2,1,0:T(8,128)(2,1)S(1)} %get-tuple-element.9.refs_0_, bf16[2,4,32,128]{3,2,1,0:T(8,128)(2,1)S(1)} %collective-permute-done.refs_1_, bf16[2,4,32,128]{3,2,1,0:T(8,128)(2,1)S(1)} %collective-permute-done.1.refs_2_, ...), custom_call_target="tpu_custom_call" | custom-call | tf_op jit(solution)/shard_map/pallas_call | solution.py:275
  10.7 6.4 %all-to-all-start = ((bf16[8,2,2,32,128]{4,3,2,1,0:T(8,128)(2,1)}), bf16[8,2,2,32,128]{4,3,2,1,0:T(8,128)(2,1)S(1)}, u32[]{:S(2)}, u32[]{:S(2)}) async-start(bf16[8,2,2,32,128]{4,3,2,1,0:T(8,128)(2,1)} %shard_map.74), calls=%async_computation | async-start | bytes 524288 | tf_op jit(solution)/shard_map/all_to_all | solution.py:256
  17.1 8.6 %all-to-all-done.u_ref = bf16[8,2,2,32,128]{4,3,2,1,0:T(8,128)(2,1)S(1)} async-done(((bf16[8,2,2,32,128]{4,3,2,1,0:T(8,128)(2,1)}), bf16[8,2,2,32,128]{4,3,2,1,0:T(8,128)(2,1)S(1)}, u32[]{:S(2)}, u32[]{:S(2)}) %all-to-all-start) | async-done | bytes 262176 | tf_op jit(solution)/shard_map/all_to_all | solution.py:256
  25.7 0.0 copy-done
  25.7 1.3 %shard_map.75 = bf16[8,4,2,2,8,128]{5,4,3,2,1,0:T(8,128)(2,1)} custom-call(bf16[8,2,2,32,128]{4,3,2,1,0:T(8,128)(2,1)S(1)} %all-to-all-done.u_ref, bf16[2,4,2,32,1024]{4,3,2,1,0:T(8,128)(2,1)S(1)} %copy-done), custom_call_target="tpu_custom_call" | custom-call | tf_op jit(solution)/shard_map/pallas_call | solution.py:283
  27.0 3.4 %all-to-all-start.1 = ((bf16[8,4,2,2,8,128]{5,4,3,2,1,0:T(8,128)(2,1)}), bf16[8,4,2,2,8,128]{5,4,3,2,1,0:T(8,128)(2,1)S(1)}, u32[]{:S(2)}, u32[]{:S(2)}) async-start(bf16[8,4,2,2,8,128]{5,4,3,2,1,0:T(8,128)(2,1)} %shard_map.75), calls=%async_computation.1 | async-start | bytes 524288 | tf_op jit(solution)/shard_map/all_to_all | solution.py:256
  30.4 0.4 fusion.26.t_ref
  30.8 0.7 %fusion.11.refs_5_ = bf16[128,256]{1,0:T(8,128)(2,1)S(1)} fusion(s32[128]{0:T(128)S(1)} %get-tuple-element.35, s32[128]{0:T(128)S(1)} %get-tuple-element.37, s32[256]{0:T(256)S(1)} %get-tuple-element.19, s32[256]{0:T(256)S(1)} %get-tuple-element.24, s32[128]{0:T(128)S(1)} %get-tuple-element.34, s32[128]{0:T(128)S(1)} %get-tuple-element.36, s32[]{:T(128)S(6)} %mul.56, ...), kind=kLoop, calls=%fused_computation.31 | loop fusion | flops 2228224 | bytes 78216 | tf_op jit(solution)/shard_map/convert_element_type | solution.py:218
  31.5 0.0 copy-start.6
  31.6 0.0 copy-start.2
  31.6 5.1 %all-to-all-done.1.m_ref = bf16[8,4,2,2,8,128]{5,4,3,2,1,0:T(8,128)(2,1)S(1)} async-done(((bf16[8,4,2,2,8,128]{5,4,3,2,1,0:T(8,128)(2,1)}), bf16[8,4,2,2,8,128]{5,4,3,2,1,0:T(8,128)(2,1)S(1)}, u32[]{:S(2)}, u32[]{:S(2)}) %all-to-all-start.1) | async-done | bytes 262176 | tf_op jit(solution)/shard_map/all_to_all | solution.py:256
  36.7 0.2 shard_map.76.refs_0_
  36.9 0.0 copy-start.4
  36.9 0.0 copy-start.5
  36.9 0.1 collective-permute-start.5
  37.0 2.4 %collective-permute-start.4 = (bf16[4,4,2,8,128]{4,3,2,1,0:T(8,128)(2,1)S(1)}, bf16[4,4,2,8,128]{4,3,2,1,0:T(8,128)(2,1)S(1)}, u32[]{:S(2)}, u32[]{:S(2)}) collective-permute-start(bf16[4,4,2,8,128]{4,3,2,1,0:T(8,128)(2,1)S(1)} %shard_map.76.refs_0_), channel_id=1, source_target_pairs={{0,2},{1,3},{2,0},{3,1},{4,6},{5,7},{6,4},{7,5},{8,10},{9,11},{10,... | collective-permute-start | bytes 196616 | tf_op jit(solution)/shard_map/ppermute | solution.py:253
  39.4 0.0 collective-permute-start.3
  39.4 0.0 copy-done.6
  39.4 0.1 broadcast_in_dim.17.o_ref
  39.5 0.0 copy-done.2
  39.5 0.0 copy-done.4
  39.6 0.0 copy-done.5
  39.6 0.0 copy-start.3
  39.6 0.6 %shard_map.77 = f32[32,4,8,128]{3,2,1,0:T(8,128)S(1)} custom-call(bf16[32,4,8,128]{3,2,1,0:T(8,128)(2,1)S(1)} %copy-done.2, bf16[4,8,128]{2,1,0:T(8,128)(2,1)S(1)} %copy-done.4, bf16[32,32]{1,0:T(8,128)(2,1)S(1)} %copy-done.5, f32[32,8,128]{2,1,0:T(8,128)S(1)} %broadcast_in_dim.17.o_ref), custom_call_target="tpu_custom_call" | custom-call | flops 1000000000 | bytes 1000000 | tf_op jit(solution)/shard_map/pallas_call | solution.py:272
  40.1 0.5 %collective-permute-done.5.refs_3_ = bf16[4,4,2,8,128]{4,3,2,1,0:T(8,128)(2,1)S(1)} collective-permute-done((bf16[4,4,2,8,128]{4,3,2,1,0:T(8,128)(2,1)S(1)}, bf16[4,4,2,8,128]{4,3,2,1,0:T(8,128)(2,1)S(1)}, u32[]{:S(2)}, u32[]{:S(2)}) %collective-permute-start.5) | collective-permute-done | bytes 65568 | tf_op jit(solution)/shard_map/ppermute | solution.py:253
  40.7 1.8 %collective-permute-done.4.refs_2_ = bf16[4,4,2,8,128]{4,3,2,1,0:T(8,128)(2,1)S(1)} collective-permute-done((bf16[4,4,2,8,128]{4,3,2,1,0:T(8,128)(2,1)S(1)}, bf16[4,4,2,8,128]{4,3,2,1,0:T(8,128)(2,1)S(1)}, u32[]{:S(2)}, u32[]{:S(2)}) %collective-permute-start.4) | collective-permute-done | bytes 65568 | tf_op jit(solution)/shard_map/ppermute | solution.py:253
  42.5 0.0 collective-permute-done.3.refs_1_
  42.5 0.0 copy-done.3
  42.5 1.5 %shard_map.78 = bf16[8,4,4,8,128]{4,3,2,1,0:T(8,128)(2,1)} custom-call(bf16[4,4,2,8,128]{4,3,2,1,0:T(8,128)(2,1)S(1)} %shard_map.76.refs_0_, bf16[4,4,2,8,128]{4,3,2,1,0:T(8,128)(2,1)S(1)} %collective-permute-done.3.refs_1_, bf16[4,4,2,8,128]{4,3,2,1,0:T(8,128)(2,1)S(1)} %collective-permute-done.4.refs_2_, ...), custom_call_target="tpu_custom_call" | custom-call | tf_op jit(solution)/shard_map/pallas_call | solution.py:293
  (20 shorter events, 0.2 us)
Async XLA Ops:
  0.0 25.7 %copy-start = (bf16[2,4,2,32,1024]{4,3,2,1,0:T(8,128)(2,1)S(1)}, bf16[2,4,2,32,1024]{4,3,2,1,0:T(8,128)(2,1)}, u32[]{:S(2)}) copy-start(bf16[2,4,2,32,1024]{4,3,2,1,0:T(8,128)(2,1)} %w_ref.1) | copy-start | bytes 3145732
  0.0 1.0 %copy-start.1 = (bf16[32,4,8,128]{3,2,1,0:T(8,128)(2,1)S(1)}, bf16[32,4,8,128]{3,2,1,0:T(8,128)(2,1)}, u32[]{:S(2)}) copy-start(bf16[32,4,8,128]{3,2,1,0:T(8,128)(2,1)} %x_ref.3) | copy-start | bytes 786436
  2.4 3.3 %collective-permute-start = (bf16[2,4,32,128]{3,2,1,0:T(8,128)(2,1)S(1)}, bf16[2,4,32,128]{3,2,1,0:T(8,128)(2,1)S(1)}, u32[]{:S(2)}, u32[]{:S(2)}) collective-permute-start(bf16[2,4,32,128]{3,2,1,0:T(8,128)(2,1)S(1)} %get-tuple-element.10), channel_id=1, source_target_pairs={{0,1},{1,0},{2,3},{3,2},{4,5},{5,4},{6,7},{7,6},{8,9},{9,8},{10,11... | collective-permute-start | bytes 196616 | tf_op jit(solution)/shard_map/ppermute | solution.py:253
  3.0 5.2 %collective-permute-start.1 = (bf16[2,4,32,128]{3,2,1,0:T(8,128)(2,1)S(1)}, bf16[2,4,32,128]{3,2,1,0:T(8,128)(2,1)S(1)}, u32[]{:S(2)}, u32[]{:S(2)}) collective-permute-start(bf16[2,4,32,128]{3,2,1,0:T(8,128)(2,1)S(1)} %get-tuple-element.11), channel_id=1, source_target_pairs={{0,2},{1,3},{2,0},{3,1},{4,6},{5,7},{6,4},{7,5},{8,10},{9,11},{10,... | collective-permute-start | bytes 196616 | tf_op jit(solution)/shard_map/ppermute | solution.py:253
  5.5 4.1 %collective-permute-start.2 = (bf16[2,4,32,128]{3,2,1,0:T(8,128)(2,1)S(1)}, bf16[2,4,32,128]{3,2,1,0:T(8,128)(2,1)S(1)}, u32[]{:S(2)}, u32[]{:S(2)}) collective-permute-start(bf16[2,4,32,128]{3,2,1,0:T(8,128)(2,1)S(1)} %get-tuple-element.12), channel_id=1, source_target_pairs={{0,3},{1,2},{2,1},{3,0},{4,7},{5,6},{6,5},{7,4},{8,11},{9,10},{10,... | collective-permute-start | bytes 196616 | tf_op jit(solution)/shard_map/ppermute | solution.py:253
  10.7 15.0 %all-to-all-start = ((bf16[8,2,2,32,128]{4,3,2,1,0:T(8,128)(2,1)}), bf16[8,2,2,32,128]{4,3,2,1,0:T(8,128)(2,1)S(1)}, u32[]{:S(2)}, u32[]{:S(2)}) async-start(bf16[8,2,2,32,128]{4,3,2,1,0:T(8,128)(2,1)} %shard_map.74), calls=%async_computation | async-start | bytes 524288 | tf_op jit(solution)/shard_map/all_to_all | solution.py:256
  27.0 9.7 %all-to-all-start.1 = ((bf16[8,4,2,2,8,128]{5,4,3,2,1,0:T(8,128)(2,1)}), bf16[8,4,2,2,8,128]{5,4,3,2,1,0:T(8,128)(2,1)S(1)}, u32[]{:S(2)}, u32[]{:S(2)}) async-start(bf16[8,4,2,2,8,128]{5,4,3,2,1,0:T(8,128)(2,1)} %shard_map.75), calls=%async_computation.1 | async-start | bytes 524288 | tf_op jit(solution)/shard_map/all_to_all | solution.py:256
  31.5 7.9 %copy-start.6 = (f32[32]{0:T(128)S(1)}, f32[32]{0:T(128)}, u32[]{:S(2)}) copy-start(f32[32]{0:T(128)} %param.11) | copy-start | bytes 388
  31.6 8.0 %copy-start.2 = (bf16[32,4,8,128]{3,2,1,0:T(8,128)(2,1)S(1)}, bf16[32,4,8,128]{3,2,1,0:T(8,128)(2,1)}, u32[]{:S(2)}) copy-start(bf16[32,4,8,128]{3,2,1,0:T(8,128)(2,1)} %x_ref.3) | copy-start | bytes 786436
  36.9 2.7 %copy-start.4 = (bf16[4,8,128]{2,1,0:T(8,128)(2,1)S(1)}, bf16[4,8,128]{2,1,0:T(8,128)(2,1)}, u32[]{:S(2)}) copy-start(bf16[4,8,128]{2,1,0:T(8,128)(2,1)} %d_ref.1) | copy-start | bytes 24580
  36.9 2.7 %copy-start.5 = (bf16[32,32]{1,0:T(8,128)(2,1)S(1)}, bf16[32,32]{1,0:T(8,128)(2,1)}, u32[]{:S(2)}) copy-start(bf16[32,32]{1,0:T(8,128)(2,1)} %p_ref.1) | copy-start | bytes 6148
  36.9 3.8 %collective-permute-start.5 = (bf16[4,4,2,8,128]{4,3,2,1,0:T(8,128)(2,1)S(1)}, bf16[4,4,2,8,128]{4,3,2,1,0:T(8,128)(2,1)S(1)}, u32[]{:S(2)}, u32[]{:S(2)}) collective-permute-start(bf16[4,4,2,8,128]{4,3,2,1,0:T(8,128)(2,1)S(1)} %shard_map.76.refs_0_), channel_id=1, source_target_pairs={{0,3},{1,2},{2,1},{3,0},{4,7},{5,6},{6,5},{7,4},{8,11},{9,10},{10,... | collective-permute-start | bytes 196616 | tf_op jit(solution)/shard_map/ppermute | solution.py:253
  37.0 5.5 %collective-permute-start.4 = (bf16[4,4,2,8,128]{4,3,2,1,0:T(8,128)(2,1)S(1)}, bf16[4,4,2,8,128]{4,3,2,1,0:T(8,128)(2,1)S(1)}, u32[]{:S(2)}, u32[]{:S(2)}) collective-permute-start(bf16[4,4,2,8,128]{4,3,2,1,0:T(8,128)(2,1)S(1)} %shard_map.76.refs_0_), channel_id=1, source_target_pairs={{0,2},{1,3},{2,0},{3,1},{4,6},{5,7},{6,4},{7,5},{8,10},{9,11},{10,... | collective-permute-start | bytes 196616 | tf_op jit(solution)/shard_map/ppermute | solution.py:253
  39.4 3.1 %collective-permute-start.3 = (bf16[4,4,2,8,128]{4,3,2,1,0:T(8,128)(2,1)S(1)}, bf16[4,4,2,8,128]{4,3,2,1,0:T(8,128)(2,1)S(1)}, u32[]{:S(2)}, u32[]{:S(2)}) collective-permute-start(bf16[4,4,2,8,128]{4,3,2,1,0:T(8,128)(2,1)S(1)} %shard_map.76.refs_0_), channel_id=1, source_target_pairs={{0,1},{1,0},{2,3},{3,2},{4,5},{5,4},{6,7},{7,6},{8,9},{9,8},{10,11... | collective-permute-start | bytes 196616 | tf_op jit(solution)/shard_map/ppermute | solution.py:253
  39.6 2.9 %copy-start.3 = (bf16[256,512]{1,0:T(8,128)(2,1)S(1)}, bf16[256,512]{1,0:T(8,128)(2,1)}, u32[]{:S(2)}) copy-start(bf16[256,512]{1,0:T(8,128)(2,1)} %constant.234.clone.refs_6_) | copy-start | bytes 786436

commit v5 on v4

--- a/solution.py
+++ b/solution.py
@@ -43,40 +43,53 @@
     return jnp.cos(2.0 * math.pi / length * (winding % length).astype(jnp.float32))
 
 
-def to_partial(plan, x_ref, *refs):
-    outs, (spectrum, pieces, waves) = refs[: plan.ry], refs[plan.ry :]
-    rows, c, cx, cy, ny = plan.c * plan.cx * plan.cy, plan.c, plan.cx, plan.cy, plan.ny
+def prepare(plan, waves_ref, forward_ref, regroup_ref):
+    cy, ny, size = plan.cy, plan.ny, plan.c * plan.cy
     mine = lax.axis_index("gy")
+    row, lane = iota(waves_ref.shape, 0), iota(waves_ref.shape, 1)
+    winding = row // cy * (mine * cy + row % cy) - lane // GROUP * (ny // 4)
+    waves_ref[...] = wave(winding + ny, ny)
     z, lane = iota((LANES, LANES), 0), iota((LANES, LANES), 1)
     turn = (lane // QUARTER + 1) // 2 * (plan.nz // 4)
-    forward = wave(z * (lane % QUARTER) + turn, plan.nz).astype(jnp.bfloat16)
-    spectrum[...] = dot(x_ref[...].reshape(rows, LANES), forward)
-    half = plan.my // 2
-    shape = ((half + 1) * cy, LANES)
-    row, lane = iota(shape, 0), iota(shape, 1)
-    winding = row // cy * (mine * cy + row % cy) - lane // GROUP * (ny // 4)
-    waves[...] = wave(winding + ny, ny)
-    low = iota((c, LANES), 1) < GROUP
-    for x in range(cx):
-        planes = [spectrum[pl.ds(x * cy + y, c, stride=cx * cy), :] for y in range(cy)]
-        sums = []
-        for k in range(half + 1):
-            total = None
-            for y in range(cy):
-                term = waves[pl.ds(k * cy + y, 1), :] * planes[y]
-                total = term if total is None else total + term
-            sums.append((total, pltpu.roll(total, GROUP, 1)))
-        for i in range(plan.my // 2):
-            sides = []
-            for side, j in enumerate((2 * i, 2 * i + 1)):
-                if j < half:
-                    a, b = sums[j]
-                    sides.append(a + b)
-                else:
-                    a, b = sums[plan.my - j]
-                    sides.append(b - a if side else a - b)
-            value = jnp.where(low, sides[0], sides[1]).astype(jnp.bfloat16)
-            pieces[i // plan.pairs, i % plan.pairs, x] = value
+    forward_ref[...] = wave(z * (lane % QUARTER) + turn, plan.nz).astype(jnp.bfloat16)
+    row, column = iota((size, size), 0), iota((size, size), 1)
+    same = row % plan.c * cy + row // plan.c == column
+    regroup_ref[...] = same.astype(jnp.float32).astype(jnp.bfloat16)
+
+
+def to_partial(plan, x_ref, waves, forward_ref, regroup_ref, *refs):
+    outs, (pieces,) = refs[: plan.ry], refs[plan.ry :]
+    c, cx, cy = plan.c, plan.cx, plan.cy
+    size, half = c * cy, plan.my // 2
+    mine = lax.axis_index("gy")
+    forward, regroup = forward_ref[...], regroup_ref[...]
+    low = iota((c // 2, LANES), 1) < GROUP
+    for x in range(0, cx, 2):
+        pair = [x_ref[:, x + i].reshape(size, LANES) for i in range(2)]
+        pair = dot(regroup, jnp.concatenate(pair, axis=1)).astype(jnp.bfloat16)
+        for i in range(2):
+            spectrum = dot(pair[:, i * LANES : (i + 1) * LANES], forward)
+            for part in range(2):
+                begin = part * (c // 2)
+                planes = [spectrum[y * c + begin : y * c + begin + c // 2] for y in range(cy)]
+                sums = []
+                for k in range(half + 1):
+                    total = None
+                    for y in range(cy):
+                        term = waves[pl.ds(k * cy + y, 1), :] * planes[y]
+                        total = term if total is None else total + term
+                    sums.append((total, pltpu.roll(total, GROUP, 1)))
+                for t in range(plan.my // 2):
+                    sides = []
+                    for side, j in enumerate((2 * t, 2 * t + 1)):
+                        if j < half:
+                            a, b = sums[j]
+                            sides.append(a + b)
+                        else:
+                            a, b = sums[plan.my - j]
+                            sides.append(b - a if side else a - b)
+                    value = jnp.where(low, sides[0], sides[1]).astype(jnp.bfloat16)
+                    pieces[t // plan.pairs, t % plan.pairs, x + i, pl.ds(begin, c // 2)] = value
     for k in range(plan.ry):
         outs[k][...] = pieces[mine ^ k]
 
@@ -177,9 +190,10 @@
 
 
 def finish(plan, *refs):
-    parts, (b_ref, y_ref, z_ref, out_ref) = refs[: plan.ry], refs[plan.ry :]
+    parts, (b_ref, y_ref, z_ref, out_hbm, held_out, sems) = refs[: plan.ry], refs[plan.ry :]
     size = plan.kyd * 2 * plan.blocks
     half = plan.blocks * plan.cy
+    copies = []
     for x in range(plan.cx):
         held = jnp.concatenate([part[x].reshape(size, LANES) for part in parts], axis=0)
         lines = dot(y_ref[...], held).astype(jnp.bfloat16)
@@ -189,7 +203,11 @@
             v = spectral[:, o * LANES : (o + 1) * LANES].reshape(plan.blocks, plan.cy, LANES)
             v = v + b_ref[:, o, x]
             gelu = 0.5 * v * (1.0 + lax.erf(v * math.sqrt(0.5)))
-            out_ref[:, o, x] = gelu.astype(jnp.bfloat16)
+            held_out[x, :, o] = gelu.astype(jnp.bfloat16)
+        copies.append(pltpu.make_async_copy(held_out.at[x], out_hbm.at[:, :, x], sems.at[x]))
+        copies[-1].start()
+    for copy in copies:
+        copy.wait()
 
 
 def x_table(plan):
@@ -228,12 +246,13 @@
     return jnp.asarray(value.astype(np.float32).astype(jnp.bfloat16))
 
 
-def call(n, body, plan, out, scratch=(), flops=0, moved=0):
-    vmem = pl.BlockSpec(memory_space=pltpu.VMEM)
+def call(n, body, plan, out, scratch=(), flops=0, moved=0, outer=(pltpu.VMEM, pltpu.VMEM)):
+    near = pl.BlockSpec(memory_space=outer[0])
+    vmem = pl.BlockSpec(memory_space=outer[1])
     return pl.pallas_call(
         functools.partial(body, plan),
         out_shape=out,
-        in_specs=[vmem] * n,
+        in_specs=[near] * n,
         out_specs=jax.tree.map(lambda _: vmem, out),
         compiler_params=pltpu.CompilerParams(vmem_limit_bytes=16 * 2**20),
         scratch_shapes=list(scratch),
@@ -257,20 +276,33 @@
             value, "gx", split_axis=0, concat_axis=0, axis_index_groups=order, tiled=True
         )
 
+    size = c * cy
+    tables = call(
+        0,
+        prepare,
+        plan,
+        [
+            shape(((plan.my // 2 + 1) * cy, LANES), f32),
+            shape((LANES, LANES), bf16),
+            shape((size, size), bf16),
+        ],
+        flops=10**9,
+        moved=4 * 10**6,
+    )()
     partial = call(
-        1,
+        4,
         to_partial,
         plan,
         [shape((plan.pairs, cx, c, LANES), bf16)] * ry,
-        scratch=[
-            pltpu.VMEM((c * cx * cy, LANES), f32),
-            pltpu.VMEM((ry, plan.pairs, cx, c, LANES), bf16),
-            pltpu.VMEM(((plan.my // 2 + 1) * cy, LANES), f32),
-        ],
-    )(inputs)
+        scratch=[pltpu.VMEM((ry, plan.pairs, cx, c, LANES), bf16)],
+    )(inputs, *tables)
     lines = [swap(partial[k], k) for k in range(ry)]
     base = call(4, local_terms, plan, shape((c, cx, cy, nz), f32), flops=10**9, moved=10**6)(
         inputs, diffusion, pointwise, jnp.broadcast_to(offsets[:, None, None], (c, cy, LANES))
+    )
+    x_inverse, y_inverse = x_table(plan), y_table(plan)
+    lines, base, x_inverse, y_inverse = lax.optimization_barrier(
+        (lines, base, x_inverse, y_inverse)
     )
     modes = call(
         ry,
@@ -288,11 +320,16 @@
         scratch=[pltpu.VMEM((kyd, kxd, 2, b, LANES), f32)],
     )(modes, spectral)
     mixed = exchange(mixed)
-    held = call(2, from_kx, plan, shape((cx, kyd, 2, b, LANES), bf16))(mixed, x_table(plan))
+    held = call(2, from_kx, plan, shape((cx, kyd, 2, b, LANES), bf16))(mixed, x_inverse)
     parts = [swap(held, k) for k in range(ry)]
-    out = call(ry + 3, finish, plan, shape((b, plan.per, cx, cy, nz), bf16))(
-        *parts, base.reshape(b, plan.per, cx, cy, nz), y_table(plan), z_table(plan)
-    )
+    out = call(
+        ry + 3,
+        finish,
+        plan,
+        shape((b, plan.per, cx, cy, nz), bf16),
+        scratch=[pltpu.VMEM((cx, b, plan.per, cy, nz), bf16), pltpu.SemaphoreType.DMA((cx,))],
+        outer=(pltpu.VMEM, pl.ANY),
+    )(*parts, base.reshape(b, plan.per, cx, cy, nz), y_inverse, z_table(plan))
     return out.reshape(c, cx, cy, nz)
 
 

time: 44.4 us -> 42 us (0.946)
  blocking collectives: 0 us -> 24.2 us
  waiting for transfers between devices: 19.9 us -> 5.25 us
  starting transfers between devices: 15.4 us -> 5.08 us
  Pallas kernels: 5.98 us -> 4.4 us
    all_to_all x0 -> x2, blocking collectives: none -> 24.2 us  [exchange(): lax.all_to_all(value, 'gx', split_axis=0, concat_axis=0, axis_index_group...]
    all_to_all x2 -> x0, waiting for transfers between devices: 13.7 us -> none  [exchange(): lax.all_to_all(value, 'gx', split_axis=0, concat_axis=0, axis_index_group...]
    all_to_all x2 -> x0, starting transfers between devices: 9.76 us -> none  [exchange(): lax.all_to_all(value, 'gx', split_axis=0, concat_axis=0, axis_index_group...]
    ppermute x6, waiting for transfers between devices: 6.21 us -> 5.25 us  [swap(): lax.ppermute(value, 'gy', [(i, i ^ k) for i in range(ry)])]
    pallas_call x1, Pallas kernels: 1.09 us -> 0.39 us  [on_device(): call(ry, to_modes, plan, shape((rx, kxd, plan.pairs, c, LANES), bf16), sc...]
    pallas_call x1, Pallas kernels: 1.33 us -> 0.63 us  [on_device(): call(2, mix, plan, shape((rx, kyd, kxd, 2, b, LANES), bf16), scratch=[plt...]
    ppermute x6, starting transfers between devices: 5.69 us -> 5.08 us  [swap(): lax.ppermute(value, 'gy', [(i, i ^ k) for i in range(ry)])]
    pallas_call x2 -> x3, Pallas kernels: 2.84 us -> 2.67 us  [the longest x1 1.47 us: on_device(): call(ry + 3, finish, plan, shape((b, plan.per, cx, cy, nz), bf16), scratc...]
  transfers between devices with their start and end apart: 8 -> 6, of which waited for: 6 -> 3; matrix products, arithmetic and copies ran while one was open for 3% -> 3% of each run, Pallas kernels for 1% -> 1%
where the time goes in v5:
time: 42 us; the launch traced here: 41.7 us
  blocking collectives  24.2 us (58%)
  waiting for transfers between devices  5.25 us (12%)
  starting transfers between devices  5.08 us (12%)
  Pallas kernels  4.4 us (10%)
  other arithmetic  1.27 us (3%)
  local copies, waits for them, and re-layouts  1.22 us (3%)
    all_to_all x2, blocking collectives, exchange(): lax.all_to_all(value, 'gx', split_axis=0, concat_axis=0, axis_index_group...  24.2 us
    ppermute x6, waiting for transfers between devices, swap(): lax.ppermute(value, 'gy', [(i, i ^ k) for i in range(ry)])  5.25 us
    ppermute x6, starting transfers between devices, swap(): lax.ppermute(value, 'gy', [(i, i ^ k) for i in range(ry)])  5.08 us
    pallas_call x1, Pallas kernels, on_device(): call(ry + 3, finish, plan, shape((b, plan.per, cx, cy, nz), bf16), scratc...  1.47 us
    unnamed x12, local copies, waits for them, and re-layouts  1.13 us
  transfers between devices with their start and end apart: 6, of which 3 were waited for; matrix products, arithmetic and copies ran while one was open for 3% of the time, Pallas kernels for 1%

profile of v5, /device:TPU:0, one launch (start us, length us, event | category | flops | bytes accessed | tf_op | source)
XLA Modules:
  0.0 41.7 jit_solution(5178087021696174341)
XLA Ops:
  0.0 0.0 copy-start.1
  0.0 0.4 %shard_map.73 = (f32[72,128]{1,0:T(8,128)S(1)}, bf16[128,128]{1,0:T(8,128)(2,1)S(1)}, bf16[256,256]{1,0:T(8,128)(2,1)S(1)}) custom-call(), custom_call_target="tpu_custom_call" | custom-call | flops 1000000000 | bytes 4000000 | tf_op jit(solution)/shard_map/pallas_call | solution.py:280
  0.4 0.5 %copy-done.1 = bf16[32,4,8,128]{3,2,1,0:T(8,128)(2,1)S(1)} copy-done((bf16[32,4,8,128]{3,2,1,0:T(8,128)(2,1)S(1)}, bf16[32,4,8,128]{3,2,1,0:T(8,128)(2,1)}, u32[]{:S(2)}) %copy-start.1) | copy-done | bytes 262168
  1.0 0.8 %shard_map.74 = (bf16[2,4,32,128]{3,2,1,0:T(8,128)(2,1)S(1)}, bf16[2,4,32,128]{3,2,1,0:T(8,128)(2,1)S(1)}, bf16[2,4,32,128]{3,2,1,0:T(8,128)(2,1)S(1)}, bf16[2,4,32,128]{3,2,1,0:T(8,128)(2,1)S(1)}) custom-call(bf16[32,4,8,128]{3,2,1,0:T(8,128)(2,1)S(1)} %copy-done.1, f32[72,128]{1,0:T(8,128)S(1)} %get-tuple-element.19.waves, ...), custom_call_target="tpu_custom_call" | custom-call | tf_op jit(solution)/shard_map/pallas_call | solution.py:292
  1.7 0.6 %collective-permute-start = (bf16[2,4,32,128]{3,2,1,0:T(8,128)(2,1)S(1)}, bf16[2,4,32,128]{3,2,1,0:T(8,128)(2,1)S(1)}, u32[]{:S(2)}, u32[]{:S(2)}) collective-permute-start(bf16[2,4,32,128]{3,2,1,0:T(8,128)(2,1)S(1)} %get-tuple-element.23), channel_id=1, source_target_pairs={{0,1},{1,0},{2,3},{3,2},{4,5},{5,4},{6,7},{7,6},{8,9},{9,8},{10,11... | collective-permute-start | bytes 196616 | tf_op jit(solution)/shard_map/ppermute | solution.py:272
  2.3 2.6 %collective-permute-start.1 = (bf16[2,4,32,128]{3,2,1,0:T(8,128)(2,1)S(1)}, bf16[2,4,32,128]{3,2,1,0:T(8,128)(2,1)S(1)}, u32[]{:S(2)}, u32[]{:S(2)}) collective-permute-start(bf16[2,4,32,128]{3,2,1,0:T(8,128)(2,1)S(1)} %get-tuple-element.24), channel_id=1, source_target_pairs={{0,2},{1,3},{2,0},{3,1},{4,6},{5,7},{6,4},{7,5},{8,10},{9,11},{10,... | collective-permute-start | bytes 196616 | tf_op jit(solution)/shard_map/ppermute | solution.py:272
  4.8 0.0 collective-permute-start.2
  5.1 0.4 fusion.26.t_ref
  5.5 0.0 copy-start.5
  5.5 0.7 %fusion.11.refs_5_ = bf16[128,256]{1,0:T(8,128)(2,1)S(1)} fusion(s32[128]{0:T(128)S(1)} %get-tuple-element.57, s32[128]{0:T(128)S(1)} %get-tuple-element.59, s32[256]{0:T(256)S(1)} %get-tuple-element.39, s32[256]{0:T(256)S(1)} %get-tuple-element.44, s32[128]{0:T(128)S(1)} %get-tuple-element.56, s32[128]{0:T(128)S(1)} %get-tuple-element.58, s32[]{:T(128)S(6)} %mul.56, ...), kind=kLoop, calls=%fused_computation.31 | loop fusion | flops 2228224 | bytes 78216 | tf_op jit(solution)/shard_map/convert_element_type | solution.py:236
  6.3 0.0 copy-done.5
  6.3 0.0 copy-start.3
  6.3 0.0 copy-start.4
  6.3 0.1 broadcast_in_dim.16.o_ref
  6.4 0.6 %copy-done.3 = bf16[4,8,128]{2,1,0:T(8,128)(2,1)S(1)} copy-done((bf16[4,8,128]{2,1,0:T(8,128)(2,1)S(1)}, bf16[4,8,128]{2,1,0:T(8,128)(2,1)}, u32[]{:S(2)}) %copy-start.3) | copy-done | bytes 8216
  7.0 0.0 copy-done.4
  7.0 0.5 %shard_map.75 = f32[32,4,8,128]{3,2,1,0:T(8,128)S(1)} custom-call(bf16[32,4,8,128]{3,2,1,0:T(8,128)(2,1)S(1)} %copy-done.1, bf16[4,8,128]{2,1,0:T(8,128)(2,1)S(1)} %copy-done.3, bf16[32,32]{1,0:T(8,128)(2,1)S(1)} %copy-done.4, f32[32,8,128]{2,1,0:T(8,128)S(1)} %broadcast_in_dim.16.o_ref), custom_call_target="tpu_custom_call" | custom-call | flops 1000000000 | bytes 1000000 | tf_op jit(solution)/shard_map/pallas_call | solution.py:300
  7.6 0.0 copy-start
  7.6 0.0 collective-permute-done.refs_1_
  7.6 0.0 collective-permute-done.1.refs_2_
  7.6 1.3 %collective-permute-done.2.refs_3_ = bf16[2,4,32,128]{3,2,1,0:T(8,128)(2,1)S(1)} collective-permute-done((bf16[2,4,32,128]{3,2,1,0:T(8,128)(2,1)S(1)}, bf16[2,4,32,128]{3,2,1,0:T(8,128)(2,1)S(1)}, u32[]{:S(2)}, u32[]{:S(2)}) %collective-permute-start.2) | collective-permute-done | bytes 65568 | tf_op jit(solution)/shard_map/ppermute | solution.py:272
  8.9 0.4 shard_map.76
  9.3 14.8 %all_to_all.10.u_ref = bf16[8,2,2,32,128]{4,3,2,1,0:T(8,128)(2,1)S(1)} all-to-all(bf16[8,2,2,32,128]{4,3,2,1,0:T(8,128)(2,1)S(1)} %shard_map.76), channel_id=1, replica_groups={{8,0,4,12,16,20,24,28},{9,1,5,13,17,21,25,29},{10,2,6,14,18,22,26,30},{..., dimensions={0} | all-to-all | bytes 524288 | tf_op jit(solution)/shard_map/all_to_all | solution.py:275
  24.1 0.0 copy-done
  24.1 0.6 %shard_map.77 = bf16[8,4,2,2,8,128]{5,4,3,2,1,0:T(8,128)(2,1)S(1)} custom-call(bf16[8,2,2,32,128]{4,3,2,1,0:T(8,128)(2,1)S(1)} %all_to_all.10.u_ref, bf16[2,4,2,32,1024]{4,3,2,1,0:T(8,128)(2,1)S(1)} %copy-done), custom_call_target="tpu_custom_call" | custom-call | tf_op jit(solution)/shard_map/pallas_call | solution.py:315
  24.8 9.4 %all_to_all.11.m_ref = bf16[8,4,2,2,8,128]{5,4,3,2,1,0:T(8,128)(2,1)S(1)} all-to-all(bf16[8,4,2,2,8,128]{5,4,3,2,1,0:T(8,128)(2,1)S(1)} %shard_map.77), channel_id=1, replica_groups={{8,0,4,12,16,20,24,28},{9,1,5,13,17,21,25,29},{10,2,6,14,18,22,26,30},{..., dimensions={0} | all-to-all | bytes 524288 | tf_op jit(solution)/shard_map/all_to_all | solution.py:275
  34.1 0.0 copy-start.2
  34.1 0.2 shard_map.78.refs_0_
  34.3 0.1 collective-permute-start.5
  34.4 1.6 %collective-permute-start.4 = (bf16[4,4,2,8,128]{4,3,2,1,0:T(8,128)(2,1)S(1)}, bf16[4,4,2,8,128]{4,3,2,1,0:T(8,128)(2,1)S(1)}, u32[]{:S(2)}, u32[]{:S(2)}) collective-permute-start(bf16[4,4,2,8,128]{4,3,2,1,0:T(8,128)(2,1)S(1)} %shard_map.78.refs_0_), channel_id=1, source_target_pairs={{0,2},{1,3},{2,0},{3,1},{4,6},{5,7},{6,4},{7,5},{8,10},{9,11},{10,... | collective-permute-start | bytes 196616 | tf_op jit(solution)/shard_map/ppermute | solution.py:272
  36.0 0.2 collective-permute-start.3
  36.2 2.4 %collective-permute-done.5.refs_3_ = bf16[4,4,2,8,128]{4,3,2,1,0:T(8,128)(2,1)S(1)} collective-permute-done((bf16[4,4,2,8,128]{4,3,2,1,0:T(8,128)(2,1)S(1)}, bf16[4,4,2,8,128]{4,3,2,1,0:T(8,128)(2,1)S(1)}, u32[]{:S(2)}, u32[]{:S(2)}) %collective-permute-start.5) | collective-permute-done | bytes 65568 | tf_op jit(solution)/shard_map/ppermute | solution.py:272
  38.7 1.5 %collective-permute-done.4.refs_2_ = bf16[4,4,2,8,128]{4,3,2,1,0:T(8,128)(2,1)S(1)} collective-permute-done((bf16[4,4,2,8,128]{4,3,2,1,0:T(8,128)(2,1)S(1)}, bf16[4,4,2,8,128]{4,3,2,1,0:T(8,128)(2,1)S(1)}, u32[]{:S(2)}, u32[]{:S(2)}) %collective-permute-start.4) | collective-permute-done | bytes 65568 | tf_op jit(solution)/shard_map/ppermute | solution.py:272
  40.2 0.0 collective-permute-done.3.refs_1_
  40.2 0.0 copy-done.2
  40.2 1.5 %shard_map.79 = bf16[8,4,4,8,128]{4,3,2,1,0:T(8,128)(2,1)} custom-call(bf16[4,4,2,8,128]{4,3,2,1,0:T(8,128)(2,1)S(1)} %shard_map.78.refs_0_, bf16[4,4,2,8,128]{4,3,2,1,0:T(8,128)(2,1)S(1)} %collective-permute-done.3.refs_1_, bf16[4,4,2,8,128]{4,3,2,1,0:T(8,128)(2,1)S(1)} %collective-permute-done.4.refs_2_, ...), custom_call_target="tpu_custom_call" | custom-call | tf_op jit(solution)/shard_map/pallas_call | solution.py:325
  (19 shorter events, 0.1 us)
Async XLA Ops:
  0.0 0.9 %copy-start.1 = (bf16[32,4,8,128]{3,2,1,0:T(8,128)(2,1)S(1)}, bf16[32,4,8,128]{3,2,1,0:T(8,128)(2,1)}, u32[]{:S(2)}) copy-start(bf16[32,4,8,128]{3,2,1,0:T(8,128)(2,1)} %x_ref.3) | copy-start | bytes 786436
  1.7 5.9 %collective-permute-start = (bf16[2,4,32,128]{3,2,1,0:T(8,128)(2,1)S(1)}, bf16[2,4,32,128]{3,2,1,0:T(8,128)(2,1)S(1)}, u32[]{:S(2)}, u32[]{:S(2)}) collective-permute-start(bf16[2,4,32,128]{3,2,1,0:T(8,128)(2,1)S(1)} %get-tuple-element.23), channel_id=1, source_target_pairs={{0,1},{1,0},{2,3},{3,2},{4,5},{5,4},{6,7},{7,6},{8,9},{9,8},{10,11... | collective-permute-start | bytes 196616 | tf_op jit(solution)/shard_map/ppermute | solution.py:272
  2.3 5.3 %collective-permute-start.1 = (bf16[2,4,32,128]{3,2,1,0:T(8,128)(2,1)S(1)}, bf16[2,4,32,128]{3,2,1,0:T(8,128)(2,1)S(1)}, u32[]{:S(2)}, u32[]{:S(2)}) collective-permute-start(bf16[2,4,32,128]{3,2,1,0:T(8,128)(2,1)S(1)} %get-tuple-element.24), channel_id=1, source_target_pairs={{0,2},{1,3},{2,0},{3,1},{4,6},{5,7},{6,4},{7,5},{8,10},{9,11},{10,... | collective-permute-start | bytes 196616 | tf_op jit(solution)/shard_map/ppermute | solution.py:272
  4.8 4.1 %collective-permute-start.2 = (bf16[2,4,32,128]{3,2,1,0:T(8,128)(2,1)S(1)}, bf16[2,4,32,128]{3,2,1,0:T(8,128)(2,1)S(1)}, u32[]{:S(2)}, u32[]{:S(2)}) collective-permute-start(bf16[2,4,32,128]{3,2,1,0:T(8,128)(2,1)S(1)} %get-tuple-element.25), channel_id=1, source_target_pairs={{0,3},{1,2},{2,1},{3,0},{4,7},{5,6},{6,5},{7,4},{8,11},{9,10},{10,... | collective-permute-start | bytes 196616 | tf_op jit(solution)/shard_map/ppermute | solution.py:272
  5.5 0.8 %copy-start.5 = (f32[32]{0:T(128)S(1)}, f32[32]{0:T(128)}, u32[]{:S(2)}) copy-start(f32[32]{0:T(128)} %param.11) | copy-start | bytes 388
  6.3 0.7 %copy-start.3 = (bf16[4,8,128]{2,1,0:T(8,128)(2,1)S(1)}, bf16[4,8,128]{2,1,0:T(8,128)(2,1)}, u32[]{:S(2)}) copy-start(bf16[4,8,128]{2,1,0:T(8,128)(2,1)} %d_ref.1) | copy-start | bytes 24580
  6.3 0.7 %copy-start.4 = (bf16[32,32]{1,0:T(8,128)(2,1)S(1)}, bf16[32,32]{1,0:T(8,128)(2,1)}, u32[]{:S(2)}) copy-start(bf16[32,32]{1,0:T(8,128)(2,1)} %p_ref.1) | copy-start | bytes 6148
  7.6 16.6 %copy-start = (bf16[2,4,2,32,1024]{4,3,2,1,0:T(8,128)(2,1)S(1)}, bf16[2,4,2,32,1024]{4,3,2,1,0:T(8,128)(2,1)}, u32[]{:S(2)}) copy-start(bf16[2,4,2,32,1024]{4,3,2,1,0:T(8,128)(2,1)} %w_ref.1) | copy-start | bytes 3145732
  34.1 6.0 %copy-start.2 = (bf16[256,512]{1,0:T(8,128)(2,1)S(1)}, bf16[256,512]{1,0:T(8,128)(2,1)}, u32[]{:S(2)}) copy-start(bf16[256,512]{1,0:T(8,128)(2,1)} %constant.234.clone.refs_6_) | copy-start | bytes 786436
  34.3 4.3 %collective-permute-start.5 = (bf16[4,4,2,8,128]{4,3,2,1,0:T(8,128)(2,1)S(1)}, bf16[4,4,2,8,128]{4,3,2,1,0:T(8,128)(2,1)S(1)}, u32[]{:S(2)}, u32[]{:S(2)}) collective-permute-start(bf16[4,4,2,8,128]{4,3,2,1,0:T(8,128)(2,1)S(1)} %shard_map.78.refs_0_), channel_id=1, source_target_pairs={{0,3},{1,2},{2,1},{3,0},{4,7},{5,6},{6,5},{7,4},{8,11},{9,10},{10,... | collective-permute-start | bytes 196616 | tf_op jit(solution)/shard_map/ppermute | solution.py:272
  34.4 5.8 %collective-permute-start.4 = (bf16[4,4,2,8,128]{4,3,2,1,0:T(8,128)(2,1)S(1)}, bf16[4,4,2,8,128]{4,3,2,1,0:T(8,128)(2,1)S(1)}, u32[]{:S(2)}, u32[]{:S(2)}) collective-permute-start(bf16[4,4,2,8,128]{4,3,2,1,0:T(8,128)(2,1)S(1)} %shard_map.78.refs_0_), channel_id=1, source_target_pairs={{0,2},{1,3},{2,0},{3,1},{4,6},{5,7},{6,4},{7,5},{8,10},{9,11},{10,... | collective-permute-start | bytes 196616 | tf_op jit(solution)/shard_map/ppermute | solution.py:272
  36.0 4.2 %collective-permute-start.3 = (bf16[4,4,2,8,128]{4,3,2,1,0:T(8,128)(2,1)S(1)}, bf16[4,4,2,8,128]{4,3,2,1,0:T(8,128)(2,1)S(1)}, u32[]{:S(2)}, u32[]{:S(2)}) collective-permute-start(bf16[4,4,2,8,128]{4,3,2,1,0:T(8,128)(2,1)S(1)} %shard_map.78.refs_0_), channel_id=1, source_target_pairs={{0,1},{1,0},{2,3},{3,2},{4,5},{5,4},{6,7},{7,6},{8,9},{9,8},{10,11... | collective-permute-start | bytes 196616 | tf_op jit(solution)/shard_map/ppermute | solution.py:272

commit v6 on v5

--- a/solution.py
+++ b/solution.py
@@ -8,6 +8,7 @@
 from jax.experimental import pallas as pl
 from jax.experimental.pallas import tpu as pltpu
 from jax.sharding import PartitionSpec as P
+
 
 LANES = 128
 GROUP = LANES // 2
@@ -192,19 +193,22 @@
 def finish(plan, *refs):
     parts, (b_ref, y_ref, z_ref, out_hbm, held_out, sems) = refs[: plan.ry], refs[plan.ry :]
     size = plan.kyd * 2 * plan.blocks
-    half = plan.blocks * plan.cy
-    copies = []
+    half, cy = plan.blocks * plan.cy, plan.cy
+    lines = []
     for x in range(plan.cx):
         held = jnp.concatenate([part[x].reshape(size, LANES) for part in parts], axis=0)
-        lines = dot(y_ref[...], held).astype(jnp.bfloat16)
-        lines = jnp.concatenate([lines[:half], lines[half:]], axis=1)
-        spectral = dot(lines, z_ref[...])
+        line = dot(y_ref[...], held)
+        lines.append(jnp.concatenate([line[:half], line[half:]], axis=1))
+    copies = []
+    for j in range(plan.blocks):
+        rows = jnp.concatenate([line[j * cy : (j + 1) * cy] for line in lines], axis=0)
+        spectral = dot(rows.astype(jnp.bfloat16), z_ref[...])
         for o in range(plan.per):
-            v = spectral[:, o * LANES : (o + 1) * LANES].reshape(plan.blocks, plan.cy, LANES)
-            v = v + b_ref[:, o, x]
+            v = spectral[:, o * LANES : (o + 1) * LANES].reshape(plan.cx, cy, LANES)
+            v = v + b_ref[j, o]
             gelu = 0.5 * v * (1.0 + lax.erf(v * math.sqrt(0.5)))
-            held_out[x, :, o] = gelu.astype(jnp.bfloat16)
-        copies.append(pltpu.make_async_copy(held_out.at[x], out_hbm.at[:, :, x], sems.at[x]))
+            held_out[j, o] = gelu.astype(jnp.bfloat16)
+        copies.append(pltpu.make_async_copy(held_out.at[j], out_hbm.at[j], sems.at[j]))
         copies[-1].start()
     for copy in copies:
         copy.wait()
@@ -269,7 +273,9 @@
     order = [plan.order]
 
     def swap(value, k):
-        return lax.ppermute(value, "gy", [(i, i ^ k) for i in range(ry)]) if k else value
+        if k == 0:
+            return value
+        return lax.ppermute(value, "gy", [(i, i ^ k) for i in range(ry)])
 
     def exchange(value):
         return lax.all_to_all(
@@ -327,7 +333,7 @@
         finish,
         plan,
         shape((b, plan.per, cx, cy, nz), bf16),
-        scratch=[pltpu.VMEM((cx, b, plan.per, cy, nz), bf16), pltpu.SemaphoreType.DMA((cx,))],
+        scratch=[pltpu.VMEM((b, plan.per, cx, cy, nz), bf16), pltpu.SemaphoreType.DMA((b,))],
         outer=(pltpu.VMEM, pl.ANY),
     )(*parts, base.reshape(b, plan.per, cx, cy, nz), y_inverse, z_table(plan))
     return out.reshape(c, cx, cy, nz)

time: 42 us -> 41.8 us (level)
  no operation moved by 1% of the time
where the time goes in v6:
time: 41.8 us; the launch traced here: 41.5 us
  blocking collectives  24.2 us (58%)
  waiting for transfers between devices  5.25 us (13%)
  starting transfers between devices  5.08 us (12%)
  Pallas kernels  4.24 us (10%)
  other arithmetic  1.27 us (3%)
  local copies, waits for them, and re-layouts  1.22 us (3%)
    all_to_all x2, blocking collectives, exchange(): lax.all_to_all(value, 'gx', split_axis=0, concat_axis=0, axis_index_group...  24.2 us
    ppermute x6, waiting for transfers between devices, swap(): return lax.ppermute(value, 'gy', [(i, i ^ k) for i in range(ry)])  5.25 us
    ppermute x6, starting transfers between devices, swap(): return lax.ppermute(value, 'gy', [(i, i ^ k) for i in range(ry)])  5.08 us
    pallas_call x1, Pallas kernels, on_device(): call(ry + 3, finish, plan, shape((b, plan.per, cx, cy, nz), bf16), scratc...  1.3 us
    unnamed x12, local copies, waits for them, and re-layouts  1.13 us
  transfers between devices with their start and end apart: 6, of which 3 were waited for; matrix products, arithmetic and copies ran while one was open for 3% of the time, Pallas kernels for 1%

profile of v6, /device:TPU:0, one launch (start us, length us, event | category | flops | bytes accessed | tf_op | source)
XLA Modules:
  0.0 41.5 jit_solution(2701179615324143077)
XLA Ops:
  0.0 0.0 copy-start.1
  0.0 0.4 %shard_map.73 = (f32[72,128]{1,0:T(8,128)S(1)}, bf16[128,128]{1,0:T(8,128)(2,1)S(1)}, bf16[256,256]{1,0:T(8,128)(2,1)S(1)}) custom-call(), custom_call_target="tpu_custom_call" | custom-call | flops 1000000000 | bytes 4000000 | tf_op jit(solution)/shard_map/pallas_call | solution.py:286
  0.4 0.5 %copy-done.1 = bf16[32,4,8,128]{3,2,1,0:T(8,128)(2,1)S(1)} copy-done((bf16[32,4,8,128]{3,2,1,0:T(8,128)(2,1)S(1)}, bf16[32,4,8,128]{3,2,1,0:T(8,128)(2,1)}, u32[]{:S(2)}) %copy-start.1) | copy-done | bytes 262168
  1.0 0.8 %shard_map.74 = (bf16[2,4,32,128]{3,2,1,0:T(8,128)(2,1)S(1)}, bf16[2,4,32,128]{3,2,1,0:T(8,128)(2,1)S(1)}, bf16[2,4,32,128]{3,2,1,0:T(8,128)(2,1)S(1)}, bf16[2,4,32,128]{3,2,1,0:T(8,128)(2,1)S(1)}) custom-call(bf16[32,4,8,128]{3,2,1,0:T(8,128)(2,1)S(1)} %copy-done.1, f32[72,128]{1,0:T(8,128)S(1)} %get-tuple-element.19.waves, ...), custom_call_target="tpu_custom_call" | custom-call | tf_op jit(solution)/shard_map/pallas_call | solution.py:298
  1.7 0.6 %collective-permute-start = (bf16[2,4,32,128]{3,2,1,0:T(8,128)(2,1)S(1)}, bf16[2,4,32,128]{3,2,1,0:T(8,128)(2,1)S(1)}, u32[]{:S(2)}, u32[]{:S(2)}) collective-permute-start(bf16[2,4,32,128]{3,2,1,0:T(8,128)(2,1)S(1)} %get-tuple-element.23), channel_id=1, source_target_pairs={{0,1},{1,0},{2,3},{3,2},{4,5},{5,4},{6,7},{7,6},{8,9},{9,8},{10,11... | collective-permute-start | bytes 196616 | tf_op jit(solution)/shard_map/ppermute | solution.py:278
  2.3 2.6 %collective-permute-start.1 = (bf16[2,4,32,128]{3,2,1,0:T(8,128)(2,1)S(1)}, bf16[2,4,32,128]{3,2,1,0:T(8,128)(2,1)S(1)}, u32[]{:S(2)}, u32[]{:S(2)}) collective-permute-start(bf16[2,4,32,128]{3,2,1,0:T(8,128)(2,1)S(1)} %get-tuple-element.24), channel_id=1, source_target_pairs={{0,2},{1,3},{2,0},{3,1},{4,6},{5,7},{6,4},{7,5},{8,10},{9,11},{10,... | collective-permute-start | bytes 196616 | tf_op jit(solution)/shard_map/ppermute | solution.py:278
  4.8 0.0 collective-permute-start.2
  5.1 0.4 fusion.26.t_ref
  5.5 0.0 copy-start.5
  5.5 0.7 %fusion.11.refs_5_ = bf16[128,256]{1,0:T(8,128)(2,1)S(1)} fusion(s32[128]{0:T(128)S(1)} %get-tuple-element.57, s32[128]{0:T(128)S(1)} %get-tuple-element.59, s32[256]{0:T(256)S(1)} %get-tuple-element.39, s32[256]{0:T(256)S(1)} %get-tuple-element.44, s32[128]{0:T(128)S(1)} %get-tuple-element.56, s32[128]{0:T(128)S(1)} %get-tuple-element.58, s32[]{:T(128)S(6)} %mul.56, ...), kind=kLoop, calls=%fused_computation.31 | loop fusion | flops 2228224 | bytes 78216 | tf_op jit(solution)/shard_map/convert_element_type | solution.py:240
  6.3 0.0 copy-done.5
  6.3 0.0 copy-start.3
  6.3 0.0 copy-start.4
  6.3 0.1 broadcast_in_dim.16.o_ref
  6.4 0.6 %copy-done.3 = bf16[4,8,128]{2,1,0:T(8,128)(2,1)S(1)} copy-done((bf16[4,8,128]{2,1,0:T(8,128)(2,1)S(1)}, bf16[4,8,128]{2,1,0:T(8,128)(2,1)}, u32[]{:S(2)}) %copy-start.3) | copy-done | bytes 8216
  7.0 0.0 copy-done.4
  7.0 0.5 %shard_map.75 = f32[32,4,8,128]{3,2,1,0:T(8,128)S(1)} custom-call(bf16[32,4,8,128]{3,2,1,0:T(8,128)(2,1)S(1)} %copy-done.1, bf16[4,8,128]{2,1,0:T(8,128)(2,1)S(1)} %copy-done.3, bf16[32,32]{1,0:T(8,128)(2,1)S(1)} %copy-done.4, f32[32,8,128]{2,1,0:T(8,128)S(1)} %broadcast_in_dim.16.o_ref), custom_call_target="tpu_custom_call" | custom-call | flops 1000000000 | bytes 1000000 | tf_op jit(solution)/shard_map/pallas_call | solution.py:306
  7.6 0.0 copy-start
  7.6 0.0 collective-permute-done.refs_1_
  7.6 0.0 collective-permute-done.1.refs_2_
  7.6 1.3 %collective-permute-done.2.refs_3_ = bf16[2,4,32,128]{3,2,1,0:T(8,128)(2,1)S(1)} collective-permute-done((bf16[2,4,32,128]{3,2,1,0:T(8,128)(2,1)S(1)}, bf16[2,4,32,128]{3,2,1,0:T(8,128)(2,1)S(1)}, u32[]{:S(2)}, u32[]{:S(2)}) %collective-permute-start.2) | collective-permute-done | bytes 65568 | tf_op jit(solution)/shard_map/ppermute | solution.py:278
  8.9 0.4 shard_map.76
  9.3 14.8 %all_to_all.10.u_ref = bf16[8,2,2,32,128]{4,3,2,1,0:T(8,128)(2,1)S(1)} all-to-all(bf16[8,2,2,32,128]{4,3,2,1,0:T(8,128)(2,1)S(1)} %shard_map.76), channel_id=1, replica_groups={{8,0,4,12,16,20,24,28},{9,1,5,13,17,21,25,29},{10,2,6,14,18,22,26,30},{..., dimensions={0} | all-to-all | bytes 524288 | tf_op jit(solution)/shard_map/all_to_all | solution.py:281
  24.1 0.0 copy-done
  24.1 0.6 %shard_map.77 = bf16[8,4,2,2,8,128]{5,4,3,2,1,0:T(8,128)(2,1)S(1)} custom-call(bf16[8,2,2,32,128]{4,3,2,1,0:T(8,128)(2,1)S(1)} %all_to_all.10.u_ref, bf16[2,4,2,32,1024]{4,3,2,1,0:T(8,128)(2,1)S(1)} %copy-done), custom_call_target="tpu_custom_call" | custom-call | tf_op jit(solution)/shard_map/pallas_call | solution.py:321
  24.8 9.4 %all_to_all.11.m_ref = bf16[8,4,2,2,8,128]{5,4,3,2,1,0:T(8,128)(2,1)S(1)} all-to-all(bf16[8,4,2,2,8,128]{5,4,3,2,1,0:T(8,128)(2,1)S(1)} %shard_map.77), channel_id=1, replica_groups={{8,0,4,12,16,20,24,28},{9,1,5,13,17,21,25,29},{10,2,6,14,18,22,26,30},{..., dimensions={0} | all-to-all | bytes 524288 | tf_op jit(solution)/shard_map/all_to_all | solution.py:281
  34.1 0.0 copy-start.2
  34.1 0.2 shard_map.78.refs_0_
  34.3 0.1 collective-permute-start.5
  34.4 1.6 %collective-permute-start.4 = (bf16[4,4,2,8,128]{4,3,2,1,0:T(8,128)(2,1)S(1)}, bf16[4,4,2,8,128]{4,3,2,1,0:T(8,128)(2,1)S(1)}, u32[]{:S(2)}, u32[]{:S(2)}) collective-permute-start(bf16[4,4,2,8,128]{4,3,2,1,0:T(8,128)(2,1)S(1)} %shard_map.78.refs_0_), channel_id=1, source_target_pairs={{0,2},{1,3},{2,0},{3,1},{4,6},{5,7},{6,4},{7,5},{8,10},{9,11},{10,... | collective-permute-start | bytes 196616 | tf_op jit(solution)/shard_map/ppermute | solution.py:278
  36.0 0.2 collective-permute-start.3
  36.2 2.4 %collective-permute-done.5.refs_3_ = bf16[4,4,2,8,128]{4,3,2,1,0:T(8,128)(2,1)S(1)} collective-permute-done((bf16[4,4,2,8,128]{4,3,2,1,0:T(8,128)(2,1)S(1)}, bf16[4,4,2,8,128]{4,3,2,1,0:T(8,128)(2,1)S(1)}, u32[]{:S(2)}, u32[]{:S(2)}) %collective-permute-start.5) | collective-permute-done | bytes 65568 | tf_op jit(solution)/shard_map/ppermute | solution.py:278
  38.7 1.5 %collective-permute-done.4.refs_2_ = bf16[4,4,2,8,128]{4,3,2,1,0:T(8,128)(2,1)S(1)} collective-permute-done((bf16[4,4,2,8,128]{4,3,2,1,0:T(8,128)(2,1)S(1)}, bf16[4,4,2,8,128]{4,3,2,1,0:T(8,128)(2,1)S(1)}, u32[]{:S(2)}, u32[]{:S(2)}) %collective-permute-start.4) | collective-permute-done | bytes 65568 | tf_op jit(solution)/shard_map/ppermute | solution.py:278
  40.2 0.0 collective-permute-done.3.refs_1_
  40.2 0.0 copy-done.2
  40.2 1.3 %shard_map.79 = bf16[8,4,4,8,128]{4,3,2,1,0:T(8,128)(2,1)} custom-call(bf16[4,4,2,8,128]{4,3,2,1,0:T(8,128)(2,1)S(1)} %shard_map.78.refs_0_, bf16[4,4,2,8,128]{4,3,2,1,0:T(8,128)(2,1)S(1)} %collective-permute-done.3.refs_1_, bf16[4,4,2,8,128]{4,3,2,1,0:T(8,128)(2,1)S(1)} %collective-permute-done.4.refs_2_, ...), custom_call_target="tpu_custom_call" | custom-call | tf_op jit(solution)/shard_map/pallas_call | solution.py:331
  (19 shorter events, 0.1 us)
Async XLA Ops:
  0.0 0.9 %copy-start.1 = (bf16[32,4,8,128]{3,2,1,0:T(8,128)(2,1)S(1)}, bf16[32,4,8,128]{3,2,1,0:T(8,128)(2,1)}, u32[]{:S(2)}) copy-start(bf16[32,4,8,128]{3,2,1,0:T(8,128)(2,1)} %x_ref.3) | copy-start | bytes 786436
  1.7 5.9 %collective-permute-start = (bf16[2,4,32,128]{3,2,1,0:T(8,128)(2,1)S(1)}, bf16[2,4,32,128]{3,2,1,0:T(8,128)(2,1)S(1)}, u32[]{:S(2)}, u32[]{:S(2)}) collective-permute-start(bf16[2,4,32,128]{3,2,1,0:T(8,128)(2,1)S(1)} %get-tuple-element.23), channel_id=1, source_target_pairs={{0,1},{1,0},{2,3},{3,2},{4,5},{5,4},{6,7},{7,6},{8,9},{9,8},{10,11... | collective-permute-start | bytes 196616 | tf_op jit(solution)/shard_map/ppermute | solution.py:278
  2.3 5.3 %collective-permute-start.1 = (bf16[2,4,32,128]{3,2,1,0:T(8,128)(2,1)S(1)}, bf16[2,4,32,128]{3,2,1,0:T(8,128)(2,1)S(1)}, u32[]{:S(2)}, u32[]{:S(2)}) collective-permute-start(bf16[2,4,32,128]{3,2,1,0:T(8,128)(2,1)S(1)} %get-tuple-element.24), channel_id=1, source_target_pairs={{0,2},{1,3},{2,0},{3,1},{4,6},{5,7},{6,4},{7,5},{8,10},{9,11},{10,... | collective-permute-start | bytes 196616 | tf_op jit(solution)/shard_map/ppermute | solution.py:278
  4.8 4.1 %collective-permute-start.2 = (bf16[2,4,32,128]{3,2,1,0:T(8,128)(2,1)S(1)}, bf16[2,4,32,128]{3,2,1,0:T(8,128)(2,1)S(1)}, u32[]{:S(2)}, u32[]{:S(2)}) collective-permute-start(bf16[2,4,32,128]{3,2,1,0:T(8,128)(2,1)S(1)} %get-tuple-element.25), channel_id=1, source_target_pairs={{0,3},{1,2},{2,1},{3,0},{4,7},{5,6},{6,5},{7,4},{8,11},{9,10},{10,... | collective-permute-start | bytes 196616 | tf_op jit(solution)/shard_map/ppermute | solution.py:278
  5.5 0.8 %copy-start.5 = (f32[32]{0:T(128)S(1)}, f32[32]{0:T(128)}, u32[]{:S(2)}) copy-start(f32[32]{0:T(128)} %param.11) | copy-start | bytes 388
  6.3 0.7 %copy-start.3 = (bf16[4,8,128]{2,1,0:T(8,128)(2,1)S(1)}, bf16[4,8,128]{2,1,0:T(8,128)(2,1)}, u32[]{:S(2)}) copy-start(bf16[4,8,128]{2,1,0:T(8,128)(2,1)} %d_ref.1) | copy-start | bytes 24580
  6.3 0.7 %copy-start.4 = (bf16[32,32]{1,0:T(8,128)(2,1)S(1)}, bf16[32,32]{1,0:T(8,128)(2,1)}, u32[]{:S(2)}) copy-start(bf16[32,32]{1,0:T(8,128)(2,1)} %p_ref.1) | copy-start | bytes 6148
  7.6 16.6 %copy-start = (bf16[2,4,2,32,1024]{4,3,2,1,0:T(8,128)(2,1)S(1)}, bf16[2,4,2,32,1024]{4,3,2,1,0:T(8,128)(2,1)}, u32[]{:S(2)}) copy-start(bf16[2,4,2,32,1024]{4,3,2,1,0:T(8,128)(2,1)} %w_ref.1) | copy-start | bytes 3145732
  34.1 6.0 %copy-start.2 = (bf16[256,512]{1,0:T(8,128)(2,1)S(1)}, bf16[256,512]{1,0:T(8,128)(2,1)}, u32[]{:S(2)}) copy-start(bf16[256,512]{1,0:T(8,128)(2,1)} %constant.234.clone.refs_6_) | copy-start | bytes 786436
  34.3 4.3 %collective-permute-start.5 = (bf16[4,4,2,8,128]{4,3,2,1,0:T(8,128)(2,1)S(1)}, bf16[4,4,2,8,128]{4,3,2,1,0:T(8,128)(2,1)S(1)}, u32[]{:S(2)}, u32[]{:S(2)}) collective-permute-start(bf16[4,4,2,8,128]{4,3,2,1,0:T(8,128)(2,1)S(1)} %shard_map.78.refs_0_), channel_id=1, source_target_pairs={{0,3},{1,2},{2,1},{3,0},{4,7},{5,6},{6,5},{7,4},{8,11},{9,10},{10,... | collective-permute-start | bytes 196616 | tf_op jit(solution)/shard_map/ppermute | solution.py:278
  34.4 5.8 %collective-permute-start.4 = (bf16[4,4,2,8,128]{4,3,2,1,0:T(8,128)(2,1)S(1)}, bf16[4,4,2,8,128]{4,3,2,1,0:T(8,128)(2,1)S(1)}, u32[]{:S(2)}, u32[]{:S(2)}) collective-permute-start(bf16[4,4,2,8,128]{4,3,2,1,0:T(8,128)(2,1)S(1)} %shard_map.78.refs_0_), channel_id=1, source_target_pairs={{0,2},{1,3},{2,0},{3,1},{4,6},{5,7},{6,4},{7,5},{8,10},{9,11},{10,... | collective-permute-start | bytes 196616 | tf_op jit(solution)/shard_map/ppermute | solution.py:278
  36.0 4.2 %collective-permute-start.3 = (bf16[4,4,2,8,128]{4,3,2,1,0:T(8,128)(2,1)S(1)}, bf16[4,4,2,8,128]{4,3,2,1,0:T(8,128)(2,1)S(1)}, u32[]{:S(2)}, u32[]{:S(2)}) collective-permute-start(bf16[4,4,2,8,128]{4,3,2,1,0:T(8,128)(2,1)S(1)} %shard_map.78.refs_0_), channel_id=1, source_target_pairs={{0,1},{1,0},{2,3},{3,2},{4,5},{5,4},{6,7},{7,6},{8,9},{9,8},{10,11... | collective-permute-start | bytes 196616 | tf_op jit(solution)/shard_map/ppermute | solution.py:278

commit v7 on v6

--- a/solution.py
+++ b/solution.py
@@ -26,7 +26,7 @@
         self.pairs = self.kyd // 2
         self.blocks = self.c * self.mz // LANES
         self.per = LANES // self.mz
-        first = ranks_x // 4
+        first = ranks_x // 2 + 1
         self.order = [first] + [i for i in range(ranks_x) if i != first]
         assert self.nz == LANES and self.mz == QUARTER and self.kyd % 2 == 0
         assert ranks_y & (ranks_y - 1) == 0 and self.blocks == 8 and self.cy == 8
@@ -327,7 +327,8 @@
     )(modes, spectral)
     mixed = exchange(mixed)
     held = call(2, from_kx, plan, shape((cx, kyd, 2, b, LANES), bf16))(mixed, x_inverse)
-    parts = [swap(held, k) for k in range(ry)]
+    across = swap(held, 3)
+    parts = [held, swap(held, 1), swap(across, 1), across]
     out = call(
         ry + 3,
         finish,

time: 41.8 us -> 39.5 us (0.945)
  waiting for transfers between devices: 5.25 us -> 3.54 us
  blocking collectives: 24.2 us -> 22.5 us
  starting transfers between devices: 5.08 us -> 6.21 us
    all_to_all x2, blocking collectives: 24.2 us -> 22.5 us  [exchange(): lax.all_to_all(value, 'gx', split_axis=0, concat_axis=0, axis_index_group...]
    ppermute x6, waiting for transfers between devices: 5.25 us -> 3.54 us  [swap(): return lax.ppermute(value, 'gy', [(i, i ^ k) for i in range(ry)])]
    ppermute x6, starting transfers between devices: 5.08 us -> 6.21 us  [swap(): return lax.ppermute(value, 'gy', [(i, i ^ k) for i in range(ry)])]
where the time goes in v7:
time: 39.5 us; the launch traced here: 39.2 us
  blocking collectives  22.5 us (57%)
  starting transfers between devices  6.21 us (16%)
  Pallas kernels  4.24 us (11%)
  waiting for transfers between devices  3.54 us (9%)
  other arithmetic  1.27 us (3%)
  local copies, waits for them, and re-layouts  1.22 us (3%)
    all_to_all x2, blocking collectives, exchange(): lax.all_to_all(value, 'gx', split_axis=0, concat_axis=0, axis_index_group...  22.5 us
    ppermute x6, starting transfers between devices, swap(): return lax.ppermute(value, 'gy', [(i, i ^ k) for i in range(ry)])  6.21 us
    ppermute x6, waiting for transfers between devices, swap(): return lax.ppermute(value, 'gy', [(i, i ^ k) for i in range(ry)])  3.54 us
    pallas_call x1, Pallas kernels, on_device(): call(ry + 3, finish, plan, shape((b, plan.per, cx, cy, nz), bf16), scratc...  1.3 us
    unnamed x12, local copies, waits for them, and re-layouts  1.13 us
  transfers between devices with their start and end apart: 6, of which 3 were waited for; matrix products, arithmetic and copies ran while one was open for 3% of the time, Pallas kernels for 1%

profile of v7, /device:TPU:0, one launch (start us, length us, event | category | flops | bytes accessed | tf_op | source)
XLA Modules:
  0.0 39.2 jit_solution(14610153249495771170)
XLA Ops:
  0.0 0.0 copy-start.1
  0.0 0.4 %shard_map.73 = (f32[72,128]{1,0:T(8,128)S(1)}, bf16[128,128]{1,0:T(8,128)(2,1)S(1)}, bf16[256,256]{1,0:T(8,128)(2,1)S(1)}) custom-call(), custom_call_target="tpu_custom_call" | custom-call | flops 1000000000 | bytes 4000000 | tf_op jit(solution)/shard_map/pallas_call | solution.py:286
  0.4 0.5 %copy-done.1 = bf16[32,4,8,128]{3,2,1,0:T(8,128)(2,1)S(1)} copy-done((bf16[32,4,8,128]{3,2,1,0:T(8,128)(2,1)S(1)}, bf16[32,4,8,128]{3,2,1,0:T(8,128)(2,1)}, u32[]{:S(2)}) %copy-start.1) | copy-done | bytes 262168
  1.0 0.8 %shard_map.74 = (bf16[2,4,32,128]{3,2,1,0:T(8,128)(2,1)S(1)}, bf16[2,4,32,128]{3,2,1,0:T(8,128)(2,1)S(1)}, bf16[2,4,32,128]{3,2,1,0:T(8,128)(2,1)S(1)}, bf16[2,4,32,128]{3,2,1,0:T(8,128)(2,1)S(1)}) custom-call(bf16[32,4,8,128]{3,2,1,0:T(8,128)(2,1)S(1)} %copy-done.1, f32[72,128]{1,0:T(8,128)S(1)} %get-tuple-element.19.waves, ...), custom_call_target="tpu_custom_call" | custom-call | tf_op jit(solution)/shard_map/pallas_call | solution.py:298
  1.7 0.6 %collective-permute-start = (bf16[2,4,32,128]{3,2,1,0:T(8,128)(2,1)S(1)}, bf16[2,4,32,128]{3,2,1,0:T(8,128)(2,1)S(1)}, u32[]{:S(2)}, u32[]{:S(2)}) collective-permute-start(bf16[2,4,32,128]{3,2,1,0:T(8,128)(2,1)S(1)} %get-tuple-element.23), channel_id=1, source_target_pairs={{0,1},{1,0},{2,3},{3,2},{4,5},{5,4},{6,7},{7,6},{8,9},{9,8},{10,11... | collective-permute-start | bytes 196616 | tf_op jit(solution)/shard_map/ppermute | solution.py:278
  2.3 2.6 %collective-permute-start.1 = (bf16[2,4,32,128]{3,2,1,0:T(8,128)(2,1)S(1)}, bf16[2,4,32,128]{3,2,1,0:T(8,128)(2,1)S(1)}, u32[]{:S(2)}, u32[]{:S(2)}) collective-permute-start(bf16[2,4,32,128]{3,2,1,0:T(8,128)(2,1)S(1)} %get-tuple-element.24), channel_id=1, source_target_pairs={{0,2},{1,3},{2,0},{3,1},{4,6},{5,7},{6,4},{7,5},{8,10},{9,11},{10,... | collective-permute-start | bytes 196616 | tf_op jit(solution)/shard_map/ppermute | solution.py:278
  4.8 0.0 collective-permute-start.2
  5.1 0.4 fusion.26.t_ref
  5.5 0.0 copy-start.5
  5.5 0.7 %fusion.11.refs_5_ = bf16[128,256]{1,0:T(8,128)(2,1)S(1)} fusion(s32[128]{0:T(128)S(1)} %get-tuple-element.57, s32[128]{0:T(128)S(1)} %get-tuple-element.59, s32[256]{0:T(256)S(1)} %get-tuple-element.39, s32[256]{0:T(256)S(1)} %get-tuple-element.44, s32[128]{0:T(128)S(1)} %get-tuple-element.56, s32[128]{0:T(128)S(1)} %get-tuple-element.58, s32[]{:T(128)S(6)} %mul.56, ...), kind=kLoop, calls=%fused_computation.31 | loop fusion | flops 2228224 | bytes 78216 | tf_op jit(solution)/shard_map/convert_element_type | solution.py:240
  6.3 0.0 copy-done.5
  6.3 0.0 copy-start.3
  6.3 0.0 copy-start.4
  6.3 0.1 broadcast_in_dim.16.o_ref
  6.4 0.6 %copy-done.3 = bf16[4,8,128]{2,1,0:T(8,128)(2,1)S(1)} copy-done((bf16[4,8,128]{2,1,0:T(8,128)(2,1)S(1)}, bf16[4,8,128]{2,1,0:T(8,128)(2,1)}, u32[]{:S(2)}) %copy-start.3) | copy-done | bytes 8216
  7.0 0.0 copy-done.4
  7.0 0.5 %shard_map.75 = f32[32,4,8,128]{3,2,1,0:T(8,128)S(1)} custom-call(bf16[32,4,8,128]{3,2,1,0:T(8,128)(2,1)S(1)} %copy-done.1, bf16[4,8,128]{2,1,0:T(8,128)(2,1)S(1)} %copy-done.3, bf16[32,32]{1,0:T(8,128)(2,1)S(1)} %copy-done.4, f32[32,8,128]{2,1,0:T(8,128)S(1)} %broadcast_in_dim.16.o_ref), custom_call_target="tpu_custom_call" | custom-call | flops 1000000000 | bytes 1000000 | tf_op jit(solution)/shard_map/pallas_call | solution.py:306
  7.6 0.0 copy-start
  7.6 0.0 collective-permute-done.refs_1_
  7.6 0.0 collective-permute-done.1.refs_2_
  7.6 1.3 %collective-permute-done.2.refs_3_ = bf16[2,4,32,128]{3,2,1,0:T(8,128)(2,1)S(1)} collective-permute-done((bf16[2,4,32,128]{3,2,1,0:T(8,128)(2,1)S(1)}, bf16[2,4,32,128]{3,2,1,0:T(8,128)(2,1)S(1)}, u32[]{:S(2)}, u32[]{:S(2)}) %collective-permute-start.2) | collective-permute-done | bytes 65568 | tf_op jit(solution)/shard_map/ppermute | solution.py:278
  8.9 0.4 shard_map.76
  9.3 13.1 %all_to_all.10.u_ref = bf16[8,2,2,32,128]{4,3,2,1,0:T(8,128)(2,1)S(1)} all-to-all(bf16[8,2,2,32,128]{4,3,2,1,0:T(8,128)(2,1)S(1)} %shard_map.76), channel_id=1, replica_groups={{20,0,4,8,12,16,24,28},{21,1,5,9,13,17,25,29},{22,2,6,10,14,18,26,30},{..., dimensions={0} | all-to-all | bytes 524288 | tf_op jit(solution)/shard_map/all_to_all | solution.py:281
  22.4 0.0 copy-done
  22.4 0.6 %shard_map.77 = bf16[8,4,2,2,8,128]{5,4,3,2,1,0:T(8,128)(2,1)S(1)} custom-call(bf16[8,2,2,32,128]{4,3,2,1,0:T(8,128)(2,1)S(1)} %all_to_all.10.u_ref, bf16[2,4,2,32,1024]{4,3,2,1,0:T(8,128)(2,1)S(1)} %copy-done), custom_call_target="tpu_custom_call" | custom-call | tf_op jit(solution)/shard_map/pallas_call | solution.py:321
  23.0 9.4 %all_to_all.11.m_ref = bf16[8,4,2,2,8,128]{5,4,3,2,1,0:T(8,128)(2,1)S(1)} all-to-all(bf16[8,4,2,2,8,128]{5,4,3,2,1,0:T(8,128)(2,1)S(1)} %shard_map.77), channel_id=1, replica_groups={{20,0,4,8,12,16,24,28},{21,1,5,9,13,17,25,29},{22,2,6,10,14,18,26,30},{..., dimensions={0} | all-to-all | bytes 524288 | tf_op jit(solution)/shard_map/all_to_all | solution.py:281
  32.4 0.0 copy-start.2
  32.4 0.2 shard_map.78.refs_0_
  32.6 0.1 collective-permute-start.4
  32.7 2.4 %collective-permute-start.3 = (bf16[4,4,2,8,128]{4,3,2,1,0:T(8,128)(2,1)S(1)}, bf16[4,4,2,8,128]{4,3,2,1,0:T(8,128)(2,1)S(1)}, u32[]{:S(2)}, u32[]{:S(2)}) collective-permute-start(bf16[4,4,2,8,128]{4,3,2,1,0:T(8,128)(2,1)S(1)} %shard_map.78.refs_0_), channel_id=1, source_target_pairs={{0,1},{1,0},{2,3},{3,2},{4,5},{5,4},{6,7},{7,6},{8,9},{9,8},{10,11... | collective-permute-start | bytes 196616 | tf_op jit(solution)/shard_map/ppermute | solution.py:278
  35.0 1.3 %collective-permute-done.4.refs_3_ = bf16[4,4,2,8,128]{4,3,2,1,0:T(8,128)(2,1)S(1)} collective-permute-done((bf16[4,4,2,8,128]{4,3,2,1,0:T(8,128)(2,1)S(1)}, bf16[4,4,2,8,128]{4,3,2,1,0:T(8,128)(2,1)S(1)}, u32[]{:S(2)}, u32[]{:S(2)}) %collective-permute-start.4) | collective-permute-done | bytes 65568 | tf_op jit(solution)/shard_map/ppermute | solution.py:278
  36.4 0.6 %collective-permute-start.5 = (bf16[4,4,2,8,128]{4,3,2,1,0:T(8,128)(2,1)S(1)}, bf16[4,4,2,8,128]{4,3,2,1,0:T(8,128)(2,1)S(1)}, u32[]{:S(2)}, u32[]{:S(2)}) collective-permute-start(bf16[4,4,2,8,128]{4,3,2,1,0:T(8,128)(2,1)S(1)} %collective-permute-done.4.refs_3_), channel_id=1, source_target_pairs={{0,1},{1,0},{2,3},{3,2},{4,5},{5,4},{6,7},{7,6},{8,9},{9,8},{10,11... | collective-permute-start | bytes 196616 | tf_op jit(solution)/shard_map/ppermute | solution.py:278
  37.0 0.0 collective-permute-done.3.refs_1_
  37.0 0.9 %collective-permute-done.5.refs_2_ = bf16[4,4,2,8,128]{4,3,2,1,0:T(8,128)(2,1)S(1)} collective-permute-done((bf16[4,4,2,8,128]{4,3,2,1,0:T(8,128)(2,1)S(1)}, bf16[4,4,2,8,128]{4,3,2,1,0:T(8,128)(2,1)S(1)}, u32[]{:S(2)}, u32[]{:S(2)}) %collective-permute-start.5) | collective-permute-done | bytes 65568 | tf_op jit(solution)/shard_map/ppermute | solution.py:278
  37.9 0.0 copy-done.2
  37.9 1.3 %shard_map.79 = bf16[8,4,4,8,128]{4,3,2,1,0:T(8,128)(2,1)} custom-call(bf16[4,4,2,8,128]{4,3,2,1,0:T(8,128)(2,1)S(1)} %shard_map.78.refs_0_, bf16[4,4,2,8,128]{4,3,2,1,0:T(8,128)(2,1)S(1)} %collective-permute-done.3.refs_1_, bf16[4,4,2,8,128]{4,3,2,1,0:T(8,128)(2,1)S(1)} %collective-permute-done.5.refs_2_, ...), custom_call_target="tpu_custom_call" | custom-call | tf_op jit(solution)/shard_map/pallas_call | solution.py:332
  (19 shorter events, 0.1 us)
Async XLA Ops:
  0.0 0.9 %copy-start.1 = (bf16[32,4,8,128]{3,2,1,0:T(8,128)(2,1)S(1)}, bf16[32,4,8,128]{3,2,1,0:T(8,128)(2,1)}, u32[]{:S(2)}) copy-start(bf16[32,4,8,128]{3,2,1,0:T(8,128)(2,1)} %x_ref.3) | copy-start | bytes 786436
  1.7 5.9 %collective-permute-start = (bf16[2,4,32,128]{3,2,1,0:T(8,128)(2,1)S(1)}, bf16[2,4,32,128]{3,2,1,0:T(8,128)(2,1)S(1)}, u32[]{:S(2)}, u32[]{:S(2)}) collective-permute-start(bf16[2,4,32,128]{3,2,1,0:T(8,128)(2,1)S(1)} %get-tuple-element.23), channel_id=1, source_target_pairs={{0,1},{1,0},{2,3},{3,2},{4,5},{5,4},{6,7},{7,6},{8,9},{9,8},{10,11... | collective-permute-start | bytes 196616 | tf_op jit(solution)/shard_map/ppermute | solution.py:278
  2.3 5.3 %collective-permute-start.1 = (bf16[2,4,32,128]{3,2,1,0:T(8,128)(2,1)S(1)}, bf16[2,4,32,128]{3,2,1,0:T(8,128)(2,1)S(1)}, u32[]{:S(2)}, u32[]{:S(2)}) collective-permute-start(bf16[2,4,32,128]{3,2,1,0:T(8,128)(2,1)S(1)} %get-tuple-element.24), channel_id=1, source_target_pairs={{0,2},{1,3},{2,0},{3,1},{4,6},{5,7},{6,4},{7,5},{8,10},{9,11},{10,... | collective-permute-start | bytes 196616 | tf_op jit(solution)/shard_map/ppermute | solution.py:278
  4.8 4.1 %collective-permute-start.2 = (bf16[2,4,32,128]{3,2,1,0:T(8,128)(2,1)S(1)}, bf16[2,4,32,128]{3,2,1,0:T(8,128)(2,1)S(1)}, u32[]{:S(2)}, u32[]{:S(2)}) collective-permute-start(bf16[2,4,32,128]{3,2,1,0:T(8,128)(2,1)S(1)} %get-tuple-element.25), channel_id=1, source_target_pairs={{0,3},{1,2},{2,1},{3,0},{4,7},{5,6},{6,5},{7,4},{8,11},{9,10},{10,... | collective-permute-start | bytes 196616 | tf_op jit(solution)/shard_map/ppermute | solution.py:278
  5.5 0.8 %copy-start.5 = (f32[32]{0:T(128)S(1)}, f32[32]{0:T(128)}, u32[]{:S(2)}) copy-start(f32[32]{0:T(128)} %param.11) | copy-start | bytes 388
  6.3 0.7 %copy-start.3 = (bf16[4,8,128]{2,1,0:T(8,128)(2,1)S(1)}, bf16[4,8,128]{2,1,0:T(8,128)(2,1)}, u32[]{:S(2)}) copy-start(bf16[4,8,128]{2,1,0:T(8,128)(2,1)} %d_ref.1) | copy-start | bytes 24580
  6.3 0.7 %copy-start.4 = (bf16[32,32]{1,0:T(8,128)(2,1)S(1)}, bf16[32,32]{1,0:T(8,128)(2,1)}, u32[]{:S(2)}) copy-start(bf16[32,32]{1,0:T(8,128)(2,1)} %p_ref.1) | copy-start | bytes 6148
  7.6 14.8 %copy-start = (bf16[2,4,2,32,1024]{4,3,2,1,0:T(8,128)(2,1)S(1)}, bf16[2,4,2,32,1024]{4,3,2,1,0:T(8,128)(2,1)}, u32[]{:S(2)}) copy-start(bf16[2,4,2,32,1024]{4,3,2,1,0:T(8,128)(2,1)} %w_ref.1) | copy-start | bytes 3145732
  32.4 5.5 %copy-start.2 = (bf16[256,512]{1,0:T(8,128)(2,1)S(1)}, bf16[256,512]{1,0:T(8,128)(2,1)}, u32[]{:S(2)}) copy-start(bf16[256,512]{1,0:T(8,128)(2,1)} %constant.234.clone.refs_6_) | copy-start | bytes 786436
  32.6 3.8 %collective-permute-start.4 = (bf16[4,4,2,8,128]{4,3,2,1,0:T(8,128)(2,1)S(1)}, bf16[4,4,2,8,128]{4,3,2,1,0:T(8,128)(2,1)S(1)}, u32[]{:S(2)}, u32[]{:S(2)}) collective-permute-start(bf16[4,4,2,8,128]{4,3,2,1,0:T(8,128)(2,1)S(1)} %shard_map.78.refs_0_), channel_id=1, source_target_pairs={{0,3},{1,2},{2,1},{3,0},{4,7},{5,6},{6,5},{7,4},{8,11},{9,10},{10,... | collective-permute-start | bytes 196616 | tf_op jit(solution)/shard_map/ppermute | solution.py:278
  32.7 4.3 %collective-permute-start.3 = (bf16[4,4,2,8,128]{4,3,2,1,0:T(8,128)(2,1)S(1)}, bf16[4,4,2,8,128]{4,3,2,1,0:T(8,128)(2,1)S(1)}, u32[]{:S(2)}, u32[]{:S(2)}) collective-permute-start(bf16[4,4,2,8,128]{4,3,2,1,0:T(8,128)(2,1)S(1)} %shard_map.78.refs_0_), channel_id=1, source_target_pairs={{0,1},{1,0},{2,3},{3,2},{4,5},{5,4},{6,7},{7,6},{8,9},{9,8},{10,11... | collective-permute-start | bytes 196616 | tf_op jit(solution)/shard_map/ppermute | solution.py:278
  36.4 1.5 %collective-permute-start.5 = (bf16[4,4,2,8,128]{4,3,2,1,0:T(8,128)(2,1)S(1)}, bf16[4,4,2,8,128]{4,3,2,1,0:T(8,128)(2,1)S(1)}, u32[]{:S(2)}, u32[]{:S(2)}) collective-permute-start(bf16[4,4,2,8,128]{4,3,2,1,0:T(8,128)(2,1)S(1)} %collective-permute-done.4.refs_3_), channel_id=1, source_target_pairs={{0,1},{1,0},{2,3},{3,2},{4,5},{5,4},{6,7},{7,6},{8,9},{9,8},{10,11... | collective-permute-start | bytes 196616 | tf_op jit(solution)/shard_map/ppermute | solution.py:278

commit v8 on v7

--- a/solution.py
+++ b/solution.py
@@ -146,12 +146,14 @@
             for side in range(2):
                 ky = 2 * p + side
                 u_real, u_imag = spread(2 * side), spread(2 * side + 1)
+                u_sum, u_gap = u_real + u_imag, u_imag - u_real
                 for j in range(plan.blocks):
                     at = pl.ds(j * LANES, LANES)
                     w_real = w_ref[kx, ky, 0, :, at].astype(jnp.float32)
                     w_imag = w_ref[kx, ky, 1, :, at].astype(jnp.float32)
-                    y_real = jnp.sum(w_real * u_real - w_imag * u_imag, axis=0, keepdims=True)
-                    y_imag = jnp.sum(w_real * u_imag + w_imag * u_real, axis=0, keepdims=True)
+                    both = jnp.sum((w_real + w_imag) * u_real, axis=0, keepdims=True)
+                    y_real = both - jnp.sum(w_imag * u_sum, axis=0, keepdims=True)
+                    y_imag = both + jnp.sum(w_real * u_gap, axis=0, keepdims=True)
                     sums[ky, kx, 0, pl.ds(j, 1), :] = y_real
                     sums[ky, kx, 1, pl.ds(j, 1), :] = y_imag
     mixed = sums[...].astype(jnp.bfloat16)

time: 39.5 us -> 39.6 us (level)
  no operation moved by 1% of the time
where the time goes in v8:
time: 39.6 us; the launch traced here: 39.2 us
  blocking collectives  22.5 us (57%)
  starting transfers between devices  6.21 us (16%)
  Pallas kernels  4.25 us (11%)
  waiting for transfers between devices  3.54 us (9%)
  other arithmetic  1.27 us (3%)
  local copies, waits for them, and re-layouts  1.22 us (3%)
    all_to_all x2, blocking collectives, exchange(): lax.all_to_all(value, 'gx', split_axis=0, concat_axis=0, axis_index_group...  22.5 us
    ppermute x6, starting transfers between devices, swap(): return lax.ppermute(value, 'gy', [(i, i ^ k) for i in range(ry)])  6.21 us
    ppermute x6, waiting for transfers between devices, swap(): return lax.ppermute(value, 'gy', [(i, i ^ k) for i in range(ry)])  3.54 us
    pallas_call x1, Pallas kernels, on_device(): call(ry + 3, finish, plan, shape((b, plan.per, cx, cy, nz), bf16), scratc...  1.3 us
    unnamed x12, local copies, waits for them, and re-layouts  1.13 us
  transfers between devices with their start and end apart: 6, of which 3 were waited for; matrix products, arithmetic and copies ran while one was open for 3% of the time, Pallas kernels for 1%

profile of v8, /device:TPU:0, one launch (start us, length us, event | category | flops | bytes accessed | tf_op | source)
XLA Modules:
  0.0 39.2 jit_solution(5958086860207271022)
XLA Ops:
  0.0 0.0 copy-start.1
  0.0 0.4 %shard_map.73 = (f32[72,128]{1,0:T(8,128)S(1)}, bf16[128,128]{1,0:T(8,128)(2,1)S(1)}, bf16[256,256]{1,0:T(8,128)(2,1)S(1)}) custom-call(), custom_call_target="tpu_custom_call" | custom-call | flops 1000000000 | bytes 4000000 | tf_op jit(solution)/shard_map/pallas_call | solution.py:288
  0.4 0.5 %copy-done.1 = bf16[32,4,8,128]{3,2,1,0:T(8,128)(2,1)S(1)} copy-done((bf16[32,4,8,128]{3,2,1,0:T(8,128)(2,1)S(1)}, bf16[32,4,8,128]{3,2,1,0:T(8,128)(2,1)}, u32[]{:S(2)}) %copy-start.1) | copy-done | bytes 262168
  1.0 0.8 %shard_map.74 = (bf16[2,4,32,128]{3,2,1,0:T(8,128)(2,1)S(1)}, bf16[2,4,32,128]{3,2,1,0:T(8,128)(2,1)S(1)}, bf16[2,4,32,128]{3,2,1,0:T(8,128)(2,1)S(1)}, bf16[2,4,32,128]{3,2,1,0:T(8,128)(2,1)S(1)}) custom-call(bf16[32,4,8,128]{3,2,1,0:T(8,128)(2,1)S(1)} %copy-done.1, f32[72,128]{1,0:T(8,128)S(1)} %get-tuple-element.19.waves, ...), custom_call_target="tpu_custom_call" | custom-call | tf_op jit(solution)/shard_map/pallas_call | solution.py:300
  1.7 0.6 %collective-permute-start = (bf16[2,4,32,128]{3,2,1,0:T(8,128)(2,1)S(1)}, bf16[2,4,32,128]{3,2,1,0:T(8,128)(2,1)S(1)}, u32[]{:S(2)}, u32[]{:S(2)}) collective-permute-start(bf16[2,4,32,128]{3,2,1,0:T(8,128)(2,1)S(1)} %get-tuple-element.23), channel_id=1, source_target_pairs={{0,1},{1,0},{2,3},{3,2},{4,5},{5,4},{6,7},{7,6},{8,9},{9,8},{10,11... | collective-permute-start | bytes 196616 | tf_op jit(solution)/shard_map/ppermute | solution.py:280
  2.3 2.6 %collective-permute-start.1 = (bf16[2,4,32,128]{3,2,1,0:T(8,128)(2,1)S(1)}, bf16[2,4,32,128]{3,2,1,0:T(8,128)(2,1)S(1)}, u32[]{:S(2)}, u32[]{:S(2)}) collective-permute-start(bf16[2,4,32,128]{3,2,1,0:T(8,128)(2,1)S(1)} %get-tuple-element.24), channel_id=1, source_target_pairs={{0,2},{1,3},{2,0},{3,1},{4,6},{5,7},{6,4},{7,5},{8,10},{9,11},{10,... | collective-permute-start | bytes 196616 | tf_op jit(solution)/shard_map/ppermute | solution.py:280
  4.8 0.0 collective-permute-start.2
  5.1 0.4 fusion.26.t_ref
  5.5 0.0 copy-start.5
  5.5 0.7 %fusion.11.refs_5_ = bf16[128,256]{1,0:T(8,128)(2,1)S(1)} fusion(s32[128]{0:T(128)S(1)} %get-tuple-element.57, s32[128]{0:T(128)S(1)} %get-tuple-element.59, s32[256]{0:T(256)S(1)} %get-tuple-element.39, s32[256]{0:T(256)S(1)} %get-tuple-element.44, s32[128]{0:T(128)S(1)} %get-tuple-element.56, s32[128]{0:T(128)S(1)} %get-tuple-element.58, s32[]{:T(128)S(6)} %mul.56, ...), kind=kLoop, calls=%fused_computation.31 | loop fusion | flops 2228224 | bytes 78216 | tf_op jit(solution)/shard_map/convert_element_type | solution.py:242
  6.3 0.0 copy-done.5
  6.3 0.0 copy-start.3
  6.3 0.0 copy-start.4
  6.3 0.1 broadcast_in_dim.16.o_ref
  6.4 0.6 %copy-done.3 = bf16[4,8,128]{2,1,0:T(8,128)(2,1)S(1)} copy-done((bf16[4,8,128]{2,1,0:T(8,128)(2,1)S(1)}, bf16[4,8,128]{2,1,0:T(8,128)(2,1)}, u32[]{:S(2)}) %copy-start.3) | copy-done | bytes 8216
  7.0 0.0 copy-done.4
  7.0 0.5 %shard_map.75 = f32[32,4,8,128]{3,2,1,0:T(8,128)S(1)} custom-call(bf16[32,4,8,128]{3,2,1,0:T(8,128)(2,1)S(1)} %copy-done.1, bf16[4,8,128]{2,1,0:T(8,128)(2,1)S(1)} %copy-done.3, bf16[32,32]{1,0:T(8,128)(2,1)S(1)} %copy-done.4, f32[32,8,128]{2,1,0:T(8,128)S(1)} %broadcast_in_dim.16.o_ref), custom_call_target="tpu_custom_call" | custom-call | flops 1000000000 | bytes 1000000 | tf_op jit(solution)/shard_map/pallas_call | solution.py:308
  7.6 0.0 copy-start
  7.6 0.0 collective-permute-done.refs_1_
  7.6 0.0 collective-permute-done.1.refs_2_
  7.6 1.3 %collective-permute-done.2.refs_3_ = bf16[2,4,32,128]{3,2,1,0:T(8,128)(2,1)S(1)} collective-permute-done((bf16[2,4,32,128]{3,2,1,0:T(8,128)(2,1)S(1)}, bf16[2,4,32,128]{3,2,1,0:T(8,128)(2,1)S(1)}, u32[]{:S(2)}, u32[]{:S(2)}) %collective-permute-start.2) | collective-permute-done | bytes 65568 | tf_op jit(solution)/shard_map/ppermute | solution.py:280
  8.9 0.4 shard_map.76
  9.3 13.1 %all_to_all.10.u_ref = bf16[8,2,2,32,128]{4,3,2,1,0:T(8,128)(2,1)S(1)} all-to-all(bf16[8,2,2,32,128]{4,3,2,1,0:T(8,128)(2,1)S(1)} %shard_map.76), channel_id=1, replica_groups={{20,0,4,8,12,16,24,28},{21,1,5,9,13,17,25,29},{22,2,6,10,14,18,26,30},{..., dimensions={0} | all-to-all | bytes 524288 | tf_op jit(solution)/shard_map/all_to_all | solution.py:283
  22.4 0.0 copy-done
  22.4 0.6 %shard_map.77 = bf16[8,4,2,2,8,128]{5,4,3,2,1,0:T(8,128)(2,1)S(1)} custom-call(bf16[8,2,2,32,128]{4,3,2,1,0:T(8,128)(2,1)S(1)} %all_to_all.10.u_ref, bf16[2,4,2,32,1024]{4,3,2,1,0:T(8,128)(2,1)S(1)} %copy-done), custom_call_target="tpu_custom_call" | custom-call | tf_op jit(solution)/shard_map/pallas_call | solution.py:323
  23.0 9.4 %all_to_all.11.m_ref = bf16[8,4,2,2,8,128]{5,4,3,2,1,0:T(8,128)(2,1)S(1)} all-to-all(bf16[8,4,2,2,8,128]{5,4,3,2,1,0:T(8,128)(2,1)S(1)} %shard_map.77), channel_id=1, replica_groups={{20,0,4,8,12,16,24,28},{21,1,5,9,13,17,25,29},{22,2,6,10,14,18,26,30},{..., dimensions={0} | all-to-all | bytes 524288 | tf_op jit(solution)/shard_map/all_to_all | solution.py:283
  32.4 0.0 copy-start.2
  32.4 0.2 shard_map.78.refs_0_
  32.6 0.1 collective-permute-start.4
  32.7 2.4 %collective-permute-start.3 = (bf16[4,4,2,8,128]{4,3,2,1,0:T(8,128)(2,1)S(1)}, bf16[4,4,2,8,128]{4,3,2,1,0:T(8,128)(2,1)S(1)}, u32[]{:S(2)}, u32[]{:S(2)}) collective-permute-start(bf16[4,4,2,8,128]{4,3,2,1,0:T(8,128)(2,1)S(1)} %shard_map.78.refs_0_), channel_id=1, source_target_pairs={{0,1},{1,0},{2,3},{3,2},{4,5},{5,4},{6,7},{7,6},{8,9},{9,8},{10,11... | collective-permute-start | bytes 196616 | tf_op jit(solution)/shard_map/ppermute | solution.py:280
  35.1 1.3 %collective-permute-done.4.refs_3_ = bf16[4,4,2,8,128]{4,3,2,1,0:T(8,128)(2,1)S(1)} collective-permute-done((bf16[4,4,2,8,128]{4,3,2,1,0:T(8,128)(2,1)S(1)}, bf16[4,4,2,8,128]{4,3,2,1,0:T(8,128)(2,1)S(1)}, u32[]{:S(2)}, u32[]{:S(2)}) %collective-permute-start.4) | collective-permute-done | bytes 65568 | tf_op jit(solution)/shard_map/ppermute | solution.py:280
  36.4 0.6 %collective-permute-start.5 = (bf16[4,4,2,8,128]{4,3,2,1,0:T(8,128)(2,1)S(1)}, bf16[4,4,2,8,128]{4,3,2,1,0:T(8,128)(2,1)S(1)}, u32[]{:S(2)}, u32[]{:S(2)}) collective-permute-start(bf16[4,4,2,8,128]{4,3,2,1,0:T(8,128)(2,1)S(1)} %collective-permute-done.4.refs_3_), channel_id=1, source_target_pairs={{0,1},{1,0},{2,3},{3,2},{4,5},{5,4},{6,7},{7,6},{8,9},{9,8},{10,11... | collective-permute-start | bytes 196616 | tf_op jit(solution)/shard_map/ppermute | solution.py:280
  37.0 0.0 collective-permute-done.3.refs_1_
  37.0 0.9 %collective-permute-done.5.refs_2_ = bf16[4,4,2,8,128]{4,3,2,1,0:T(8,128)(2,1)S(1)} collective-permute-done((bf16[4,4,2,8,128]{4,3,2,1,0:T(8,128)(2,1)S(1)}, bf16[4,4,2,8,128]{4,3,2,1,0:T(8,128)(2,1)S(1)}, u32[]{:S(2)}, u32[]{:S(2)}) %collective-permute-start.5) | collective-permute-done | bytes 65568 | tf_op jit(solution)/shard_map/ppermute | solution.py:280
  37.9 0.0 copy-done.2
  37.9 1.3 %shard_map.79 = bf16[8,4,4,8,128]{4,3,2,1,0:T(8,128)(2,1)} custom-call(bf16[4,4,2,8,128]{4,3,2,1,0:T(8,128)(2,1)S(1)} %shard_map.78.refs_0_, bf16[4,4,2,8,128]{4,3,2,1,0:T(8,128)(2,1)S(1)} %collective-permute-done.3.refs_1_, bf16[4,4,2,8,128]{4,3,2,1,0:T(8,128)(2,1)S(1)} %collective-permute-done.5.refs_2_, ...), custom_call_target="tpu_custom_call" | custom-call | tf_op jit(solution)/shard_map/pallas_call | solution.py:334
  (19 shorter events, 0.1 us)
Async XLA Ops:
  0.0 0.9 %copy-start.1 = (bf16[32,4,8,128]{3,2,1,0:T(8,128)(2,1)S(1)}, bf16[32,4,8,128]{3,2,1,0:T(8,128)(2,1)}, u32[]{:S(2)}) copy-start(bf16[32,4,8,128]{3,2,1,0:T(8,128)(2,1)} %x_ref.3) | copy-start | bytes 786436
  1.7 5.9 %collective-permute-start = (bf16[2,4,32,128]{3,2,1,0:T(8,128)(2,1)S(1)}, bf16[2,4,32,128]{3,2,1,0:T(8,128)(2,1)S(1)}, u32[]{:S(2)}, u32[]{:S(2)}) collective-permute-start(bf16[2,4,32,128]{3,2,1,0:T(8,128)(2,1)S(1)} %get-tuple-element.23), channel_id=1, source_target_pairs={{0,1},{1,0},{2,3},{3,2},{4,5},{5,4},{6,7},{7,6},{8,9},{9,8},{10,11... | collective-permute-start | bytes 196616 | tf_op jit(solution)/shard_map/ppermute | solution.py:280
  2.3 5.3 %collective-permute-start.1 = (bf16[2,4,32,128]{3,2,1,0:T(8,128)(2,1)S(1)}, bf16[2,4,32,128]{3,2,1,0:T(8,128)(2,1)S(1)}, u32[]{:S(2)}, u32[]{:S(2)}) collective-permute-start(bf16[2,4,32,128]{3,2,1,0:T(8,128)(2,1)S(1)} %get-tuple-element.24), channel_id=1, source_target_pairs={{0,2},{1,3},{2,0},{3,1},{4,6},{5,7},{6,4},{7,5},{8,10},{9,11},{10,... | collective-permute-start | bytes 196616 | tf_op jit(solution)/shard_map/ppermute | solution.py:280
  4.8 4.1 %collective-permute-start.2 = (bf16[2,4,32,128]{3,2,1,0:T(8,128)(2,1)S(1)}, bf16[2,4,32,128]{3,2,1,0:T(8,128)(2,1)S(1)}, u32[]{:S(2)}, u32[]{:S(2)}) collective-permute-start(bf16[2,4,32,128]{3,2,1,0:T(8,128)(2,1)S(1)} %get-tuple-element.25), channel_id=1, source_target_pairs={{0,3},{1,2},{2,1},{3,0},{4,7},{5,6},{6,5},{7,4},{8,11},{9,10},{10,... | collective-permute-start | bytes 196616 | tf_op jit(solution)/shard_map/ppermute | solution.py:280
  5.5 0.8 %copy-start.5 = (f32[32]{0:T(128)S(1)}, f32[32]{0:T(128)}, u32[]{:S(2)}) copy-start(f32[32]{0:T(128)} %param.11) | copy-start | bytes 388
  6.3 0.7 %copy-start.3 = (bf16[4,8,128]{2,1,0:T(8,128)(2,1)S(1)}, bf16[4,8,128]{2,1,0:T(8,128)(2,1)}, u32[]{:S(2)}) copy-start(bf16[4,8,128]{2,1,0:T(8,128)(2,1)} %d_ref.1) | copy-start | bytes 24580
  6.3 0.7 %copy-start.4 = (bf16[32,32]{1,0:T(8,128)(2,1)S(1)}, bf16[32,32]{1,0:T(8,128)(2,1)}, u32[]{:S(2)}) copy-start(bf16[32,32]{1,0:T(8,128)(2,1)} %p_ref.1) | copy-start | bytes 6148
  7.6 14.8 %copy-start = (bf16[2,4,2,32,1024]{4,3,2,1,0:T(8,128)(2,1)S(1)}, bf16[2,4,2,32,1024]{4,3,2,1,0:T(8,128)(2,1)}, u32[]{:S(2)}) copy-start(bf16[2,4,2,32,1024]{4,3,2,1,0:T(8,128)(2,1)} %w_ref.1) | copy-start | bytes 3145732
  32.4 5.5 %copy-start.2 = (bf16[256,512]{1,0:T(8,128)(2,1)S(1)}, bf16[256,512]{1,0:T(8,128)(2,1)}, u32[]{:S(2)}) copy-start(bf16[256,512]{1,0:T(8,128)(2,1)} %constant.234.clone.refs_6_) | copy-start | bytes 786436
  32.6 3.8 %collective-permute-start.4 = (bf16[4,4,2,8,128]{4,3,2,1,0:T(8,128)(2,1)S(1)}, bf16[4,4,2,8,128]{4,3,2,1,0:T(8,128)(2,1)S(1)}, u32[]{:S(2)}, u32[]{:S(2)}) collective-permute-start(bf16[4,4,2,8,128]{4,3,2,1,0:T(8,128)(2,1)S(1)} %shard_map.78.refs_0_), channel_id=1, source_target_pairs={{0,3},{1,2},{2,1},{3,0},{4,7},{5,6},{6,5},{7,4},{8,11},{9,10},{10,... | collective-permute-start | bytes 196616 | tf_op jit(solution)/shard_map/ppermute | solution.py:280
  32.7 4.3 %collective-permute-start.3 = (bf16[4,4,2,8,128]{4,3,2,1,0:T(8,128)(2,1)S(1)}, bf16[4,4,2,8,128]{4,3,2,1,0:T(8,128)(2,1)S(1)}, u32[]{:S(2)}, u32[]{:S(2)}) collective-permute-start(bf16[4,4,2,8,128]{4,3,2,1,0:T(8,128)(2,1)S(1)} %shard_map.78.refs_0_), channel_id=1, source_target_pairs={{0,1},{1,0},{2,3},{3,2},{4,5},{5,4},{6,7},{7,6},{8,9},{9,8},{10,11... | collective-permute-start | bytes 196616 | tf_op jit(solution)/shard_map/ppermute | solution.py:280
  36.4 1.5 %collective-permute-start.5 = (bf16[4,4,2,8,128]{4,3,2,1,0:T(8,128)(2,1)S(1)}, bf16[4,4,2,8,128]{4,3,2,1,0:T(8,128)(2,1)S(1)}, u32[]{:S(2)}, u32[]{:S(2)}) collective-permute-start(bf16[4,4,2,8,128]{4,3,2,1,0:T(8,128)(2,1)S(1)} %collective-permute-done.4.refs_3_), channel_id=1, source_target_pairs={{0,1},{1,0},{2,3},{3,2},{4,5},{5,4},{6,7},{7,6},{8,9},{9,8},{10,11... | collective-permute-start | bytes 196616 | tf_op jit(solution)/shard_map/ppermute | solution.py:280
